TPU v7x, 256 devices: a whole 4x4x8 slice. The times are simulated.
256 devices in a mesh: seq: 64 (over z, x, core), head: 4 (over y).
Axes of the slice: x: 4, y: 4, z: 8, core: 2. Of those that a mesh axis runs over, the one named last changes fastest.
Arguments:
- queries: bfloat16 [32768, 4096], P('seq', 'head'), may hold values from -6 to 6
- keys: bfloat16 [32768, 4096], P('seq', 'head'), may hold values from -6 to 6
- values: bfloat16 [32768, 4096], P('seq', 'head'), may hold values from -6 to 6
- med_weight: float32 [2, 32, 4], P(None, 'head'), may hold values from -3 to 3
- coarse_weight: float32 [2, 32, 64], P(None, 'head'), may hold values from -0.75 to 0.75
- out_weight: bfloat16 [4096, 4096], P('head'), may hold values from -0.09375 to 0.09375
Outputs:
- mixed: bfloat16 [32768, 4096], P('seq', 'head')
All inputs are finite; a program needn't handle non-finite values.
Results may differ from a plain program's by a relative error of at most 0.013.
Values may be sent and summed in bfloat16 or wider, within the bound.
No kernel may reach another device: no remote copies, remote signals or barrier semaphores. Data moves between devices by JAX's collectives and lax.ppermute only.
A program may use at most 128 MiB of HBM per device.

v0:
```python
import math

import jax
import jax.numpy as jnp
from jax import lax
from jax.sharding import PartitionSpec as P

HEAD_DIM = 128
WIN = 512
MED = 4
COARSE = 64


def shifted(block, axis, distance):
    devices = range(lax.axis_size(axis))
    route = [(i - distance, i) for i in devices if i - distance in devices]
    return lax.ppermute(block, axis, route)


def in_one_piece(arrays, axis, dim, along):
    ends, at = ([], 0)
    for a in arrays[:-1]:
        at += a.shape[along]
        ends.append(at)
    both = jnp.concatenate(arrays, axis=along)
    return tuple(jnp.split(lax.all_gather(both, axis, axis=dim, tiled=True), ends, axis=along))


def summarize(tensor, weight, ratio):
    groups = tensor.shape[0] // ratio
    grouped = tensor.reshape(groups, ratio, tensor.shape[1], tensor.shape[2]).astype(jnp.float32)
    return jnp.einsum("jrhd,hr->jhd", grouped, weight).astype(jnp.bfloat16)


def attend_block(query_blk, query_place, key_all, value_all, key_place, usable, score_scale):
    scores = (
        jnp.einsum("qhd,khd->hqk", query_blk, key_all, preferred_element_type=jnp.float32)
        * score_scale
    )
    allowed = (key_place[None, :] <= query_place[:, None]) & usable[None, :]
    scores = jnp.where(allowed[None], scores, -jnp.inf)
    row_peak = jnp.max(scores, axis=-1)
    exp_scores = jnp.exp(scores - row_peak[..., None])
    row_total = jnp.sum(exp_scores, axis=-1)
    weighted = jnp.einsum(
        "hqk,khd->hqd",
        exp_scores.astype(jnp.bfloat16),
        value_all,
        preferred_element_type=jnp.float32,
    )
    return (row_peak, row_total, weighted)


def body(queries, keys, values, med_weight, coarse_weight, out_weight):
    tok_rows = queries.shape[0]
    head_count = queries.shape[1] // HEAD_DIM
    flat_width = head_count * HEAD_DIM
    score_scale = 1.0 / math.sqrt(HEAD_DIM)
    position = lax.axis_index("seq")
    query3 = queries.reshape(tok_rows, head_count, HEAD_DIM)
    key3 = keys.reshape(tok_rows, head_count, HEAD_DIM)
    value3 = values.reshape(tok_rows, head_count, HEAD_DIM)
    edge_keys, edge_values = shifted((keys, values), "seq", 1)
    edge_keys = edge_keys.reshape(WIN, head_count, HEAD_DIM)
    edge_values = edge_values.reshape(WIN, head_count, HEAD_DIM)
    med_keys = summarize(key3, med_weight[0], MED).reshape(-1, flat_width)
    med_values = summarize(value3, med_weight[1], MED).reshape(-1, flat_width)
    coarse_keys = summarize(key3, coarse_weight[0], COARSE).reshape(-1, flat_width)
    coarse_values = summarize(value3, coarse_weight[1], COARSE).reshape(-1, flat_width)
    moved = shifted((med_keys, med_values), "seq", 2)
    fetched = [moved]
    for distance in (3, 4):
        moved = shifted((moved[0], moved[1]), "seq", 1)
        fetched.append(moved)
    key_list = [key3]
    value_list = [value3]
    place_list = [jnp.arange(tok_rows, dtype=jnp.int32)]
    usable_list = [jnp.ones((tok_rows,), bool)]
    key_list.append(edge_keys)
    value_list.append(edge_values)
    place_list.append(jnp.full((WIN,), -1, jnp.int32))
    usable_list.append(jnp.broadcast_to(position >= 1, (WIN,)))
    for distance, fetched_pair in zip((2, 3, 4), fetched):
        med_rows = fetched_pair[0].shape[0]
        key_list.append(fetched_pair[0].reshape(med_rows, head_count, HEAD_DIM))
        value_list.append(fetched_pair[1].reshape(med_rows, head_count, HEAD_DIM))
        place_list.append(jnp.full((med_rows,), -1, jnp.int32))
        usable_list.append(jnp.broadcast_to(position >= distance, (med_rows,)))
    per_coarse = tok_rows // COARSE
    gathered_keys, gathered_values = in_one_piece((coarse_keys, coarse_values), "seq", 0, 1)
    rows_all = gathered_keys.shape[0]
    key_list.append(gathered_keys.reshape(rows_all, head_count, HEAD_DIM))
    value_list.append(gathered_values.reshape(rows_all, head_count, HEAD_DIM))
    place_list.append(jnp.full((rows_all,), -1, jnp.int32))
    usable_list.append(jnp.arange(rows_all, dtype=jnp.int32) // per_coarse <= position - 1)
    key_all = jnp.concatenate(key_list, 0)
    value_all = jnp.concatenate(value_list, 0)
    key_place = jnp.concatenate(place_list, 0)
    usable = jnp.concatenate(usable_list, 0)
    block_rows = math.gcd(tok_rows, 512)
    block_count = tok_rows // block_rows
    query_blocks = query3.reshape(block_count, block_rows, head_count, HEAD_DIM)

    def local_pass(index):
        query_place = index * block_rows + jnp.arange(block_rows, dtype=jnp.int32)
        return attend_block(
            query_blocks[index], query_place, key_all, value_all, key_place, usable, score_scale
        )

    row_peak, row_total, weighted = lax.map(local_pass, jnp.arange(block_count, dtype=jnp.int32))
    row_peak = row_peak.transpose(1, 0, 2).reshape(head_count, tok_rows)
    row_total = row_total.transpose(1, 0, 2).reshape(head_count, tok_rows)
    weighted = weighted.transpose(1, 0, 2, 3).reshape(head_count, tok_rows, HEAD_DIM)
    attention = (weighted / row_total[..., None]).astype(jnp.bfloat16)
    attention = attention.transpose(1, 0, 2).reshape(tok_rows, flat_width)
    term = lax.dot_general(
        out_weight, attention, (((0,), (1,)), ((), ())), preferred_element_type=jnp.float32
    )
    mixed = (
        lax.psum_scatter(
            lax.optimization_barrier(term.astype(jnp.bfloat16))
            .astype(jnp.float32)
            .astype(jnp.bfloat16),
            "head",
            scatter_dimension=0,
            tiled=True,
        )
        .astype(jnp.float32)
        .T
    )
    return mixed.astype(jnp.bfloat16)


def solution(mesh):
    placed = (
        P("seq", "head"),
        P("seq", "head"),
        P("seq", "head"),
        P(None, "head", None),
        P(None, "head", None),
        P("head", None),
    )
    return jax.shard_map(
        body, mesh=mesh, in_specs=placed, out_specs=P("seq", "head"), check_vma=False
    )
```

profile of v0, /device:TPU:96, one launch (start us, length us, event | category | flops | bytes accessed | tf_op | source)
XLA Modules:
  0.0 210.5 jit_solution(14652034411456848675)
XLA Ops:
  11.6 1.9 collective-permute-start.4
  16.5 3.4 %collective-permute-start.1 = (bf16[128,1024]{0,1:T(8,128)(2,1)S(1)}, bf16[128,1024]{0,1:T(8,128)(2,1)}, u32[]{:S(2)}, u32[]{:S(2)}) collective-permute-start(bf16[128,1024]{0,1:T(8,128)(2,1)S(1)} %bitcast.106), channel_id=1, source_target_pairs={{0,8},{4,12},{8,16},{12,20},{16,24},{20,28},{24,32},{28,36},{32,40... | collective-permute-start | bytes 786440 | tf_op jit(solution)/shard_map/ppermute | solution.py:17
  20.8 3.4 %collective-permute-start.5 = (bf16[128,1024]{0,1:T(8,128)(2,1)}, bf16[128,1024]{0,1:T(8,128)(2,1)}, u32[]{:S(2)}, u32[]{:S(2)}) collective-permute-start(bf16[128,1024]{0,1:T(8,128)(2,1)} %bitcast.30), channel_id=1, source_target_pairs={{0,8},{4,12},{8,16},{12,20},{16,24},{20,28},{24,32},{28,36},{32,40... | collective-permute-start | bytes 786440 | tf_op jit(solution)/shard_map/ppermute | solution.py:17
  25.7 2.7 %collective-permute-start = (bf16[512,1024]{0,1:T(8,128)(2,1)S(1)}, bf16[512,1024]{0,1:T(8,128)(2,1)}, u32[]{:S(2)}, u32[]{:S(2)}) collective-permute-start(bf16[512,1024]{0,1:T(8,128)(2,1)S(1)} %copy.23), channel_id=1, source_target_pairs={{0,4},{4,8},{8,12},{12,16},{16,20},{20,24},{24,28},{28,32},{32,36}... | collective-permute-start | bytes 3145736 | tf_op jit(solution)/shard_map/ppermute | solution.py:17
  28.4 2.3 %copy.33 = bf16[512,1024]{0,1:T(8,128)(2,1)} copy(bf16[512,1024]{1,0:T(8,128)(2,1)} %param.8) | data formatting | bytes 2097152 | tf_op args[2]
  33.3 7.6 %collective-permute-start.2 = (bf16[128,1024]{0,1:T(8,128)(2,1)}, bf16[128,1024]{0,1:T(8,128)(2,1)}, u32[]{:S(2)}, u32[]{:S(2)}) collective-permute-start(bf16[128,1024]{0,1:T(8,128)(2,1)} %collective-permute-done.1), channel_id=1, source_target_pairs={{0,4},{4,8},{8,12},{12,16},{16,20},{20,24},{24,28},{28,32},{32,36}... | collective-permute-start | bytes 786440 | tf_op jit(solution)/shard_map/ppermute | solution.py:17
  42.4 1.9 collective-permute-start.6
  44.3 12.3 %collective-permute-done.2 = bf16[128,1024]{0,1:T(8,128)(2,1)} collective-permute-done((bf16[128,1024]{0,1:T(8,128)(2,1)}, bf16[128,1024]{0,1:T(8,128)(2,1)}, u32[]{:S(2)}, u32[]{:S(2)}) %collective-permute-start.2) | collective-permute-done | bytes 262176 | tf_op jit(solution)/shard_map/ppermute | solution.py:17
  56.7 1.9 collective-permute-start.3
  58.6 2.3 %constant_dynamic-update-slice_fusion.5 = bf16[1920,8,128]{0,2,1:T(8,128)(2,1)} fusion(bf16[512,8,128]{0,2,1:T(8,128)(2,1)} %bitcast.102), kind=kLoop, calls=%fused_computation.28 | loop fusion | bytes 2097152
  60.9 2.4 %constant_dynamic-update-slice_fusion.12 = bf16[1920,8,128]{2,0,1:T(8,128)(2,1)} fusion(bf16[512,8,128]{2,0,1:T(8,128)(2,1)} %copy.26), kind=kLoop, calls=%fused_computation.35 | loop fusion | bytes 2097152
  66.2 2.1 collective-permute-start.7
  68.3 1.8 copy.30
  70.2 2.3 %copy.34 = bf16[512,1024]{0,1:T(8,128)(2,1)} copy(bf16[512,1024]{1,0:T(8,128)(2,1)} %collective-permute-done.4) | data formatting | bytes 2097152 | tf_op jit(solution)/shard_map/ppermute | solution.py:17
  72.4 2.3 %constant_dynamic-update-slice_fusion.4 = bf16[1920,8,128]{0,2,1:T(8,128)(2,1)} fusion(bf16[1920,8,128]{0,2,1:T(8,128)(2,1)} %constant_dynamic-update-slice_fusion.5, bf16[512,8,128]{0,2,1:T(8,128)(2,1)} %bitcast.103), kind=kLoop, calls=%fused_computation.27 | loop fusion | bytes 2097152
  85.9 4.7 %all-gather.2.cloned.1.call-done = bf16[512,2048]{1,0:T(8,128)(2,1)} async-done(((bf16[8,2048]{1,0:T(8,128)(2,1)}), bf16[512,2048]{1,0:T(8,128)(2,1)}) %all-gather.2.cloned.1.call-update) | async-done | bytes 2097168 | tf_op jit(solution)/shard_map/all_gather | solution.py:26
  90.6 2.7 %fusion.24 = (bf16[512,1024]{1,0:T(8,128)(2,1)S(1)}, bf16[512,1024]{1,0:T(8,128)(2,1)}) fusion(bf16[512,2048]{1,0:T(8,128)(2,1)} %all-gather.2.cloned.1.call-done), kind=kLoop, calls=%fused_computation.54 | loop fusion | bytes 4194304 | tf_op jit(solution)/shard_map/split | solution.py:26
  96.2 2.3 %copy.35 = bf16[512,1024]{0,1:T(8,128)(2,1)} copy(bf16[512,1024]{1,0:T(8,128)(2,1)} %get-tuple-element.20) | data formatting | bytes 2097152 | tf_op jit(solution)/shard_map/split | solution.py:26
  98.5 2.4 %constant_dynamic-update-slice_fusion = bf16[1920,8,128]{0,2,1:T(8,128)(2,1)} fusion(bf16[1920,8,128]{0,2,1:T(8,128)(2,1)} %constant_dynamic-update-slice_fusion.1, bf16[512,8,128]{0,2,1:T(8,128)(2,1)} %bitcast.104), kind=kLoop, calls=%fused_computation.23 | loop fusion | bytes 2097152 | tf_op jit(solution)/shard_map/concatenate | solution.py:97
  102.1 14.7 %fusion.2 = (f32[8,512]{1,0:T(8,128)S(1)}, f32[8,1920,512]{2,1,0:T(8,128)}) fusion(pred[512,1920]{0,1:T(8,128)(4,1)S(1)} %fusion.7, bf16[1920,8,128]{2,0,1:T(8,128)(2,1)} %constant_dynamic-update-slice_fusion.7, bf16[512,1024]{1,0:T(8,128)(2,1)S(1)} %copy-done), kind=kOutput, calls=%fused_computation.4 | convolution fusion | flops 2036854784 | bytes 37437440 | tf_op jit(solution)/shard_map/while/body/eval_jaxpr/qhd,khd->hqk/dot_general | solution.py:37
  116.8 13.8 %fusion = f32[8,512]{1,0:T(8,128)S(1)} fusion(f32[8,1920,512]{2,1,0:T(8,128)} %get-tuple-element.36, f32[8,512]{1,0:T(8,128)S(1)} %get-tuple-element.34, pred[512,1920]{0,1:T(8,128)(4,1)S(1)} %fusion.7), kind=kLoop, calls=%fused_computation.2 | loop fusion | flops 31453184 | bytes 32473088 | tf_op jit(solution)/shard_map/while/body/eval_jaxpr/reduce_sum | solution.py:44
  130.6 15.2 %fusion.8 = bf16[512,8,128]{0,2,1:T(8,128)(2,1)S(1)} fusion(bf16[1920,8,128]{0,2,1:T(8,128)(2,1)} %constant_dynamic-update-slice_fusion, f32[8,1920,512]{2,1,0:T(8,128)} %get-tuple-element.36, f32[8,512]{1,0:T(8,128)S(1)} %get-tuple-element.34, pred[512,1920]{0,1:T(8,128)(4,1)S(1)} %fusion.7, f32[512,8]{0,1:T(8,128)S(1)} %bitcast.109), kind=kOutput, calls=%fused_computation.12 | convolution fusion | flops 2045771776 | bytes 37453824 | tf_op jit(solution)/shard_map/while/body/eval_jaxpr/hqk,khd->hqd/dot_general | solution.py:45
  145.8 9.6 %fusion.6 = bf16[4096,512]{0,1:T(8,128)(2,1)} fusion(bf16[512,1024]{0,1:T(8,128)(2,1)S(1)} %bitcast.112, bf16[1024,4096]{1,0:T(8,128)(2,1)} %param.11), kind=kOutput, calls=%fused_computation.8 | convolution fusion | flops 4297064448 | bytes 13631488 | tf_op jit(solution)/shard_map/dot_general | solution.py:116
  155.4 48.2 %reduce-scatter.2.cloned.1.call-done = bf16[1024,512]{0,1:T(8,128)(2,1)} async-done(((bf16[4096,512]{0,1:T(8,128)(2,1)}), bf16[1024,512]{0,1:T(8,128)(2,1)}) %reduce-scatter.2.cloned.1.call-update) | async-done | bytes 1048592 | tf_op jit(solution)/shard_map/reduce_scatter | solution.py:120
  (65 shorter events, 32.6 us)
Async XLA Ops:
  6.5 95.5 %copy-start = (bf16[512,1024]{1,0:T(8,128)(2,1)S(1)}, bf16[512,1024]{1,0:T(8,128)(2,1)}, u32[]{:S(2)}) copy-start(bf16[512,1024]{1,0:T(8,128)(2,1)} %param.6) | copy-start | bytes 3145732
  6.5 7.0 %copy-start.3 = (f32[2,8,4]{1,2,0:T(4,128)S(1)}, f32[2,8,4]{1,2,0:T(4,128)}, u32[]{:S(2)}) copy-start(f32[2,8,4]{1,2,0:T(4,128)} %param.9) | copy-start | bytes 772
  6.5 84.1 %all-gather.2.cloned.1.call-start = ((), (), s32[]{:S(2)}) async-start(), calls=%async_computation.1 | async-start | bytes 2129920 | tf_op jit(solution)/shard_map/all_gather | solution.py:26
  11.6 192.1 %reduce-scatter.2.cloned.1.call-start = ((), (), s32[]{:S(2)}) async-start(), calls=%async_computation.2 | async-start | bytes 5242880 | tf_op jit(solution)/shard_map/reduce_scatter | solution.py:120
  11.6 58.5 %collective-permute-start.4 = (bf16[512,1024]{1,0:T(8,128)(2,1)}, bf16[512,1024]{1,0:T(8,128)(2,1)}, u32[]{:S(2)}, u32[]{:S(2)}) collective-permute-start(bf16[512,1024]{1,0:T(8,128)(2,1)} %param.8), channel_id=1, source_target_pairs={{0,4},{4,8},{8,12},{12,16},{16,20},{20,24},{24,28},{28,32},{32,36}... | collective-permute-start | bytes 3145736 | tf_op jit(solution)/shard_map/ppermute | solution.py:17
  16.5 16.9 %collective-permute-start.1 = (bf16[128,1024]{0,1:T(8,128)(2,1)S(1)}, bf16[128,1024]{0,1:T(8,128)(2,1)}, u32[]{:S(2)}, u32[]{:S(2)}) collective-permute-start(bf16[128,1024]{0,1:T(8,128)(2,1)S(1)} %bitcast.106), channel_id=1, source_target_pairs={{0,8},{4,12},{8,16},{12,20},{16,24},{20,28},{24,32},{28,36},{32,40... | collective-permute-start | bytes 786440 | tf_op jit(solution)/shard_map/ppermute | solution.py:17
  20.8 21.6 %collective-permute-start.5 = (bf16[128,1024]{0,1:T(8,128)(2,1)}, bf16[128,1024]{0,1:T(8,128)(2,1)}, u32[]{:S(2)}, u32[]{:S(2)}) collective-permute-start(bf16[128,1024]{0,1:T(8,128)(2,1)} %bitcast.30), channel_id=1, source_target_pairs={{0,8},{4,12},{8,16},{12,20},{16,24},{20,28},{24,32},{28,36},{32,40... | collective-permute-start | bytes 786440 | tf_op jit(solution)/shard_map/ppermute | solution.py:17
  25.7 49.1 %collective-permute-start = (bf16[512,1024]{0,1:T(8,128)(2,1)S(1)}, bf16[512,1024]{0,1:T(8,128)(2,1)}, u32[]{:S(2)}, u32[]{:S(2)}) collective-permute-start(bf16[512,1024]{0,1:T(8,128)(2,1)S(1)} %copy.23), channel_id=1, source_target_pairs={{0,4},{4,8},{8,12},{12,16},{16,20},{20,24},{24,28},{28,32},{32,36}... | collective-permute-start | bytes 3145736 | tf_op jit(solution)/shard_map/ppermute | solution.py:17
  33.3 23.4 %collective-permute-start.2 = (bf16[128,1024]{0,1:T(8,128)(2,1)}, bf16[128,1024]{0,1:T(8,128)(2,1)}, u32[]{:S(2)}, u32[]{:S(2)}) collective-permute-start(bf16[128,1024]{0,1:T(8,128)(2,1)} %collective-permute-done.1), channel_id=1, source_target_pairs={{0,4},{4,8},{8,12},{12,16},{16,20},{20,24},{24,28},{28,32},{32,36}... | collective-permute-start | bytes 786440 | tf_op jit(solution)/shard_map/ppermute | solution.py:17
  42.4 23.8 %collective-permute-start.6 = (bf16[128,1024]{0,1:T(8,128)(2,1)}, bf16[128,1024]{0,1:T(8,128)(2,1)}, u32[]{:S(2)}, u32[]{:S(2)}) collective-permute-start(bf16[128,1024]{0,1:T(8,128)(2,1)} %collective-permute-done.5), channel_id=1, source_target_pairs={{0,4},{4,8},{8,12},{12,16},{16,20},{20,24},{24,28},{28,32},{32,36}... | collective-permute-start | bytes 786440 | tf_op jit(solution)/shard_map/ppermute | solution.py:17
  56.7 11.7 %collective-permute-start.3 = (bf16[128,1024]{0,1:T(8,128)(2,1)}, bf16[128,1024]{0,1:T(8,128)(2,1)}, u32[]{:S(2)}, u32[]{:S(2)}) collective-permute-start(bf16[128,1024]{0,1:T(8,128)(2,1)} %collective-permute-done.2), channel_id=1, source_target_pairs={{0,4},{4,8},{8,12},{12,16},{16,20},{20,24},{24,28},{28,32},{32,36}... | collective-permute-start | bytes 786440 | tf_op jit(solution)/shard_map/ppermute | solution.py:17
  66.2 13.7 %collective-permute-start.7 = (bf16[128,1024]{0,1:T(8,128)(2,1)}, bf16[128,1024]{0,1:T(8,128)(2,1)}, u32[]{:S(2)}, u32[]{:S(2)}) collective-permute-start(bf16[128,1024]{0,1:T(8,128)(2,1)} %collective-permute-done.6), channel_id=1, source_target_pairs={{0,4},{4,8},{8,12},{12,16},{16,20},{20,24},{24,28},{28,32},{32,36}... | collective-permute-start | bytes 786440 | tf_op jit(solution)/shard_map/ppermute | solution.py:17
  76.4 8.8 %copy-start.2 = (bf16[128,8,128]{2,0,1:T(8,128)(2,1)S(1)}, bf16[128,8,128]{2,0,1:T(8,128)(2,1)}, u32[]{:S(2)}) copy-start(bf16[128,8,128]{2,0,1:T(8,128)(2,1)} %copy.30) | copy-start | bytes 786436
  145.8 57.9 %copy-start.1 = (bf16[512,1024]{1,0:T(8,128)(2,1)S(1)}, bf16[512,1024]{1,0:T(8,128)(2,1)}, u32[]{:S(2)}) copy-start(bf16[512,1024]{1,0:T(8,128)(2,1)} %param.6) | copy-start | bytes 3145732
Sparse Core Ops, SparseCore 0:
  11.7 78.8 all-gather.1
  155.5 48.0 reduce-scatter.1
where the time goes:
time: 214 us; the launch traced here: 210 us
  waiting for transfers between devices  65.3 us (31%)
  local copies, waits for them, and re-layouts  48.8 us (23%)
  matrix products  40.1 us (19%)
  starting transfers between devices  24.9 us (12%)
  other arithmetic  17.6 us (8%)
  between operations  13.7 us (6%)
    reduce_scatter x1, waiting for transfers between devices, body(): lax.psum_scatter(lax.optimization_barrier(term.astype(jnp.bfloat16)).asty...  48.2 us
    unnamed x32, local copies, waits for them, and re-layouts  25.7 us
    ppermute x8, starting transfers between devices, shifted(): return lax.ppermute(block, axis, route)  24.9 us
    dot_general x1, matrix products, attend_block(): jnp.einsum('hqk,khd->hqd', exp_scores.astype(jnp.bfloat16), value_all, pr...  15.2 us
    dot_general x1, matrix products, attend_block(): jnp.einsum('qhd,khd->hqk', query_blk, key_all, preferred_element_type=jnp...  14.7 us
    reduce_sum x1, other arithmetic, attend_block(): row_total = jnp.sum(exp_scores, axis=-1)  13.8 us
    ppermute x8, waiting for transfers between devices, shifted(): return lax.ppermute(block, axis, route)  12.4 us
    dot_general x1, matrix products, body(): lax.dot_general(out_weight, attention, (((0,), (1,)), ((), ())), preferre...  9.59 us
  transfers between devices with their start and end apart: 10, of which 3 were waited for; matrix products, arithmetic and copies ran while one was open for 17% of the time, Pallas kernels for 0%

commit v1 on v0

v1 whole, which is shorter than its diff:
```python
import functools
import math

import jax
import jax.numpy as jnp
from jax import lax
from jax.experimental import pallas as pl
from jax.experimental.pallas import tpu as pltpu
from jax.sharding import PartitionSpec as P

HEAD_DIM = 128
WIN = 512
MED = 4
COARSE = 64
NEG = -1e30
EXP2_SCALE = math.log2(math.e) / math.sqrt(HEAD_DIM)
F32 = jnp.float32
BF16 = jnp.bfloat16


def mm(a, b):
    return lax.dot_general(a, b, (((1,), (0,)), ((), ())), preferred_element_type=F32)


def mm_t(a, b):
    return lax.dot_general(a, b, (((1,), (1,)), ((), ())), preferred_element_type=F32)


def pool_kernel(heads, k_ref, v_ref, mw_ref, cw_ref, med_ref, coarse_ref):
    rows = k_ref.shape[0]
    n_med, n_coarse = rows // MED, rows // COARSE
    med_on = (
        lax.broadcasted_iota(jnp.int32, (n_med, rows), 1) // MED
        == lax.broadcasted_iota(jnp.int32, (n_med, rows), 0)
    )
    coarse_on = (
        lax.broadcasted_iota(jnp.int32, (n_coarse, rows), 1) // COARSE
        == lax.broadcasted_iota(jnp.int32, (n_coarse, rows), 0)
    )

    def pooled(on, w, x):
        spread = jnp.where(on, w, 0.0)
        high = spread.astype(BF16)
        low = (spread - high.astype(F32)).astype(BF16)
        return mm(high, x) + mm(low, x)

    for t, ref in enumerate((k_ref, v_ref)):
        for h in range(heads):
            cols = pl.ds(h * HEAD_DIM, HEAD_DIM)
            at = pl.ds((t * heads + h) * HEAD_DIM, HEAD_DIM)
            x = ref[:, cols]
            row = pl.ds(t * heads + h, 1)
            med_ref[:, at] = pooled(med_on, mw_ref[row, :], x).astype(BF16)
            coarse_ref[:, at] = pooled(coarse_on, cw_ref[row, :], x).astype(BF16)


def pool(keys, values, med_weight, coarse_weight):
    rows, width = keys.shape
    heads = width // HEAD_DIM
    mw = jnp.tile(med_weight.reshape(2 * heads, MED), (1, rows // MED))
    cw = jnp.tile(coarse_weight.reshape(2 * heads, COARSE), (1, rows // COARSE))
    return pl.pallas_call(
        functools.partial(pool_kernel, heads),
        out_shape=(
            jax.ShapeDtypeStruct((rows // MED, 2 * width), BF16),
            jax.ShapeDtypeStruct((rows // COARSE, 2 * width), BF16),
        ),
        compiler_params=pltpu.CompilerParams(vmem_limit_bytes=32 << 20),
        cost_estimate=pl.CostEstimate(
            flops=4 * 136 * rows * 2 * width, bytes_accessed=3 << 20, transcendentals=0
        ),
        name="pool",
    )(keys, values, mw, cw)


def near_kernel(tile, pos_ref, q_ref, k_ref, v_ref, ek_ref, ev_ref, acc_ref, stat_ref):
    rows = q_ref.shape[0]
    has_edge = pos_ref[0] >= 1
    lane = lax.broadcasted_iota(jnp.int32, (tile, 128), 1)
    on_diag = lax.broadcasted_iota(jnp.int32, (tile, tile), 1) <= lax.broadcasted_iota(
        jnp.int32, (tile, tile), 0
    )
    for i in range(rows // tile):
        at = pl.ds(i * tile, tile)
        q = q_ref[at, :]
        diag = jnp.where(on_diag, mm_t(q, k_ref[at, :]), NEG)
        edge = jnp.where(has_edge, mm_t(q, ek_ref[...]), NEG)
        peak = jnp.maximum(
            jnp.max(diag, axis=1, keepdims=True), jnp.max(edge, axis=1, keepdims=True)
        )
        if i:
            past = mm_t(q, k_ref[: i * tile, :])
            peak = jnp.maximum(peak, jnp.max(past, axis=1, keepdims=True))
        p = jnp.exp2((diag - peak) * EXP2_SCALE)
        total = jnp.sum(p, axis=1, keepdims=True)
        acc = mm(p.astype(BF16), v_ref[at, :])
        p = jnp.exp2((edge - peak) * EXP2_SCALE)
        total += jnp.sum(p, axis=1, keepdims=True)
        acc += mm(p.astype(BF16), ev_ref[...])
        if i:
            p = jnp.exp2((past - peak) * EXP2_SCALE)
            total += jnp.sum(p, axis=1, keepdims=True)
            acc += mm(p.astype(BF16), v_ref[: i * tile, :])
        acc_ref[at, :] = acc
        stat_ref[0, at, :] = jnp.where(lane == 0, peak, total)


def near(position, queries, keys, values, edge_keys, edge_values):
    rows, width = queries.shape
    heads = width // HEAD_DIM
    col = pl.BlockSpec((rows, HEAD_DIM), lambda h, *_: (0, h))
    return pl.pallas_call(
        functools.partial(near_kernel, 256),
        out_shape=(
            jax.ShapeDtypeStruct((rows, width), F32),
            jax.ShapeDtypeStruct((heads, rows, 128), F32),
        ),
        grid_spec=pltpu.PrefetchScalarGridSpec(
            num_scalar_prefetch=1,
            grid=(heads,),
            in_specs=[col] * 5,
            out_specs=(col, pl.BlockSpec((1, rows, 128), lambda h, *_: (h, 0, 0))),
        ),
        compiler_params=pltpu.CompilerParams(vmem_limit_bytes=32 << 20),
        cost_estimate=pl.CostEstimate(
            flops=4 * rows * 2 * rows * width, bytes_accessed=9 << 20, transcendentals=0
        ),
        name="near",
    )(position, queries, keys, values, edge_keys, edge_values)


def far_kernel(
    tile, per_coarse, pos_ref, q_ref, m2k, m2v, m3k, m3v, m4k, m4v, ck, cv, acc_ref, stat_ref, out_ref
):
    rows = q_ref.shape[0]
    pos = pos_ref[0]
    n_coarse = ck.shape[0]
    usable = lax.broadcasted_iota(jnp.int32, (1, n_coarse), 1) < pos * per_coarse
    for i in range(rows // tile):
        at = pl.ds(i * tile, tile)
        q = q_ref[at, :]
        parts = []
        for distance, k in ((2, m2k), (3, m3k), (4, m4k)):
            parts.append(jnp.where(pos >= distance, mm_t(q, k[...]), NEG))
        parts.append(jnp.where(usable, mm_t(q, ck[...]), NEG))
        stat = stat_ref[0, at, :]
        near_peak, near_total = stat[:, 0:1], stat[:, 1:2]
        peak = near_peak
        for s in parts:
            peak = jnp.maximum(peak, jnp.max(s, axis=1, keepdims=True))
        shrink = jnp.exp2((near_peak - peak) * EXP2_SCALE)
        total = near_total * shrink
        acc = acc_ref[at, :] * shrink
        for s, v in zip(parts, (m2v, m3v, m4v, cv)):
            p = jnp.exp2((s - peak) * EXP2_SCALE)
            total += jnp.sum(p, axis=1, keepdims=True)
            acc += mm(p.astype(BF16), v[...])
        out_ref[at, :] = (acc / total).astype(BF16)


def far(position, queries, meds, coarse, acc, stat, chunk, chunks):
    rows, width = queries.shape
    heads = width // HEAD_DIM
    part = rows // chunks
    n_med, n_coarse = meds[0].shape[0], coarse.shape[0]
    col = pl.BlockSpec((part, HEAD_DIM), lambda h, *_: (chunk, h))
    summary = []
    operands = []
    for x, n in ((meds[0], n_med), (meds[1], n_med), (meds[2], n_med), (coarse, n_coarse)):
        summary.append(pl.BlockSpec((n, HEAD_DIM), lambda h, *_: (0, h)))
        summary.append(pl.BlockSpec((n, HEAD_DIM), lambda h, *_: (0, heads + h)))
        operands += [x, x]
    return pl.pallas_call(
        functools.partial(far_kernel, part, rows // COARSE),
        out_shape=jax.ShapeDtypeStruct((part, width), BF16),
        grid_spec=pltpu.PrefetchScalarGridSpec(
            num_scalar_prefetch=1,
            grid=(heads,),
            in_specs=[col]
            + summary
            + [col, pl.BlockSpec((1, part, 128), lambda h, *_: (h, chunk, 0))],
            out_specs=pl.BlockSpec((part, HEAD_DIM), lambda h, *_: (0, h)),
        ),
        compiler_params=pltpu.CompilerParams(vmem_limit_bytes=32 << 20),
        cost_estimate=pl.CostEstimate(
            flops=4 * part * (3 * n_med + n_coarse) * width,
            bytes_accessed=6 << 20,
            transcendentals=0,
        ),
        name="far",
    )(position, queries, *operands, acc, stat)


def project_kernel(members, head_ref, a_ref, w_ref, *outs):
    for k in range(members):

        @pl.when(pl.program_id(0) == k)
        def _():
            outs[k][...] = mm(a_ref[...], w_ref[...]).astype(BF16)


def project(head, attention, weight, members):
    rows, depth = attention.shape
    width = weight.shape[1] // members
    whole = pl.BlockSpec((rows, width), lambda k, *_: (0, 0))
    return pl.pallas_call(
        functools.partial(project_kernel, members),
        out_shape=[jax.ShapeDtypeStruct((rows, width), BF16)] * members,
        grid_spec=pltpu.PrefetchScalarGridSpec(
            num_scalar_prefetch=1,
            grid=(members,),
            in_specs=[
                pl.BlockSpec((rows, depth), lambda k, *_: (0, 0)),
                pl.BlockSpec((depth, width), lambda k, head: (0, (head[0] + k) % members)),
            ],
            out_specs=[whole] * members,
        ),
        compiler_params=pltpu.CompilerParams(vmem_limit_bytes=32 << 20),
        cost_estimate=pl.CostEstimate(
            flops=2 * rows * depth * width * members,
            bytes_accessed=2 * depth * width * members,
            transcendentals=0,
        ),
        name="project",
    )(head, attention, weight)


def shifted(block, axis, distance):
    devices = range(lax.axis_size(axis))
    return lax.ppermute(
        block, axis, [(i - distance, i) for i in devices if i - distance in devices]
    )


def body(queries, keys, values, med_weight, coarse_weight, out_weight):
    n_seq = lax.axis_size("seq")
    members = lax.axis_size("head")
    position = lax.axis_index("seq")
    pos = position.astype(jnp.int32).reshape(1)
    head = lax.axis_index("head").astype(jnp.int32).reshape(1)

    med, coarse = pool(keys, values, med_weight, coarse_weight)
    inner = 8
    groups = [[a * inner + b for b in range(inner)] for a in range(n_seq // inner)]
    across = [[a * inner + b for a in range(n_seq // inner)] for b in range(inner)]
    near_coarse = lax.all_gather(coarse, "seq", axis=0, tiled=True, axis_index_groups=groups)
    all_coarse = lax.all_gather(near_coarse, "seq", axis=0, tiled=True, axis_index_groups=across)

    edge_keys = shifted(keys, "seq", 1)
    edge_values = shifted(values, "seq", 1)
    med2 = shifted(med, "seq", 2)
    med4 = shifted(med, "seq", 4)
    other = jnp.where(position % 2 == 0, med2, med4)
    med3 = lax.ppermute(other, "seq", [(i, i ^ 1) for i in range(n_seq)])

    acc, stat = near(pos, queries, keys, values, edge_keys, edge_values)
    chunks = 2
    pieces = []
    for c in range(chunks):
        attention = far(pos, queries, (med2, med3, med4), all_coarse, acc, stat, c, chunks)
        partial = project(head, attention, out_weight, members)
        total = partial[0].astype(F32)
        for k in (2, 1, 3):
            got = lax.ppermute(
                partial[k], "head", [(i, (i + k) % members) for i in range(members)]
            )
            total = total + got.astype(F32)
        pieces.append(total.astype(BF16))
    return jnp.concatenate(pieces, axis=0)


def solution(mesh):
    placed = (
        P("seq", "head"),
        P("seq", "head"),
        P("seq", "head"),
        P(None, "head", None),
        P(None, "head", None),
        P("head", None),
    )
    return jax.shard_map(
        body, mesh=mesh, in_specs=placed, out_specs=P("seq", "head"), check_vma=False
    )
```

time: 214 us -> 182 us (0.85)
  matrix products: 40.1 us -> 0 us
  Pallas kernels: 0 us -> 38.6 us
  local copies, waits for them, and re-layouts: 48.8 us -> 16.9 us
  other arithmetic: 17.6 us -> 2.62 us
  blocking collectives: 0 us -> 14.3 us
  waiting for transfers between devices: 65.3 us -> 70.2 us
    ppermute x8 -> x11, waiting for transfers between devices: 12.4 us -> 70.2 us  [the longest x4 57.8 us: shifted(): lax.ppermute(block, axis, [(i - distance, i) for i in devices if i - dist...]
    reduce_scatter x1 -> x0, waiting for transfers between devices: 48.2 us -> none  [body(): lax.psum_scatter(lax.optimization_barrier(term.astype(jnp.bfloat16)).asty...]
    dot_general x5 -> x0, matrix products: 40.1 us -> none  [the longest x1 15.2 us: attend_block(): jnp.einsum('hqk,khd->hqd', exp_scores.astype(jnp.bfloat16), value_all, pr...]
    pallas_call x0 -> x6, Pallas kernels: none -> 38.6 us  [the longest x2 18 us: far(): pl.pallas_call(functools.partial(far_kernel, part, rows // COARSE), out_s...]
    all_gather x0 -> x1, blocking collectives: none -> 14.3 us  [body(): lax.all_gather(coarse, 'seq', axis=0, tiled=True, axis_index_groups=groups)]
    reduce_sum x1 -> x0, other arithmetic: 13.8 us -> none  [attend_block(): row_total = jnp.sum(exp_scores, axis=-1)]
    unnamed x32 -> x35, local copies, waits for them, and re-layouts: 25.7 us -> 15.9 us
    reshape x6 -> x0, local copies, waits for them, and re-layouts: 9.26 us -> none  [the longest x3 4.73 us: body(): key_list.append(fetched_pair[0].reshape(med_rows, head_count, HEAD_DIM))]
  transfers between devices with their start and end apart: 10 -> 12, of which waited for: 3 -> 6; matrix products, arithmetic and copies ran while one was open for 17% -> 1% of each run, Pallas kernels for 0% -> 13%
where the time goes in v1:
time: 182 us; the launch traced here: 180 us
  waiting for transfers between devices  70.2 us (39%)
  Pallas kernels  38.6 us (21%)
  starting transfers between devices  23.7 us (13%)
  local copies, waits for them, and re-layouts  16.9 us (9%)
  blocking collectives  14.3 us (8%)
  between operations  13.6 us (7%)
  other arithmetic  2.62 us (1%)
    ppermute x4, waiting for transfers between devices, shifted(): lax.ppermute(block, axis, [(i - distance, i) for i in devices if i - dist...  57.8 us
    pallas_call x2, Pallas kernels, far(): pl.pallas_call(functools.partial(far_kernel, part, rows // COARSE), out_s...  18 us
    unnamed x35, local copies, waits for them, and re-layouts  15.9 us
    all_gather x1, blocking collectives, body(): lax.all_gather(coarse, 'seq', axis=0, tiled=True, axis_index_groups=groups)  14.3 us
    ppermute x4, starting transfers between devices, shifted(): lax.ppermute(block, axis, [(i - distance, i) for i in devices if i - dist...  13.8 us
    ppermute x6, waiting for transfers between devices, body(): lax.ppermute(partial[k], 'head', [(i, (i + k) % members) for i in range(m...  12.4 us
    pallas_call x1, Pallas kernels, near(): pl.pallas_call(functools.partial(near_kernel, 256), out_shape=(jax.ShapeD...  10.6 us
    ppermute x6, starting transfers between devices, body(): lax.ppermute(partial[k], 'head', [(i, (i + k) % members) for i in range(m...  9.91 us
  transfers between devices with their start and end apart: 12, of which 6 were waited for; matrix products, arithmetic and copies ran while one was open for 1% of the time, Pallas kernels for 13%

profile of v1, /device:TPU:96, one launch (start us, length us, event | category | flops | bytes accessed | tf_op | source)
XLA Modules:
  0.0 179.9 jit_solution(13160974763620248276)
XLA Ops:
  10.7 3.0 %pool.1 = (bf16[128,2048]{1,0:T(8,128)(2,1)}, bf16[8,2048]{1,0:T(8,128)(2,1)S(1)}) custom-call(bf16[512,1024]{1,0:T(8,128)(2,1)S(1)} %copy-done.9, bf16[512,1024]{1,0:T(8,128)(2,1)S(1)} %copy-done.12, f32[16,512]{1,0:T(8,128)S(1)} %copy.10.mw_ref, f32[16,512]{1,0:T(8,128)S(1)} %tile.25.cw_ref), custom_call_target="tpu_custom_call" | custom-call | flops 570425344 | bytes 3145728 | tf_op jit(solution)/shard_map/pool/pallas_call | solution.py:62
  13.7 14.3 %all_gather.6 = bf16[64,2048]{1,0:T(8,128)(2,1)} all-gather(bf16[8,2048]{1,0:T(8,128)(2,1)S(1)} %get-tuple-element.18), channel_id=1, replica_groups={{0,4,8,12,16,20,24,28},{32,36,40,44,48,52,56,60},{64,68,72,76,80,84,88,..., dimensions={0}, use_global_device_ids=true | all-gather | bytes 294912 | tf_op jit(solution)/shard_map/all_gather | solution.py:246
  27.9 3.4 %collective-permute-start.1 = (bf16[128,2048]{1,0:T(8,128)(2,1)}, bf16[128,2048]{1,0:T(8,128)(2,1)S(1)}, u32[]{:S(2)}, u32[]{:S(2)}) collective-permute-start(bf16[128,2048]{1,0:T(8,128)(2,1)} %get-tuple-element.17), channel_id=1, source_target_pairs={{0,16},{4,20},{8,24},{12,28},{16,32},{20,36},{24,40},{28,44},{32,4... | collective-permute-start | bytes 1572872 | tf_op jit(solution)/shard_map/ppermute | solution.py:230
  31.3 3.7 %collective-permute-start = (bf16[128,2048]{1,0:T(8,128)(2,1)}, bf16[128,2048]{1,0:T(8,128)(2,1)S(1)}, u32[]{:S(2)}, u32[]{:S(2)}) collective-permute-start(bf16[128,2048]{1,0:T(8,128)(2,1)} %get-tuple-element.17), channel_id=1, source_target_pairs={{0,8},{4,12},{8,16},{12,20},{16,24},{20,28},{24,32},{28,36},{32,40... | collective-permute-start | bytes 1572872 | tf_op jit(solution)/shard_map/ppermute | solution.py:230
  35.1 1.9 %collective-permute-start.3 = (bf16[512,1024]{1,0:T(8,128)(2,1)S(1)}, bf16[512,1024]{1,0:T(8,128)(2,1)}, u32[]{:S(2)}, u32[]{:S(2)}) collective-permute-start(bf16[512,1024]{1,0:T(8,128)(2,1)S(1)} %copy-done.10), channel_id=1, source_target_pairs={{0,4},{4,8},{8,12},{12,16},{16,20},{20,24},{24,28},{28,32},{32,36}... | collective-permute-start | bytes 3145736 | tf_op jit(solution)/shard_map/ppermute | solution.py:230
  37.0 4.8 %collective-permute-start.4 = (bf16[512,1024]{1,0:T(8,128)(2,1)S(1)}, bf16[512,1024]{1,0:T(8,128)(2,1)}, u32[]{:S(2)}, u32[]{:S(2)}) collective-permute-start(bf16[512,1024]{1,0:T(8,128)(2,1)S(1)} %copy-done.13), channel_id=1, source_target_pairs={{0,4},{4,8},{8,12},{12,16},{16,20},{20,24},{24,28},{28,32},{32,36}... | collective-permute-start | bytes 3145736 | tf_op jit(solution)/shard_map/ppermute | solution.py:230
  41.8 8.1 %collective-permute-done.1.m4k.m4v = bf16[128,2048]{1,0:T(8,128)(2,1)S(1)} collective-permute-done((bf16[128,2048]{1,0:T(8,128)(2,1)}, bf16[128,2048]{1,0:T(8,128)(2,1)S(1)}, u32[]{:S(2)}, u32[]{:S(2)}) %collective-permute-start.1) | collective-permute-done | bytes 524320 | tf_op jit(solution)/shard_map/ppermute | solution.py:230
  49.9 23.9 %collective-permute-done.m2k.m2v = bf16[128,2048]{1,0:T(8,128)(2,1)S(1)} collective-permute-done((bf16[128,2048]{1,0:T(8,128)(2,1)}, bf16[128,2048]{1,0:T(8,128)(2,1)S(1)}, u32[]{:S(2)}, u32[]{:S(2)}) %collective-permute-start) | collective-permute-done | bytes 524320 | tf_op jit(solution)/shard_map/ppermute | solution.py:230
  74.7 14.5 %collective-permute-done.3.ek_ref = bf16[512,1024]{1,0:T(8,128)(2,1)} collective-permute-done((bf16[512,1024]{1,0:T(8,128)(2,1)S(1)}, bf16[512,1024]{1,0:T(8,128)(2,1)}, u32[]{:S(2)}, u32[]{:S(2)}) %collective-permute-start.3) | collective-permute-done | bytes 1048608 | tf_op jit(solution)/shard_map/ppermute | solution.py:230
  89.2 11.2 %collective-permute-done.4.ev_ref = bf16[512,1024]{1,0:T(8,128)(2,1)} collective-permute-done((bf16[512,1024]{1,0:T(8,128)(2,1)S(1)}, bf16[512,1024]{1,0:T(8,128)(2,1)}, u32[]{:S(2)}, u32[]{:S(2)}) %collective-permute-start.4) | collective-permute-done | bytes 1048608 | tf_op jit(solution)/shard_map/ppermute | solution.py:230
  104.1 10.6 %near.1 = (f32[512,1024]{1,0:T(8,128)S(1)}, f32[8,512,128]{2,1,0:T(8,128)S(1)}) custom-call(s32[1]{0:T(128)} %bitcast.1.pos_ref, bf16[512,1024]{1,0:T(8,128)(2,1)S(1)} %copy-done.6, bf16[512,1024]{1,0:T(8,128)(2,1)S(1)} %copy-done.11, bf16[512,1024]{1,0:T(8,128)(2,1)S(1)} %copy-done.14, bf16[512,1024]{1,0:T(8,128)(2,1)} %collective-permute-done.3.ek_ref, ...), custom_call_target="tpu_custom_call" | custom-call | flops 2147483648 | bytes 9437184 | tf_op jit(solution)/shard_map/near/pallas_call | solution.py:112
  114.7 1.3 copy-done.3
  116.0 1.6 copy-done
  117.6 1.6 copy-done.4
  120.4 9.0 %far.2.a_ref = bf16[256,1024]{1,0:T(8,128)(2,1)S(1)} custom-call(s32[1]{0:T(128)} %bitcast.1.pos_ref, bf16[512,1024]{1,0:T(8,128)(2,1)S(1)} %copy-done.7, bf16[128,2048]{1,0:T(8,128)(2,1)S(1)} %collective-permute-done.m2k.m2v, bf16[128,2048]{1,0:T(8,128)(2,1)S(1)} %collective-permute-done.m2k.m2v, bf16[128,2048]{1,0:T(8,128)(2,1)} %collective-permute-done.2.m3k.m3v, ...), custom_call_target="tpu_custom_call" | custom-call | flops 939524096 | bytes 6291456 | tf_op jit(solution)/shard_map/far/pallas_call | solution.py:173
  129.4 3.4 %copy-done.2 = bf16[1024,4096]{1,0:T(8,128)(2,1)S(1)} copy-done((bf16[1024,4096]{1,0:T(8,128)(2,1)S(1)}, bf16[1024,4096]{1,0:T(8,128)(2,1)}, u32[]{:S(2)}) %copy-start.2) | copy-done | bytes 8388632
  132.8 3.6 %project.2 = (bf16[256,1024]{1,0:T(8,128)(2,1)S(1)}, bf16[256,1024]{1,0:T(8,128)(2,1)S(1)}, bf16[256,1024]{1,0:T(8,128)(2,1)S(1)}, bf16[256,1024]{1,0:T(8,128)(2,1)S(1)}) custom-call(s32[1]{0:T(128)} %bitcast.head_ref, bf16[256,1024]{1,0:T(8,128)(2,1)S(1)} %far.2.a_ref, bf16[1024,4096]{1,0:T(8,128)(2,1)S(1)} %copy-done.2), custom_call_target="tpu_custom_call" | custom-call | flops 2147483648 | bytes 8388608 | tf_op jit(solution)/shard_map/project/pallas_call | solution.py:206
  136.4 3.3 %collective-permute-start.5 = (bf16[256,1024]{1,0:T(8,128)(2,1)S(1)}, bf16[256,1024]{1,0:T(8,128)(2,1)S(1)}, u32[]{:S(2)}, u32[]{:S(2)}) collective-permute-start(bf16[256,1024]{1,0:T(8,128)(2,1)S(1)} %get-tuple-element.22), channel_id=1, source_target_pairs={{0,2},{1,3},{2,0},{3,1},{4,6},{5,7},{6,4},{7,5},{8,10},{9,11},{10,... | collective-permute-start | bytes 1572872 | tf_op jit(solution)/shard_map/ppermute | solution.py:264
  140.3 2.6 %collective-permute-start.7 = (bf16[256,1024]{1,0:T(8,128)(2,1)S(1)}, bf16[256,1024]{1,0:T(8,128)(2,1)S(1)}, u32[]{:S(2)}, u32[]{:S(2)}) collective-permute-start(bf16[256,1024]{1,0:T(8,128)(2,1)S(1)} %get-tuple-element.24), channel_id=1, source_target_pairs={{0,3},{1,0},{2,1},{3,2},{4,7},{5,4},{6,5},{7,6},{8,11},{9,8},{10,9... | collective-permute-start | bytes 1572872 | tf_op jit(solution)/shard_map/ppermute | solution.py:264
  142.9 8.9 %far.3.a_ref = bf16[256,1024]{1,0:T(8,128)(2,1)S(1)} custom-call(s32[1]{0:T(128)} %bitcast.1.pos_ref, bf16[512,1024]{1,0:T(8,128)(2,1)S(1)} %copy-done.8, bf16[128,2048]{1,0:T(8,128)(2,1)S(1)} %collective-permute-done.m2k.m2v, bf16[128,2048]{1,0:T(8,128)(2,1)S(1)} %collective-permute-done.m2k.m2v, bf16[128,2048]{1,0:T(8,128)(2,1)} %collective-permute-done.2.m3k.m3v, ...), custom_call_target="tpu_custom_call" | custom-call | flops 939524096 | bytes 6291456 | tf_op jit(solution)/shard_map/far/pallas_call | solution.py:173
  151.9 3.6 %project.3 = (bf16[256,1024]{1,0:T(8,128)(2,1)S(1)}, bf16[256,1024]{1,0:T(8,128)(2,1)S(1)}, bf16[256,1024]{1,0:T(8,128)(2,1)S(1)}, bf16[256,1024]{1,0:T(8,128)(2,1)S(1)}) custom-call(s32[1]{0:T(128)} %bitcast.head_ref, bf16[256,1024]{1,0:T(8,128)(2,1)S(1)} %far.3.a_ref, bf16[1024,4096]{1,0:T(8,128)(2,1)S(1)} %bitcast.7), custom_call_target="tpu_custom_call" | custom-call | flops 2147483648 | bytes 8388608 | tf_op jit(solution)/shard_map/project/pallas_call | solution.py:206
  156.6 2.3 %collective-permute-start.10 = (bf16[256,1024]{1,0:T(8,128)(2,1)S(1)}, bf16[256,1024]{1,0:T(8,128)(2,1)S(1)}, u32[]{:S(2)}, u32[]{:S(2)}) collective-permute-start(bf16[256,1024]{1,0:T(8,128)(2,1)S(1)} %get-tuple-element.28), channel_id=1, source_target_pairs={{0,3},{1,0},{2,1},{3,2},{4,7},{5,4},{6,5},{7,6},{8,11},{9,8},{10,9... | collective-permute-start | bytes 1572872 | tf_op jit(solution)/shard_map/ppermute | solution.py:264
  159.3 7.1 %collective-permute-done.8 = bf16[256,1024]{1,0:T(8,128)(2,1)S(1)} collective-permute-done((bf16[256,1024]{1,0:T(8,128)(2,1)S(1)}, bf16[256,1024]{1,0:T(8,128)(2,1)S(1)}, u32[]{:S(2)}, u32[]{:S(2)}) %collective-permute-start.8) | collective-permute-done | bytes 524320 | tf_op jit(solution)/shard_map/ppermute | solution.py:264
  166.4 5.3 %collective-permute-done.9 = bf16[256,1024]{1,0:T(8,128)(2,1)S(1)} collective-permute-done((bf16[256,1024]{1,0:T(8,128)(2,1)S(1)}, bf16[256,1024]{1,0:T(8,128)(2,1)S(1)}, u32[]{:S(2)}, u32[]{:S(2)}) %collective-permute-start.9) | collective-permute-done | bytes 524320 | tf_op jit(solution)/shard_map/ppermute | solution.py:264
  (53 shorter events, 13.5 us)
Async XLA Ops:
  6.5 109.5 %all-gather.2.cloned.1.call-start = ((), (), s32[]{:S(2)}) async-start(), calls=%async_computation | async-start | bytes 2359296 | tf_op jit(solution)/shard_map/all_gather | solution.py:247
  8.2 1.2 copy-start.9
  10.7 24.4 %copy-start.10 = (bf16[512,1024]{1,0:T(8,128)(2,1)S(1)}, bf16[512,1024]{1,0:T(8,128)(2,1)}, u32[]{:S(2)}) copy-start(bf16[512,1024]{1,0:T(8,128)(2,1)} %k_ref.3) | copy-start | bytes 3145732
  10.7 26.3 %copy-start.13 = (bf16[512,1024]{1,0:T(8,128)(2,1)S(1)}, bf16[512,1024]{1,0:T(8,128)(2,1)}, u32[]{:S(2)}) copy-start(bf16[512,1024]{1,0:T(8,128)(2,1)} %v_ref.3) | copy-start | bytes 3145732
  27.9 22.0 %collective-permute-start.1 = (bf16[128,2048]{1,0:T(8,128)(2,1)}, bf16[128,2048]{1,0:T(8,128)(2,1)S(1)}, u32[]{:S(2)}, u32[]{:S(2)}) collective-permute-start(bf16[128,2048]{1,0:T(8,128)(2,1)} %get-tuple-element.17), channel_id=1, source_target_pairs={{0,16},{4,20},{8,24},{12,28},{16,32},{20,36},{24,40},{28,44},{32,4... | collective-permute-start | bytes 1572872 | tf_op jit(solution)/shard_map/ppermute | solution.py:230
  31.3 42.6 %collective-permute-start = (bf16[128,2048]{1,0:T(8,128)(2,1)}, bf16[128,2048]{1,0:T(8,128)(2,1)S(1)}, u32[]{:S(2)}, u32[]{:S(2)}) collective-permute-start(bf16[128,2048]{1,0:T(8,128)(2,1)} %get-tuple-element.17), channel_id=1, source_target_pairs={{0,8},{4,12},{8,16},{12,20},{16,24},{20,28},{24,32},{28,36},{32,40... | collective-permute-start | bytes 1572872 | tf_op jit(solution)/shard_map/ppermute | solution.py:230
  35.1 54.2 %collective-permute-start.3 = (bf16[512,1024]{1,0:T(8,128)(2,1)S(1)}, bf16[512,1024]{1,0:T(8,128)(2,1)}, u32[]{:S(2)}, u32[]{:S(2)}) collective-permute-start(bf16[512,1024]{1,0:T(8,128)(2,1)S(1)} %copy-done.10), channel_id=1, source_target_pairs={{0,4},{4,8},{8,12},{12,16},{16,20},{20,24},{24,28},{28,32},{32,36}... | collective-permute-start | bytes 3145736 | tf_op jit(solution)/shard_map/ppermute | solution.py:230
  37.0 63.4 %collective-permute-start.4 = (bf16[512,1024]{1,0:T(8,128)(2,1)S(1)}, bf16[512,1024]{1,0:T(8,128)(2,1)}, u32[]{:S(2)}, u32[]{:S(2)}) collective-permute-start(bf16[512,1024]{1,0:T(8,128)(2,1)S(1)} %copy-done.13), channel_id=1, source_target_pairs={{0,4},{4,8},{8,12},{12,16},{16,20},{20,24},{24,28},{28,32},{32,36}... | collective-permute-start | bytes 3145736 | tf_op jit(solution)/shard_map/ppermute | solution.py:230
  74.7 41.3 %collective-permute-start.2 = (bf16[128,2048]{1,0:T(8,128)(2,1)}, bf16[128,2048]{1,0:T(8,128)(2,1)}, u32[]{:S(2)}, u32[]{:S(2)}) collective-permute-start(bf16[128,2048]{1,0:T(8,128)(2,1)} %broadcast_select_fusion), channel_id=1, source_target_pairs={{0,4},{4,0},{8,12},{12,8},{16,20},{20,16},{24,28},{28,24},{32,36},... | collective-permute-start | bytes 1572872 | tf_op jit(solution)/shard_map/ppermute | solution.py:254
  114.7 1.3 copy-start.3
  116.0 1.6 copy-start
  117.6 1.6 copy-start.4
  120.4 22.5 %copy-start.8 = (bf16[512,1024]{1,0:T(8,128)(2,1)S(1)}, bf16[512,1024]{1,0:T(8,128)(2,1)}, u32[]{:S(2)}) copy-start(bf16[512,1024]{1,0:T(8,128)(2,1)} %q_ref.5) | copy-start | bytes 3145732
  129.4 3.4 %copy-start.2 = (bf16[1024,4096]{1,0:T(8,128)(2,1)S(1)}, bf16[1024,4096]{1,0:T(8,128)(2,1)}, u32[]{:S(2)}) copy-start(bf16[1024,4096]{1,0:T(8,128)(2,1)} %w_ref.3) | copy-start | bytes 25165828
  132.8 10.1 %copy-start.1 = (bf16[512,2048]{1,0:T(8,128)(2,1)S(1)}, bf16[512,2048]{1,0:T(8,128)(2,1)}, u32[]{:S(2)}) copy-start(bf16[512,2048]{1,0:T(8,128)(2,1)} %all-gather.2.cloned.1.call-done.ck.cv) | copy-start | bytes 6291460
  132.8 10.1 %copy-start.5 = (f32[8,512,128]{2,1,0:T(8,128)S(1)}, f32[8,512,128]{2,1,0:T(8,128)}, u32[]{:S(2)}) copy-start(f32[8,512,128]{2,1,0:T(8,128)} %copy-done.3) | copy-start | bytes 6291460
  132.8 19.0 %slice-start = ((s8[8388608]{0:T(1024)(128)(4,1)}), s8[4194304]{0:T(1024)(128)(4,1)S(1)}, s32[]{:S(2)}) async-start(s8[8388608]{0:T(1024)(128)(4,1)} %bitcast.6), calls=%async_computation.1 | async-start | bytes 8388608
  136.4 20.2 %collective-permute-start.5 = (bf16[256,1024]{1,0:T(8,128)(2,1)S(1)}, bf16[256,1024]{1,0:T(8,128)(2,1)S(1)}, u32[]{:S(2)}, u32[]{:S(2)}) collective-permute-start(bf16[256,1024]{1,0:T(8,128)(2,1)S(1)} %get-tuple-element.22), channel_id=1, source_target_pairs={{0,2},{1,3},{2,0},{3,1},{4,6},{5,7},{6,4},{7,5},{8,10},{9,11},{10,... | collective-permute-start | bytes 1572872 | tf_op jit(solution)/shard_map/ppermute | solution.py:264
  139.7 19.2 %collective-permute-start.6 = (bf16[256,1024]{1,0:T(8,128)(2,1)S(1)}, bf16[256,1024]{1,0:T(8,128)(2,1)S(1)}, u32[]{:S(2)}, u32[]{:S(2)}) collective-permute-start(bf16[256,1024]{1,0:T(8,128)(2,1)S(1)} %get-tuple-element.23), channel_id=1, source_target_pairs={{0,1},{1,2},{2,3},{3,0},{4,5},{5,6},{6,7},{7,4},{8,9},{9,10},{10,1... | collective-permute-start | bytes 1572872 | tf_op jit(solution)/shard_map/ppermute | solution.py:264
  140.3 11.5 %slice-start.1 = ((s8[8388608]{0:T(1024)(128)(4,1)}), s8[4194304]{0:T(1024)(128)(4,1)S(1)}, s32[]{:S(2)}) async-start(s8[8388608]{0:T(1024)(128)(4,1)} %bitcast.6), calls=%async_computation.2 | async-start | bytes 8388608
  140.3 18.6 %collective-permute-start.7 = (bf16[256,1024]{1,0:T(8,128)(2,1)S(1)}, bf16[256,1024]{1,0:T(8,128)(2,1)S(1)}, u32[]{:S(2)}, u32[]{:S(2)}) collective-permute-start(bf16[256,1024]{1,0:T(8,128)(2,1)S(1)} %get-tuple-element.24), channel_id=1, source_target_pairs={{0,3},{1,0},{2,1},{3,2},{4,7},{5,4},{6,5},{7,6},{8,11},{9,8},{10,9... | collective-permute-start | bytes 1572872 | tf_op jit(solution)/shard_map/ppermute | solution.py:264
  155.5 10.9 %collective-permute-start.8 = (bf16[256,1024]{1,0:T(8,128)(2,1)S(1)}, bf16[256,1024]{1,0:T(8,128)(2,1)S(1)}, u32[]{:S(2)}, u32[]{:S(2)}) collective-permute-start(bf16[256,1024]{1,0:T(8,128)(2,1)S(1)} %get-tuple-element.26), channel_id=1, source_target_pairs={{0,2},{1,3},{2,0},{3,1},{4,6},{5,7},{6,4},{7,5},{8,10},{9,11},{10,... | collective-permute-start | bytes 1572872 | tf_op jit(solution)/shard_map/ppermute | solution.py:264
  155.6 16.1 %collective-permute-start.9 = (bf16[256,1024]{1,0:T(8,128)(2,1)S(1)}, bf16[256,1024]{1,0:T(8,128)(2,1)S(1)}, u32[]{:S(2)}, u32[]{:S(2)}) collective-permute-start(bf16[256,1024]{1,0:T(8,128)(2,1)S(1)} %get-tuple-element.27), channel_id=1, source_target_pairs={{0,1},{1,2},{2,3},{3,0},{4,5},{5,6},{6,7},{7,4},{8,9},{9,10},{10,1... | collective-permute-start | bytes 1572872 | tf_op jit(solution)/shard_map/ppermute | solution.py:264
  156.6 15.1 %collective-permute-start.10 = (bf16[256,1024]{1,0:T(8,128)(2,1)S(1)}, bf16[256,1024]{1,0:T(8,128)(2,1)S(1)}, u32[]{:S(2)}, u32[]{:S(2)}) collective-permute-start(bf16[256,1024]{1,0:T(8,128)(2,1)S(1)} %get-tuple-element.28), channel_id=1, source_target_pairs={{0,3},{1,0},{2,1},{3,2},{4,7},{5,4},{6,5},{7,6},{8,11},{9,8},{10,9... | collective-permute-start | bytes 1572872 | tf_op jit(solution)/shard_map/ppermute | solution.py:264
  (5 other events, 6.1 us)
Sparse Core Ops, SparseCore 0:
  28.1 41.5 all-gather.1

commit v2 on v1

--- a/solution.py
+++ b/solution.py
@@ -12,6 +12,9 @@
 WIN = 512
 MED = 4
 COARSE = 64
+CHIPS_X = 4
+PLANE = 2 * CHIPS_X
+PLANES = 8
 NEG = -1e30
 EXP2_SCALE = math.log2(math.e) / math.sqrt(HEAD_DIM)
 F32 = jnp.float32
@@ -65,7 +68,7 @@
             jax.ShapeDtypeStruct((rows // MED, 2 * width), BF16),
             jax.ShapeDtypeStruct((rows // COARSE, 2 * width), BF16),
         ),
-        compiler_params=pltpu.CompilerParams(vmem_limit_bytes=32 << 20),
+        compiler_params=pltpu.CompilerParams(vmem_limit_bytes=60 << 20),
         cost_estimate=pl.CostEstimate(
             flops=4 * 136 * rows * 2 * width, bytes_accessed=3 << 20, transcendentals=0
         ),
@@ -121,7 +124,7 @@
             in_specs=[col] * 5,
             out_specs=(col, pl.BlockSpec((1, rows, 128), lambda h, *_: (h, 0, 0))),
         ),
-        compiler_params=pltpu.CompilerParams(vmem_limit_bytes=32 << 20),
+        compiler_params=pltpu.CompilerParams(vmem_limit_bytes=60 << 20),
         cost_estimate=pl.CostEstimate(
             flops=4 * rows * 2 * rows * width, bytes_accessed=9 << 20, transcendentals=0
         ),
@@ -130,19 +133,30 @@
 
 
 def far_kernel(
-    tile, per_coarse, pos_ref, q_ref, m2k, m2v, m3k, m3v, m4k, m4v, ck, cv, acc_ref, stat_ref, out_ref
+    tile, per_coarse, pos_ref, q_ref, m2k, m2v, m3k, m3v, m4k, m4v, mine, other, acc_ref, stat_ref, out_ref
 ):
     rows = q_ref.shape[0]
     pos = pos_ref[0]
-    n_coarse = ck.shape[0]
-    usable = lax.broadcasted_iota(jnp.int32, (1, n_coarse), 1) < pos * per_coarse
+    first = pos % 2 == 0
+    ck = jnp.where(first, mine[...], other[...])
+    cv = jnp.where(first, other[...], mine[...])
+    j = lax.broadcasted_iota(jnp.int32, (1, ck.shape[0]), 1)
+    pair = 2 * per_coarse
+    group = j // (pair * 2 * CHIPS_X)
+    step = jnp.where(group == 2, -1, jnp.where(group == 3, 2, group))
+    slot = j // (2 * pair) % CHIPS_X
+    half = j // pair % 2
+    core = j // per_coarse % 2
+    z = (pos // PLANE - step - 4 * half) & (PLANES - 1)
+    x = (pos % PLANE // 2 - slot) & (CHIPS_X - 1)
+    usable = z * PLANE + x * 2 + core < pos
     for i in range(rows // tile):
         at = pl.ds(i * tile, tile)
         q = q_ref[at, :]
         parts = []
         for distance, k in ((2, m2k), (3, m3k), (4, m4k)):
             parts.append(jnp.where(pos >= distance, mm_t(q, k[...]), NEG))
-        parts.append(jnp.where(usable, mm_t(q, ck[...]), NEG))
+        parts.append(jnp.where(usable, mm_t(q, ck), NEG))
         stat = stat_ref[0, at, :]
         near_peak, near_total = stat[:, 0:1], stat[:, 1:2]
         peak = near_peak
@@ -151,25 +165,28 @@
         shrink = jnp.exp2((near_peak - peak) * EXP2_SCALE)
         total = near_total * shrink
         acc = acc_ref[at, :] * shrink
-        for s, v in zip(parts, (m2v, m3v, m4v, cv)):
+        for s, v in zip(parts, (m2v[...], m3v[...], m4v[...], cv)):
             p = jnp.exp2((s - peak) * EXP2_SCALE)
             total += jnp.sum(p, axis=1, keepdims=True)
-            acc += mm(p.astype(BF16), v[...])
+            acc += mm(p.astype(BF16), v)
         out_ref[at, :] = (acc / total).astype(BF16)
 
 
-def far(position, queries, meds, coarse, acc, stat, chunk, chunks):
+def far(position, queries, meds, mine, other, acc, stat, chunk, chunks):
     rows, width = queries.shape
     heads = width // HEAD_DIM
     part = rows // chunks
-    n_med, n_coarse = meds[0].shape[0], coarse.shape[0]
+    n_med, n_coarse = meds[0].shape[0], mine.shape[0]
     col = pl.BlockSpec((part, HEAD_DIM), lambda h, *_: (chunk, h))
     summary = []
     operands = []
-    for x, n in ((meds[0], n_med), (meds[1], n_med), (meds[2], n_med), (coarse, n_coarse)):
-        summary.append(pl.BlockSpec((n, HEAD_DIM), lambda h, *_: (0, h)))
-        summary.append(pl.BlockSpec((n, HEAD_DIM), lambda h, *_: (0, heads + h)))
+    for x in meds:
+        summary.append(pl.BlockSpec((n_med, HEAD_DIM), lambda h, *_: (0, h)))
+        summary.append(pl.BlockSpec((n_med, HEAD_DIM), lambda h, *_: (0, heads + h)))
         operands += [x, x]
+    for x in (mine, other):
+        summary.append(pl.BlockSpec((n_coarse, HEAD_DIM), lambda h, *_: (0, h)))
+        operands.append(x)
     return pl.pallas_call(
         functools.partial(far_kernel, part, rows // COARSE),
         out_shape=jax.ShapeDtypeStruct((part, width), BF16),
@@ -181,7 +198,7 @@
             + [col, pl.BlockSpec((1, part, 128), lambda h, *_: (h, chunk, 0))],
             out_specs=pl.BlockSpec((part, HEAD_DIM), lambda h, *_: (0, h)),
         ),
-        compiler_params=pltpu.CompilerParams(vmem_limit_bytes=32 << 20),
+        compiler_params=pltpu.CompilerParams(vmem_limit_bytes=60 << 20),
         cost_estimate=pl.CostEstimate(
             flops=4 * part * (3 * n_med + n_coarse) * width,
             bytes_accessed=6 << 20,
@@ -215,7 +232,7 @@
             ],
             out_specs=[whole] * members,
         ),
-        compiler_params=pltpu.CompilerParams(vmem_limit_bytes=32 << 20),
+        compiler_params=pltpu.CompilerParams(vmem_limit_bytes=60 << 20),
         cost_estimate=pl.CostEstimate(
             flops=2 * rows * depth * width * members,
             bytes_accessed=2 * depth * width * members,
@@ -240,24 +257,57 @@
     head = lax.axis_index("head").astype(jnp.int32).reshape(1)
 
     med, coarse = pool(keys, values, med_weight, coarse_weight)
-    inner = 8
-    groups = [[a * inner + b for b in range(inner)] for a in range(n_seq // inner)]
-    across = [[a * inner + b for a in range(n_seq // inner)] for b in range(inner)]
-    near_coarse = lax.all_gather(coarse, "seq", axis=0, tiled=True, axis_index_groups=groups)
-    all_coarse = lax.all_gather(near_coarse, "seq", axis=0, tiled=True, axis_index_groups=across)
+    core0 = position % 2 == 0
+    swap = [(i, i ^ 1) for i in range(n_seq)]
+
+    def place(z, x, core):
+        return z * PLANE + x * 2 + core
+
+    def move(block, dz, dx):
+        route = [
+            (place(z, x, c), place((z + dz) % PLANES, (x + dx) % CHIPS_X, c))
+            for z in range(PLANES)
+            for x in range(CHIPS_X)
+            for c in range(2)
+        ]
+        return lax.ppermute(block, "seq", route)
 
     edge_keys = shifted(keys, "seq", 1)
     edge_values = shifted(values, "seq", 1)
+
+    width = keys.shape[1]
+    coarse_k, coarse_v = coarse[:, :width], coarse[:, width:]
+    kept = jnp.where(core0, coarse_k, coarse_v)
+    swapped = lax.ppermute(jnp.where(core0, coarse_v, coarse_k), "seq", swap)
+    pair = jnp.where(
+        core0, jnp.concatenate([kept, swapped], 0), jnp.concatenate([swapped, kept], 0)
+    )
+    quad = jnp.concatenate([pair, move(pair, 4, 0)], 0)
+    ring = jnp.concatenate([quad] + [move(quad, 0, d) for d in range(1, CHIPS_X)], 0)
+
+    turned = move(med, 0, -1)
+    last = [
+        (place(z, x, c), place(z + (x + 1) % CHIPS_X // 2, (x - 1) % CHIPS_X, c))
+        for z in range(PLANES)
+        for x in range(CHIPS_X)
+        for c in range(2)
+        if z + (x + 1) % CHIPS_X // 2 < PLANES
+    ]
+    med4 = lax.ppermute(turned, "seq", last)
+    edge_keys, edge_values, ring, med = lax.optimization_barrier(
+        (edge_keys, edge_values, ring, med)
+    )
+    rings = [move(ring, d, 0) for d in (1, -1, 2)]
     med2 = shifted(med, "seq", 2)
-    med4 = shifted(med, "seq", 4)
-    other = jnp.where(position % 2 == 0, med2, med4)
-    med3 = lax.ppermute(other, "seq", [(i, i ^ 1) for i in range(n_seq)])
-
     acc, stat = near(pos, queries, keys, values, edge_keys, edge_values)
+    rings, med2, med4, acc, stat = lax.optimization_barrier((rings, med2, med4, acc, stat))
+    mine = jnp.concatenate([ring] + rings, 0)
+    other = lax.ppermute(mine, "seq", swap)
+    med3 = lax.ppermute(jnp.where(core0, med2, med4), "seq", swap)
     chunks = 2
     pieces = []
     for c in range(chunks):
-        attention = far(pos, queries, (med2, med3, med4), all_coarse, acc, stat, c, chunks)
+        attention = far(pos, queries, (med2, med3, med4), mine, other, acc, stat, c, chunks)
         partial = project(head, attention, out_weight, members)
         total = partial[0].astype(F32)
         for k in (2, 1, 3):

time: 182 us -> 151 us (0.83)
  the two profiles are of different devices: /device:TPU:96 before, /device:TPU:38 now
where the time goes in v2:
time: 151 us
  waiting for transfers between devices  52.4 us (35%)
  Pallas kernels  49.9 us (33%)
  starting transfers between devices  40.7 us (27%)
  local copies, waits for them, and re-layouts  4.82 us (3%)
  other arithmetic  2.57 us (2%)
    ppermute x8, waiting for transfers between devices, move(): return lax.ppermute(block, 'seq', route)  26 us
    ppermute x6, waiting for transfers between devices, body(): lax.ppermute(partial[k], 'head', [(i, (i + k) % members) for i in range(m...  22.6 us
    pallas_call x2, Pallas kernels, far(): pl.pallas_call(functools.partial(far_kernel, part, rows // COARSE), out_s...  19.9 us
    ppermute x8, starting transfers between devices, move(): return lax.ppermute(block, 'seq', route)  18.2 us
    pallas_call x2, Pallas kernels, project(): pl.pallas_call(functools.partial(project_kernel, members), out_shape=[jax...  14 us
    pallas_call x1, Pallas kernels, near(): pl.pallas_call(functools.partial(near_kernel, 256), out_shape=(jax.ShapeD...  11.4 us
    ppermute x3, starting transfers between devices, shifted(): lax.ppermute(block, axis, [(i - distance, i) for i in devices if i - dist...  9.95 us
    ppermute x6, starting transfers between devices, body(): lax.ppermute(partial[k], 'head', [(i, (i + k) % members) for i in range(m...  9.74 us
  transfers between devices with their start and end apart: 21, of which 12 were waited for; matrix products, arithmetic and copies ran while one was open for 3% of the time, Pallas kernels for 22%

profile of v2, /device:TPU:38, one launch (start us, length us, event | category | flops | bytes accessed | tf_op | source)
XLA Modules:
  0.0 150.6 jit_solution(16522853732915332946)
XLA Ops:
  0.0 1.9 %collective-permute-start = (bf16[512,1024]{1,0:T(8,128)(2,1)}, bf16[512,1024]{1,0:T(8,128)(2,1)S(1)}, u32[]{:S(2)}, u32[]{:S(2)}) collective-permute-start(bf16[512,1024]{1,0:T(8,128)(2,1)} %k_ref.3), channel_id=1, source_target_pairs={{0,4},{4,8},{8,12},{12,16},{16,20},{20,24},{24,28},{28,32},{32,36}... | collective-permute-start | bytes 3145736 | tf_op jit(solution)/shard_map/ppermute | solution.py:247
  1.9 3.8 %collective-permute-start.1 = (bf16[512,1024]{1,0:T(8,128)(2,1)}, bf16[512,1024]{1,0:T(8,128)(2,1)S(1)}, u32[]{:S(2)}, u32[]{:S(2)}) collective-permute-start(bf16[512,1024]{1,0:T(8,128)(2,1)} %v_ref.3), channel_id=1, source_target_pairs={{0,4},{4,8},{8,12},{12,16},{16,20},{20,24},{24,28},{28,32},{32,36}... | collective-permute-start | bytes 3145736 | tf_op jit(solution)/shard_map/ppermute | solution.py:247
  8.7 4.5 %pool.1 = (bf16[128,2048]{1,0:T(8,128)(2,1)}, bf16[8,2048]{1,0:T(8,128)(2,1)}) custom-call(bf16[512,1024]{1,0:T(8,128)(2,1)} %k_ref.3, bf16[512,1024]{1,0:T(8,128)(2,1)} %v_ref.3, f32[16,512]{1,0:T(8,128)} %copy.10.mw_ref, f32[16,512]{1,0:T(8,128)} %tile.25.cw_ref), custom_call_target="tpu_custom_call" | custom-call | flops 570425344 | bytes 3145728 | tf_op jit(solution)/shard_map/pool/pallas_call | solution.py:65
  15.2 5.5 %collective-permute-start.3 = (bf16[16,1024]{1,0:T(8,128)(2,1)S(1)}, bf16[16,1024]{1,0:T(8,128)(2,1)S(1)}, u32[]{:S(2)}, u32[]{:S(2)}) collective-permute-start(bf16[16,1024]{1,0:T(8,128)(2,1)S(1)} %get-tuple-element.52), channel_id=1, source_target_pairs={{0,128},{4,132},{8,136},{12,140},{16,144},{20,148},{24,152},{28,15... | collective-permute-start | bytes 98312 | tf_op jit(solution)/shard_map/ppermute | solution.py:273
  23.6 2.7 %collective-permute-start.4 = (bf16[32,1024]{1,0:T(8,128)(2,1)S(1)}, bf16[32,1024]{1,0:T(8,128)(2,1)S(1)}, u32[]{:S(2)}, u32[]{:S(2)}) collective-permute-start(bf16[32,1024]{1,0:T(8,128)(2,1)S(1)} %pad_maximum_fusion.1), channel_id=1, source_target_pairs={{0,8},{4,12},{8,16},{12,20},{16,24},{20,28},{24,0},{28,4},{32,40},... | collective-permute-start | bytes 196616 | tf_op jit(solution)/shard_map/ppermute | solution.py:273
  26.3 2.4 %collective-permute-done.4 = bf16[32,1024]{1,0:T(8,128)(2,1)S(1)} collective-permute-done((bf16[32,1024]{1,0:T(8,128)(2,1)S(1)}, bf16[32,1024]{1,0:T(8,128)(2,1)S(1)}, u32[]{:S(2)}, u32[]{:S(2)}) %collective-permute-start.4) | collective-permute-done | bytes 65568 | tf_op jit(solution)/shard_map/ppermute | solution.py:273
  28.7 1.7 %collective-permute-start.5 = (bf16[32,1024]{1,0:T(8,128)(2,1)S(1)}, bf16[32,1024]{1,0:T(8,128)(2,1)S(1)}, u32[]{:S(2)}, u32[]{:S(2)}) collective-permute-start(bf16[32,1024]{1,0:T(8,128)(2,1)S(1)} %pad_maximum_fusion.1), channel_id=1, source_target_pairs={{0,16},{4,20},{8,24},{12,28},{16,0},{20,4},{24,8},{28,12},{32,48},... | collective-permute-start | bytes 196616 | tf_op jit(solution)/shard_map/ppermute | solution.py:273
  30.4 7.6 %collective-permute-done.5 = bf16[32,1024]{1,0:T(8,128)(2,1)S(1)} collective-permute-done((bf16[32,1024]{1,0:T(8,128)(2,1)S(1)}, bf16[32,1024]{1,0:T(8,128)(2,1)S(1)}, u32[]{:S(2)}, u32[]{:S(2)}) %collective-permute-start.5) | collective-permute-done | bytes 65568 | tf_op jit(solution)/shard_map/ppermute | solution.py:273
  38.6 1.9 %collective-permute-start.12 = (bf16[128,2048]{1,0:T(8,128)(2,1)}, bf16[128,2048]{1,0:T(8,128)(2,1)S(1)}, u32[]{:S(2)}, u32[]{:S(2)}) collective-permute-start(bf16[128,2048]{1,0:T(8,128)(2,1)} %collective-permute-done.11), channel_id=1, source_target_pairs={{0,24},{4,28},{8,32},{12,36},{16,40},{20,44},{24,16},{28,20},{32,5... | collective-permute-start | bytes 1572872 | tf_op jit(solution)/shard_map/ppermute | solution.py:296
  41.5 4.2 %collective-permute-start.10 = (bf16[128,2048]{1,0:T(8,128)(2,1)}, bf16[128,2048]{1,0:T(8,128)(2,1)S(1)}, u32[]{:S(2)}, u32[]{:S(2)}) collective-permute-start(bf16[128,2048]{1,0:T(8,128)(2,1)} %get-tuple-element.31), channel_id=1, source_target_pairs={{0,8},{4,12},{8,16},{12,20},{16,24},{20,28},{24,32},{28,36},{32,40... | collective-permute-start | bytes 1572872 | tf_op jit(solution)/shard_map/ppermute | solution.py:247
  45.7 4.6 %collective-permute-start.9 = (bf16[128,1024]{1,0:T(8,128)(2,1)S(1)}, bf16[128,1024]{1,0:T(8,128)(2,1)S(1)}, u32[]{:S(2)}, u32[]{:S(2)}) collective-permute-start(bf16[128,1024]{1,0:T(8,128)(2,1)S(1)} %constant_dynamic-update-slice_fusion), channel_id=1, source_target_pairs={{0,64},{4,68},{8,72},{12,76},{16,80},{20,84},{24,88},{28,92},{32,9... | collective-permute-start | bytes 786440 | tf_op jit(solution)/shard_map/ppermute | solution.py:273
  50.4 2.0 %collective-permute-start.7 = (bf16[128,1024]{1,0:T(8,128)(2,1)S(1)}, bf16[128,1024]{1,0:T(8,128)(2,1)S(1)}, u32[]{:S(2)}, u32[]{:S(2)}) collective-permute-start(bf16[128,1024]{1,0:T(8,128)(2,1)S(1)} %constant_dynamic-update-slice_fusion), channel_id=1, source_target_pairs={{0,32},{4,36},{8,40},{12,44},{16,48},{20,52},{24,56},{28,60},{32,6... | collective-permute-start | bytes 786440 | tf_op jit(solution)/shard_map/ppermute | solution.py:273
  52.4 11.4 %near.1 = (f32[512,1024]{1,0:T(8,128)}, f32[8,512,128]{2,1,0:T(8,128)}) custom-call(s32[1]{0:T(128)} %bitcast.1.pos_ref, bf16[512,1024]{1,0:T(8,128)(2,1)} %q_ref.5, bf16[512,1024]{1,0:T(8,128)(2,1)} %k_ref.3, bf16[512,1024]{1,0:T(8,128)(2,1)} %v_ref.3, bf16[512,1024]{1,0:T(8,128)(2,1)} %copy-done.6, bf16[512,1024]{1,0:T(8,128)(2,1)} %copy-done.7), custom_call_target="tpu_custom_call" | custom-call | flops 2147483648 | bytes 9437184 | tf_op jit(solution)/shard_map/near/pallas_call | solution.py:115
  63.8 14.1 %collective-permute-done.7 = bf16[128,1024]{1,0:T(8,128)(2,1)S(1)} collective-permute-done((bf16[128,1024]{1,0:T(8,128)(2,1)S(1)}, bf16[128,1024]{1,0:T(8,128)(2,1)S(1)}, u32[]{:S(2)}, u32[]{:S(2)}) %collective-permute-start.7) | collective-permute-done | bytes 262176 | tf_op jit(solution)/shard_map/ppermute | solution.py:273
  79.0 2.6 %collective-permute-done.13.m3k.m3v = bf16[128,2048]{1,0:T(8,128)(2,1)S(1)} collective-permute-done((bf16[128,2048]{1,0:T(8,128)(2,1)S(1)}, bf16[128,2048]{1,0:T(8,128)(2,1)S(1)}, u32[]{:S(2)}, u32[]{:S(2)}) %collective-permute-start.13) | collective-permute-done | bytes 524320 | tf_op jit(solution)/shard_map/ppermute | solution.py:306
  82.4 10.0 %far.2.a_ref = bf16[256,1024]{1,0:T(8,128)(2,1)} custom-call(s32[1]{0:T(128)} %bitcast.1.pos_ref, bf16[512,1024]{1,0:T(8,128)(2,1)} %q_ref.5, bf16[128,2048]{1,0:T(8,128)(2,1)} %copy-done.1, bf16[128,2048]{1,0:T(8,128)(2,1)} %copy-done.1, bf16[128,2048]{1,0:T(8,128)(2,1)} %copy-done.2, bf16[128,2048]{1,0:T(8,128)(2,1)} %copy-done.2, ...), custom_call_target="tpu_custom_call" | custom-call | flops 939524096 | bytes 6291456 | tf_op jit(solution)/shard_map/far/pallas_call | solution.py:190
  92.4 7.0 %project.2 = (bf16[256,1024]{1,0:T(8,128)(2,1)}, bf16[256,1024]{1,0:T(8,128)(2,1)}, bf16[256,1024]{1,0:T(8,128)(2,1)}, bf16[256,1024]{1,0:T(8,128)(2,1)}) custom-call(s32[1]{0:T(128)} %bitcast.head_ref, bf16[256,1024]{1,0:T(8,128)(2,1)} %far.2.a_ref, bf16[1024,4096]{1,0:T(8,128)(2,1)} %w_ref.3), custom_call_target="tpu_custom_call" | custom-call | flops 2147483648 | bytes 8388608 | tf_op jit(solution)/shard_map/project/pallas_call | solution.py:223
  99.3 3.2 %collective-permute-start.15 = (bf16[256,1024]{1,0:T(8,128)(2,1)}, bf16[256,1024]{1,0:T(8,128)(2,1)S(1)}, u32[]{:S(2)}, u32[]{:S(2)}) collective-permute-start(bf16[256,1024]{1,0:T(8,128)(2,1)} %get-tuple-element.44), channel_id=1, source_target_pairs={{0,2},{1,3},{2,0},{3,1},{4,6},{5,7},{6,4},{7,5},{8,10},{9,11},{10,... | collective-permute-start | bytes 1572872 | tf_op jit(solution)/shard_map/ppermute | solution.py:314
  103.2 2.6 %collective-permute-start.17 = (bf16[256,1024]{1,0:T(8,128)(2,1)}, bf16[256,1024]{1,0:T(8,128)(2,1)S(1)}, u32[]{:S(2)}, u32[]{:S(2)}) collective-permute-start(bf16[256,1024]{1,0:T(8,128)(2,1)} %get-tuple-element.46), channel_id=1, source_target_pairs={{0,3},{1,0},{2,1},{3,2},{4,7},{5,4},{6,5},{7,6},{8,11},{9,8},{10,9... | collective-permute-start | bytes 1572872 | tf_op jit(solution)/shard_map/ppermute | solution.py:314
  105.8 10.0 %far.3.a_ref = bf16[256,1024]{1,0:T(8,128)(2,1)} custom-call(s32[1]{0:T(128)} %bitcast.1.pos_ref, bf16[512,1024]{1,0:T(8,128)(2,1)} %q_ref.5, bf16[128,2048]{1,0:T(8,128)(2,1)} %copy-done.1, bf16[128,2048]{1,0:T(8,128)(2,1)} %copy-done.1, bf16[128,2048]{1,0:T(8,128)(2,1)} %copy-done.2, bf16[128,2048]{1,0:T(8,128)(2,1)} %copy-done.2, ...), custom_call_target="tpu_custom_call" | custom-call | flops 939524096 | bytes 6291456 | tf_op jit(solution)/shard_map/far/pallas_call | solution.py:190
  115.7 7.1 %project.3 = (bf16[256,1024]{1,0:T(8,128)(2,1)}, bf16[256,1024]{1,0:T(8,128)(2,1)}, bf16[256,1024]{1,0:T(8,128)(2,1)}, bf16[256,1024]{1,0:T(8,128)(2,1)}) custom-call(s32[1]{0:T(128)} %bitcast.head_ref, bf16[256,1024]{1,0:T(8,128)(2,1)} %far.3.a_ref, bf16[1024,4096]{1,0:T(8,128)(2,1)} %w_ref.3), custom_call_target="tpu_custom_call" | custom-call | flops 2147483648 | bytes 8388608 | tf_op jit(solution)/shard_map/project/pallas_call | solution.py:223
  123.7 2.4 %collective-permute-start.20 = (bf16[256,1024]{1,0:T(8,128)(2,1)}, bf16[256,1024]{1,0:T(8,128)(2,1)S(1)}, u32[]{:S(2)}, u32[]{:S(2)}) collective-permute-start(bf16[256,1024]{1,0:T(8,128)(2,1)} %get-tuple-element.50), channel_id=1, source_target_pairs={{0,3},{1,0},{2,1},{3,2},{4,7},{5,4},{6,5},{7,6},{8,11},{9,8},{10,9... | collective-permute-start | bytes 1572872 | tf_op jit(solution)/shard_map/ppermute | solution.py:314
  127.8 11.6 %collective-permute-done.18 = bf16[256,1024]{1,0:T(8,128)(2,1)S(1)} collective-permute-done((bf16[256,1024]{1,0:T(8,128)(2,1)}, bf16[256,1024]{1,0:T(8,128)(2,1)S(1)}, u32[]{:S(2)}, u32[]{:S(2)}) %collective-permute-start.18) | collective-permute-done | bytes 524320 | tf_op jit(solution)/shard_map/ppermute | solution.py:314
  139.4 9.3 %collective-permute-done.19 = bf16[256,1024]{1,0:T(8,128)(2,1)S(1)} collective-permute-done((bf16[256,1024]{1,0:T(8,128)(2,1)}, bf16[256,1024]{1,0:T(8,128)(2,1)S(1)}, u32[]{:S(2)}, u32[]{:S(2)}) %collective-permute-start.19) | collective-permute-done | bytes 524320 | tf_op jit(solution)/shard_map/ppermute | solution.py:314
  (61 shorter events, 16.3 us)
Async XLA Ops:
  0.0 40.5 %collective-permute-start = (bf16[512,1024]{1,0:T(8,128)(2,1)}, bf16[512,1024]{1,0:T(8,128)(2,1)S(1)}, u32[]{:S(2)}, u32[]{:S(2)}) collective-permute-start(bf16[512,1024]{1,0:T(8,128)(2,1)} %k_ref.3), channel_id=1, source_target_pairs={{0,4},{4,8},{8,12},{12,16},{16,20},{20,24},{24,28},{28,32},{32,36}... | collective-permute-start | bytes 3145736 | tf_op jit(solution)/shard_map/ppermute | solution.py:247
  1.9 38.6 %collective-permute-start.1 = (bf16[512,1024]{1,0:T(8,128)(2,1)}, bf16[512,1024]{1,0:T(8,128)(2,1)S(1)}, u32[]{:S(2)}, u32[]{:S(2)}) collective-permute-start(bf16[512,1024]{1,0:T(8,128)(2,1)} %v_ref.3), channel_id=1, source_target_pairs={{0,4},{4,8},{8,12},{12,16},{16,20},{20,24},{24,28},{28,32},{32,36}... | collective-permute-start | bytes 3145736 | tf_op jit(solution)/shard_map/ppermute | solution.py:247
  14.0 1.2 collective-permute-start.2
  15.2 7.9 %collective-permute-start.3 = (bf16[16,1024]{1,0:T(8,128)(2,1)S(1)}, bf16[16,1024]{1,0:T(8,128)(2,1)S(1)}, u32[]{:S(2)}, u32[]{:S(2)}) collective-permute-start(bf16[16,1024]{1,0:T(8,128)(2,1)S(1)} %get-tuple-element.52), channel_id=1, source_target_pairs={{0,128},{4,132},{8,136},{12,140},{16,144},{20,148},{24,152},{28,15... | collective-permute-start | bytes 98312 | tf_op jit(solution)/shard_map/ppermute | solution.py:273
  20.6 18.0 %collective-permute-start.11 = (bf16[128,2048]{1,0:T(8,128)(2,1)}, bf16[128,2048]{1,0:T(8,128)(2,1)}, u32[]{:S(2)}, u32[]{:S(2)}) collective-permute-start(bf16[128,2048]{1,0:T(8,128)(2,1)} %get-tuple-element.31), channel_id=1, source_target_pairs={{0,24},{4,28},{8,0},{12,4},{16,8},{20,12},{24,16},{28,20},{32,56},... | collective-permute-start | bytes 1572872 | tf_op jit(solution)/shard_map/ppermute | solution.py:273
  23.1 15.5 %collective-permute-start.6 = (bf16[32,1024]{1,0:T(8,128)(2,1)S(1)}, bf16[32,1024]{1,0:T(8,128)(2,1)S(1)}, u32[]{:S(2)}, u32[]{:S(2)}) collective-permute-start(bf16[32,1024]{1,0:T(8,128)(2,1)S(1)} %pad_maximum_fusion.1), channel_id=1, source_target_pairs={{0,24},{4,28},{8,0},{12,4},{16,8},{20,12},{24,16},{28,20},{32,56},... | collective-permute-start | bytes 196616 | tf_op jit(solution)/shard_map/ppermute | solution.py:273
  23.6 5.0 %collective-permute-start.4 = (bf16[32,1024]{1,0:T(8,128)(2,1)S(1)}, bf16[32,1024]{1,0:T(8,128)(2,1)S(1)}, u32[]{:S(2)}, u32[]{:S(2)}) collective-permute-start(bf16[32,1024]{1,0:T(8,128)(2,1)S(1)} %pad_maximum_fusion.1), channel_id=1, source_target_pairs={{0,8},{4,12},{8,16},{12,20},{16,24},{20,28},{24,0},{28,4},{32,40},... | collective-permute-start | bytes 196616 | tf_op jit(solution)/shard_map/ppermute | solution.py:273
  28.7 9.3 %collective-permute-start.5 = (bf16[32,1024]{1,0:T(8,128)(2,1)S(1)}, bf16[32,1024]{1,0:T(8,128)(2,1)S(1)}, u32[]{:S(2)}, u32[]{:S(2)}) collective-permute-start(bf16[32,1024]{1,0:T(8,128)(2,1)S(1)} %pad_maximum_fusion.1), channel_id=1, source_target_pairs={{0,16},{4,20},{8,24},{12,28},{16,0},{20,4},{24,8},{28,12},{32,48},... | collective-permute-start | bytes 196616 | tf_op jit(solution)/shard_map/ppermute | solution.py:273
  38.6 25.2 %collective-permute-start.12 = (bf16[128,2048]{1,0:T(8,128)(2,1)}, bf16[128,2048]{1,0:T(8,128)(2,1)S(1)}, u32[]{:S(2)}, u32[]{:S(2)}) collective-permute-start(bf16[128,2048]{1,0:T(8,128)(2,1)} %collective-permute-done.11), channel_id=1, source_target_pairs={{0,24},{4,28},{8,32},{12,36},{16,40},{20,44},{24,16},{28,20},{32,5... | collective-permute-start | bytes 1572872 | tf_op jit(solution)/shard_map/ppermute | solution.py:296
  41.5 36.4 %collective-permute-start.10 = (bf16[128,2048]{1,0:T(8,128)(2,1)}, bf16[128,2048]{1,0:T(8,128)(2,1)S(1)}, u32[]{:S(2)}, u32[]{:S(2)}) collective-permute-start(bf16[128,2048]{1,0:T(8,128)(2,1)} %get-tuple-element.31), channel_id=1, source_target_pairs={{0,8},{4,12},{8,16},{12,20},{16,24},{20,28},{24,32},{28,36},{32,40... | collective-permute-start | bytes 1572872 | tf_op jit(solution)/shard_map/ppermute | solution.py:247
  45.7 18.1 %collective-permute-start.9 = (bf16[128,1024]{1,0:T(8,128)(2,1)S(1)}, bf16[128,1024]{1,0:T(8,128)(2,1)S(1)}, u32[]{:S(2)}, u32[]{:S(2)}) collective-permute-start(bf16[128,1024]{1,0:T(8,128)(2,1)S(1)} %constant_dynamic-update-slice_fusion), channel_id=1, source_target_pairs={{0,64},{4,68},{8,72},{12,76},{16,80},{20,84},{24,88},{28,92},{32,9... | collective-permute-start | bytes 786440 | tf_op jit(solution)/shard_map/ppermute | solution.py:273
  50.4 13.5 %collective-permute-start.8 = (bf16[128,1024]{1,0:T(8,128)(2,1)S(1)}, bf16[128,1024]{1,0:T(8,128)(2,1)S(1)}, u32[]{:S(2)}, u32[]{:S(2)}) collective-permute-start(bf16[128,1024]{1,0:T(8,128)(2,1)S(1)} %constant_dynamic-update-slice_fusion), channel_id=1, source_target_pairs={{0,224},{4,228},{8,232},{12,236},{16,240},{20,244},{24,248},{28,25... | collective-permute-start | bytes 786440 | tf_op jit(solution)/shard_map/ppermute | solution.py:273
  50.4 27.6 %collective-permute-start.7 = (bf16[128,1024]{1,0:T(8,128)(2,1)S(1)}, bf16[128,1024]{1,0:T(8,128)(2,1)S(1)}, u32[]{:S(2)}, u32[]{:S(2)}) collective-permute-start(bf16[128,1024]{1,0:T(8,128)(2,1)S(1)} %constant_dynamic-update-slice_fusion), channel_id=1, source_target_pairs={{0,32},{4,36},{8,40},{12,44},{16,48},{20,52},{24,56},{28,60},{32,6... | collective-permute-start | bytes 786440 | tf_op jit(solution)/shard_map/ppermute | solution.py:273
  63.8 17.7 %copy-start = (bf16[128,2048]{1,0:T(8,128)(2,1)}, bf16[128,2048]{1,0:T(8,128)(2,1)S(1)}, u32[]{:S(2)}) copy-start(bf16[128,2048]{1,0:T(8,128)(2,1)S(1)} %collective-permute-done.12.m4k.m4v) | copy-start | bytes 1572868
  78.1 3.5 %collective-permute-start.14 = (bf16[512,1024]{1,0:T(8,128)(2,1)S(1)}, bf16[512,1024]{1,0:T(8,128)(2,1)}, u32[]{:S(2)}, u32[]{:S(2)}) collective-permute-start(bf16[512,1024]{1,0:T(8,128)(2,1)S(1)} %constant_dynamic-update-slice_fusion.5.mine), channel_id=1, source_target_pairs={{0,4},{4,0},{8,12},{12,8},{16,20},{20,16},{24,28},{28,24},{32,36},... | collective-permute-start | bytes 3145736 | tf_op jit(solution)/shard_map/ppermute | solution.py:305
  78.3 3.2 %collective-permute-start.13 = (bf16[128,2048]{1,0:T(8,128)(2,1)S(1)}, bf16[128,2048]{1,0:T(8,128)(2,1)S(1)}, u32[]{:S(2)}, u32[]{:S(2)}) collective-permute-start(bf16[128,2048]{1,0:T(8,128)(2,1)S(1)} %broadcast_select_fusion), channel_id=1, source_target_pairs={{0,4},{4,0},{8,12},{12,8},{16,20},{20,16},{24,28},{28,24},{32,36},... | collective-permute-start | bytes 1572872 | tf_op jit(solution)/shard_map/ppermute | solution.py:306
  99.3 24.4 %collective-permute-start.15 = (bf16[256,1024]{1,0:T(8,128)(2,1)}, bf16[256,1024]{1,0:T(8,128)(2,1)S(1)}, u32[]{:S(2)}, u32[]{:S(2)}) collective-permute-start(bf16[256,1024]{1,0:T(8,128)(2,1)} %get-tuple-element.44), channel_id=1, source_target_pairs={{0,2},{1,3},{2,0},{3,1},{4,6},{5,7},{6,4},{7,5},{8,10},{9,11},{10,... | collective-permute-start | bytes 1572872 | tf_op jit(solution)/shard_map/ppermute | solution.py:314
  102.5 23.9 %collective-permute-start.16 = (bf16[256,1024]{1,0:T(8,128)(2,1)}, bf16[256,1024]{1,0:T(8,128)(2,1)S(1)}, u32[]{:S(2)}, u32[]{:S(2)}) collective-permute-start(bf16[256,1024]{1,0:T(8,128)(2,1)} %get-tuple-element.45), channel_id=1, source_target_pairs={{0,1},{1,2},{2,3},{3,0},{4,5},{5,6},{6,7},{7,4},{8,9},{9,10},{10,1... | collective-permute-start | bytes 1572872 | tf_op jit(solution)/shard_map/ppermute | solution.py:314
  103.2 24.2 %collective-permute-start.17 = (bf16[256,1024]{1,0:T(8,128)(2,1)}, bf16[256,1024]{1,0:T(8,128)(2,1)S(1)}, u32[]{:S(2)}, u32[]{:S(2)}) collective-permute-start(bf16[256,1024]{1,0:T(8,128)(2,1)} %get-tuple-element.46), channel_id=1, source_target_pairs={{0,3},{1,0},{2,1},{3,2},{4,7},{5,4},{6,5},{7,6},{8,11},{9,8},{10,9... | collective-permute-start | bytes 1572872 | tf_op jit(solution)/shard_map/ppermute | solution.py:314
  115.7 11.7 %copy-start.4 = (bf16[256,1024]{1,0:T(8,128)(2,1)S(1)}, bf16[256,1024]{1,0:T(8,128)(2,1)}, u32[]{:S(2)}) copy-start(bf16[256,1024]{1,0:T(8,128)(2,1)} %get-tuple-element.43) | copy-start | bytes 1572868
  122.8 26.3 %copy-start.5 = (bf16[256,1024]{1,0:T(8,128)(2,1)S(1)}, bf16[256,1024]{1,0:T(8,128)(2,1)}, u32[]{:S(2)}) copy-start(bf16[256,1024]{1,0:T(8,128)(2,1)} %get-tuple-element.47) | copy-start | bytes 1572868
  122.8 16.6 %collective-permute-start.18 = (bf16[256,1024]{1,0:T(8,128)(2,1)}, bf16[256,1024]{1,0:T(8,128)(2,1)S(1)}, u32[]{:S(2)}, u32[]{:S(2)}) collective-permute-start(bf16[256,1024]{1,0:T(8,128)(2,1)} %get-tuple-element.48), channel_id=1, source_target_pairs={{0,2},{1,3},{2,0},{3,1},{4,6},{5,7},{6,4},{7,5},{8,10},{9,11},{10,... | collective-permute-start | bytes 1572872 | tf_op jit(solution)/shard_map/ppermute | solution.py:314
  122.8 25.9 %collective-permute-start.19 = (bf16[256,1024]{1,0:T(8,128)(2,1)}, bf16[256,1024]{1,0:T(8,128)(2,1)S(1)}, u32[]{:S(2)}, u32[]{:S(2)}) collective-permute-start(bf16[256,1024]{1,0:T(8,128)(2,1)} %get-tuple-element.49), channel_id=1, source_target_pairs={{0,1},{1,2},{2,3},{3,0},{4,5},{5,6},{6,7},{7,4},{8,9},{9,10},{10,1... | collective-permute-start | bytes 1572872 | tf_op jit(solution)/shard_map/ppermute | solution.py:314
  123.7 25.4 %collective-permute-start.20 = (bf16[256,1024]{1,0:T(8,128)(2,1)}, bf16[256,1024]{1,0:T(8,128)(2,1)S(1)}, u32[]{:S(2)}, u32[]{:S(2)}) collective-permute-start(bf16[256,1024]{1,0:T(8,128)(2,1)} %get-tuple-element.50), channel_id=1, source_target_pairs={{0,3},{1,0},{2,1},{3,2},{4,7},{5,4},{6,5},{7,6},{8,11},{9,8},{10,9... | collective-permute-start | bytes 1572872 | tf_op jit(solution)/shard_map/ppermute | solution.py:314
  (5 other events, 17.8 us)

commit v3 on v2

v3 whole, which is shorter than its diff:
```python
import functools
import math

import jax
import jax.numpy as jnp
from jax import lax
from jax.experimental import pallas as pl
from jax.experimental.pallas import tpu as pltpu
from jax.sharding import PartitionSpec as P

HEAD_DIM = 128
WIN = 512
MED = 4
COARSE = 64
CHIPS_X = 4
PLANE = 2 * CHIPS_X
PLANES = 8
NEG = -1e30
EXP2_SCALE = math.log2(math.e) / math.sqrt(HEAD_DIM)
F32 = jnp.float32
BF16 = jnp.bfloat16
HBM = pl.BlockSpec(memory_space=pltpu.HBM)
VMEM = pl.BlockSpec(memory_space=pltpu.VMEM)
SMEM = pl.BlockSpec(memory_space=pltpu.SMEM)


def in_hbm(x):
    return pltpu.with_memory_space_constraint(x, pltpu.HBM)


def mm(a, b):
    return lax.dot_general(a, b, (((1,), (0,)), ((), ())), preferred_element_type=F32)


def mm_t(a, b):
    return lax.dot_general(a, b, (((1,), (1,)), ((), ())), preferred_element_type=F32)


def head_cols(h):
    return pl.ds(h * HEAD_DIM, HEAD_DIM)


def fetch_heads(pairs, sems, heads):
    copies = []
    for h in range(heads):
        copies.append(
            [
                pltpu.make_async_copy(
                    src.at[:, head_cols(h)], dst.at[:, head_cols(h)], sems.at[t, h]
                )
                for t, (src, dst) in enumerate(pairs)
            ]
        )
        for copy in copies[h]:
            copy.start()
    return copies


def pool_kernel(
    heads, pos_ref, k_hbm, v_hbm, mw_ref, cw_ref, med_ref, kept_ref, sent_ref, k_ref, v_ref, rows_ref, sems
):
    copies = fetch_heads(((k_hbm, k_ref), (v_hbm, v_ref)), sems, heads)
    rows = k_ref.shape[0]
    n_med, n_coarse = rows // MED, rows // COARSE
    lane = lax.broadcasted_iota(jnp.int32, (heads, rows), 1)
    for slot, (ref, ratio) in enumerate(((mw_ref, MED), (cw_ref, COARSE))):
        at = lane % ratio
        for t in range(2):
            w = ref[t]
            spread = jnp.zeros((heads, rows), F32)
            for r in range(ratio):
                spread = jnp.where(at == r, w[:, r : r + 1], spread)
            high = spread.astype(BF16).astype(F32)
            rows_ref[slot, 0, t] = high
            rows_ref[slot, 1, t] = spread - high

    def on(n, ratio):
        source = lax.broadcasted_iota(jnp.int32, (n, rows), 1)
        return source // ratio == lax.broadcasted_iota(jnp.int32, (n, rows), 0)

    med_on, coarse_on = on(n_med, MED), on(n_coarse, COARSE)
    first = pos_ref[0] % 2 == 0
    for h in range(heads):
        for copy in copies[h]:
            copy.wait()
        coarse = []
        for t, ref in enumerate((k_ref, v_ref)):
            row = pl.ds(h, 1)
            left = []
            for part in range(2):
                left.append(jnp.where(med_on, rows_ref[0, part, t, row, :], 0.0))
                left.append(jnp.where(coarse_on, rows_ref[1, part, t, row, :], 0.0))
            r = mm(jnp.concatenate(left, axis=0).astype(BF16), ref[:, head_cols(h)])
            r = r[: n_med + n_coarse] + r[n_med + n_coarse :]
            med_ref[t, :, head_cols(h)] = r[:n_med].astype(BF16)
            coarse.append(r[n_med:])
        kept_ref[:, head_cols(h)] = jnp.where(first, coarse[0], coarse[1]).astype(BF16)
        sent_ref[:, head_cols(h)] = jnp.where(first, coarse[1], coarse[0]).astype(BF16)


def pool(position, keys, values, med_weight, coarse_weight):
    rows, width = keys.shape
    heads = width // HEAD_DIM
    half = jax.ShapeDtypeStruct((rows // COARSE, width), BF16)
    return pl.pallas_call(
        functools.partial(pool_kernel, heads),
        out_shape=(jax.ShapeDtypeStruct((2, rows // MED, width), BF16), half, half),
        in_specs=[SMEM, HBM, HBM, VMEM, VMEM],
        out_specs=(VMEM, VMEM, VMEM),
        scratch_shapes=[
            pltpu.VMEM((rows, width), BF16),
            pltpu.VMEM((rows, width), BF16),
            pltpu.VMEM((2, 2, 2, heads, rows), F32),
            pltpu.SemaphoreType.DMA((2, heads)),
        ],
        compiler_params=pltpu.CompilerParams(vmem_limit_bytes=12 << 20),
        cost_estimate=pl.CostEstimate(
            flops=4 * 136 * rows * 2 * width, bytes_accessed=3 << 20, transcendentals=0
        ),
        name="pool",
    )(
        position,
        in_hbm(keys),
        in_hbm(values),
        med_weight,
        coarse_weight,
    )


def attend_kernel(
    first_row, members, heads, per_coarse,
    pos_ref, head_ref, *refs,
):
    sources, w_hbm, outs = refs[:10], refs[10], refs[11 : 11 + members]
    refs = refs[11 + members :]
    targets, w_ref, att_ref, sems, w_sem = refs[:10], *refs[10:]
    q_ref, k_ref, v_ref, ek_ref, ev_ref, m2, m3, m4, mine, other = targets
    rows, width = att_ref.shape
    n_own = first_row + rows
    spans = [pl.ds(first_row, rows), pl.ds(0, n_own), pl.ds(0, n_own)] + [None] * 7
    groups = heads // 2
    copies = {}

    def start(g):
        cols = pl.ds(g * 2 * HEAD_DIM, 2 * HEAD_DIM)
        copies[g] = []
        for t, (src, dst, span) in enumerate(zip(sources, targets, spans)):
            if len(src.shape) == 3:
                src, dst = src.at[:, :, cols], dst.at[:, :, cols]
            elif span is None:
                src, dst = src.at[:, cols], dst.at[:, cols]
            else:
                src, dst = src.at[span, cols], dst.at[:, cols]
            copies[g].append(pltpu.make_async_copy(src, dst, sems.at[t, g]))
            copies[g][-1].start()

    start(0)
    start(1)
    pos = pos_ref[0]
    n_edge, n_med, n_coarse = ek_ref.shape[0], m2.shape[1], mine.shape[0]
    j = lax.broadcasted_iota(jnp.int32, (1, n_coarse), 1)
    pair = 2 * per_coarse
    group = j // (pair * 2 * CHIPS_X)
    step = jnp.where(group == 2, -1, jnp.where(group == 3, 2, group))
    slot = j // (2 * pair) % CHIPS_X
    half = j // pair % 2
    core = j // per_coarse % 2
    z = (pos // PLANE - step - 4 * half) & (PLANES - 1)
    x = (pos % PLANE // 2 - slot) & (CHIPS_X - 1)
    bias = [
        jnp.where(pos >= d, jnp.zeros((1, n), F32), jnp.full((1, n), NEG, F32))
        for d, n in ((1, n_edge), (2, n_med), (3, n_med), (4, n_med))
    ]
    bias.append(jnp.where(z * PLANE + x * 2 + core < pos, 0.0, NEG))
    bias = jnp.concatenate(bias, axis=1)
    first = pos % 2 == 0
    on_diag = lax.broadcasted_iota(jnp.int32, (rows, rows), 1) <= lax.broadcasted_iota(
        jnp.int32, (rows, rows), 0
    )
    w_copies = []
    for h in range(heads):
        if h % 2 == 0:
            g = h // 2
            for copy in copies[g]:
                copy.wait()
            if g + 2 < groups:
                start(g + 2)
            block = lax.rem(head_ref[0] + g, members)
            cols = pl.ds(pl.multiple_of(block * width, width), width)
            w_copies.append(pltpu.make_async_copy(w_hbm.at[:, cols], w_ref.at[g], w_sem.at[g]))
            w_copies[g].start()
        c = head_cols(h)
        a, b = mine[:, c], other[:, c]
        keys = [k_ref[:, c], ek_ref[:, c]] + [m[0, :, c] for m in (m2, m3, m4)]
        values = [v_ref[:, c], ev_ref[:, c]] + [m[1, :, c] for m in (m2, m3, m4)]
        keys = jnp.concatenate(keys + [jnp.where(first, a, b)], axis=0)
        values = jnp.concatenate(values + [jnp.where(first, b, a)], axis=0)
        s = mm_t(q_ref[:, c], keys)
        parts = [s[:, :first_row]] if first_row else []
        parts.append(jnp.where(on_diag, s[:, first_row:n_own], NEG))
        parts.append(s[:, n_own:] + bias)
        s = jnp.concatenate(parts, axis=1)
        peak = jnp.max(s, axis=1, keepdims=True)
        p = jnp.exp2((s - peak) * EXP2_SCALE).astype(BF16)
        got = mm(p, jnp.concatenate([values, jnp.ones_like(values)], axis=1))
        att_ref[:, c] = (got[:, :HEAD_DIM] / got[:, HEAD_DIM:]).astype(BF16)
    for k in range(members):
        w_copies[k].wait()
        outs[k][...] = mm(att_ref[...], w_ref[k]).astype(BF16)


def attend(position, head, queries, pairs, meds, coarse, weight, first_row, part):
    rows, width = queries.shape
    heads = width // HEAD_DIM
    members = weight.shape[1] // width
    operands = [queries, *pairs, *meds, *coarse]
    shapes = [x.shape for x in operands]
    shapes[:3] = [(part, width)] + [(first_row + part, width)] * 2
    n_keys = sum(shape[-2] for shape in shapes[1::2])
    return pl.pallas_call(
        functools.partial(attend_kernel, first_row, members, heads, rows // COARSE),
        out_shape=[jax.ShapeDtypeStruct((part, width), BF16)] * members,
        in_specs=[SMEM, SMEM] + [HBM] * 11,
        out_specs=[VMEM] * members,
        scratch_shapes=[pltpu.VMEM(shape, BF16) for shape in shapes]
        + [
            pltpu.VMEM((members, width, width), BF16),
            pltpu.VMEM((part, width), BF16),
            pltpu.SemaphoreType.DMA((10, heads // 2)),
            pltpu.SemaphoreType.DMA((members,)),
        ],
        compiler_params=pltpu.CompilerParams(vmem_limit_bytes=40 << 20),
        cost_estimate=pl.CostEstimate(
            flops=8 * part * n_keys * width + 2 * part * width * width * members,
            bytes_accessed=2 * width * width * members,
            transcendentals=0,
        ),
        name="attend",
    )(position, head, *[in_hbm(x) for x in operands[:3]], *operands[3:], in_hbm(weight))


def shifted(block, axis, distance):
    devices = range(lax.axis_size(axis))
    return lax.ppermute(
        block, axis, [(i - distance, i) for i in devices if i - distance in devices]
    )


def body(queries, keys, values, med_weight, coarse_weight, out_weight):
    n_seq = lax.axis_size("seq")
    members = lax.axis_size("head")
    position = lax.axis_index("seq")
    pos = position.astype(jnp.int32).reshape(1)
    head = lax.axis_index("head").astype(jnp.int32).reshape(1)
    core0 = (position & 1) == 0
    swap = [(i, i ^ 1) for i in range(n_seq)]

    def place(z, x, core):
        return z * PLANE + x * 2 + core

    def move(block, dz, dx):
        route = [
            (place(z, x, c), place((z + dz) % PLANES, (x + dx) % CHIPS_X, c))
            for z in range(PLANES)
            for x in range(CHIPS_X)
            for c in range(2)
        ]
        return lax.ppermute(block, "seq", route)

    edge_keys = shifted(keys, "seq", 1)

    med, kept, sent = pool(pos, keys, values, med_weight, coarse_weight)
    swapped = lax.ppermute(sent, "seq", swap)
    pair = jnp.where(
        core0, jnp.concatenate([kept, swapped], 0), jnp.concatenate([swapped, kept], 0)
    )
    quad = jnp.concatenate([pair, move(pair, 4, 0)], 0)
    ring = jnp.concatenate([quad] + [move(quad, 0, d) for d in range(1, CHIPS_X)], 0)

    edge_keys, values, ring, med = lax.optimization_barrier((edge_keys, values, ring, med))
    edge_values = shifted(values, "seq", 1)
    rings = [move(ring, d, 0) for d in (1, -1, 2)]
    turned = move(med, 0, -1)
    edge_values, turned, med = lax.optimization_barrier((edge_values, turned, med))
    med2 = shifted(med, "seq", 2)
    last = [
        (place(z, x, c), place(z + (x + 1) % CHIPS_X // 2, (x - 1) % CHIPS_X, c))
        for z in range(PLANES)
        for x in range(CHIPS_X)
        for c in range(2)
        if z + (x + 1) % CHIPS_X // 2 < PLANES
    ]
    med4 = lax.ppermute(turned, "seq", last)
    mine = jnp.concatenate([ring] + rings, 0)
    other = lax.ppermute(mine, "seq", swap)
    med3 = lax.ppermute(jnp.where(core0, med2, med4), "seq", swap)

    chunks = 2
    part = queries.shape[0] // chunks
    pieces = []
    for c in range(chunks):
        partial = attend(
            pos,
            head,
            queries,
            (keys, values, edge_keys, edge_values),
            (med2, med3, med4),
            (mine, other),
            out_weight,
            c * part,
            part,
        )
        total = partial[0].astype(F32)
        for k in (2, 1, 3):
            got = lax.ppermute(
                partial[k], "head", [(i, (i + k) % members) for i in range(members)]
            )
            total = total + got.astype(F32)
        pieces.append(total.astype(BF16))
    return jnp.concatenate(pieces, axis=0)


def solution(mesh):
    placed = (
        P("seq", "head"),
        P("seq", "head"),
        P("seq", "head"),
        P(None, "head", None),
        P(None, "head", None),
        P("head", None),
    )
    return jax.shard_map(
        body, mesh=mesh, in_specs=placed, out_specs=P("seq", "head"), check_vma=False
    )
```

time: 151 us -> 142 us (0.940)
  the two profiles are of different devices: /device:TPU:38 before, /device:TPU:96 now
where the time goes in v3:
time: 142 us; the launch traced here: 141 us
  waiting for transfers between devices  66.6 us (47%)
  starting transfers between devices  41.7 us (29%)
  Pallas kernels  27.4 us (19%)
  local copies, waits for them, and re-layouts  2.79 us (2%)
  other arithmetic  2.64 us (2%)
    ppermute x6, waiting for transfers between devices, body(): lax.ppermute(partial[k], 'head', [(i, (i + k) % members) for i in range(m...  27.9 us
    pallas_call x2, Pallas kernels, attend(): pl.pallas_call(functools.partial(attend_kernel, first_row, members, heads...  22.8 us
    ppermute x3, waiting for transfers between devices, shifted(): lax.ppermute(block, axis, [(i - distance, i) for i in devices if i - dist...  20.9 us
    ppermute x8, starting transfers between devices, move(): return lax.ppermute(block, 'seq', route)  16.9 us
    ppermute x8, waiting for transfers between devices, move(): return lax.ppermute(block, 'seq', route)  15 us
    ppermute x6, starting transfers between devices, body(): lax.ppermute(partial[k], 'head', [(i, (i + k) % members) for i in range(m...  9.93 us
    ppermute x1, starting transfers between devices, body(): med4 = lax.ppermute(turned, 'seq', last)  7.08 us
    ppermute x3, starting transfers between devices, shifted(): lax.ppermute(block, axis, [(i - distance, i) for i in devices if i - dist...  5.74 us
  transfers between devices with their start and end apart: 21, of which 14 were waited for; matrix products, arithmetic and copies ran while one was open for 1% of the time, Pallas kernels for 12%

profile of v3, /device:TPU:96, one launch (start us, length us, event | category | flops | bytes accessed | tf_op | source)
XLA Modules:
  0.0 141.2 jit_solution(12523291139418163526)
XLA Ops:
  0.0 1.9 %collective-permute-start = (bf16[512,1024]{1,0:T(8,128)(2,1)}, bf16[512,1024]{1,0:T(8,128)(2,1)S(1)}, u32[]{:S(2)}, u32[]{:S(2)}) collective-permute-start(bf16[512,1024]{1,0:T(8,128)(2,1)} %refs_1_.3), channel_id=1, source_target_pairs={{0,4},{4,8},{8,12},{12,16},{16,20},{20,24},{24,28},{28,32},{32,36}... | collective-permute-start | bytes 3145736 | tf_op jit(solution)/shard_map/ppermute | solution.py:244
  3.4 4.6 %pool.1 = (bf16[2,128,1024]{2,1,0:T(8,128)(2,1)}, bf16[8,1024]{1,0:T(8,128)(2,1)S(1)}, bf16[8,1024]{1,0:T(8,128)(2,1)S(1)}) custom-call(s32[1]{0:T(128)} %bitcast.pos_ref, bf16[512,1024]{1,0:T(8,128)(2,1)} %refs_1_.3, bf16[512,1024]{1,0:T(8,128)(2,1)} %refs_2_.1, f32[2,8,4]{2,1,0:T(8,128)S(1)} %copy.7.mw_ref, f32[2,8,64]{2,1,0:T(8,128)S(1)} %copy-done), custom_call_target="tpu_custom_call" | custom-call | flops 570425344 | bytes 3145728 | tf_op jit(solution)/shard_map/pool/pallas_call | solution.py:105
  8.0 1.7 %collective-permute-start.1 = (bf16[8,1024]{1,0:T(8,128)(2,1)S(1)}, bf16[8,1024]{1,0:T(8,128)(2,1)S(1)}, u32[]{:S(2)}, u32[]{:S(2)}) collective-permute-start(bf16[8,1024]{1,0:T(8,128)(2,1)S(1)} %get-tuple-element.24), channel_id=1, source_target_pairs={{0,4},{4,0},{8,12},{12,8},{16,20},{20,16},{24,28},{28,24},{32,36},... | collective-permute-start | bytes 49160 | tf_op jit(solution)/shard_map/ppermute | solution.py:273
  10.5 4.6 %collective-permute-start.2 = (bf16[16,1024]{1,0:T(8,128)(2,1)S(1)}, bf16[16,1024]{1,0:T(8,128)(2,1)S(1)}, u32[]{:S(2)}, u32[]{:S(2)}) collective-permute-start(bf16[16,1024]{1,0:T(8,128)(2,1)S(1)} %get-tuple-element.42), channel_id=1, source_target_pairs={{0,128},{4,132},{8,136},{12,140},{16,144},{20,148},{24,152},{28,15... | collective-permute-start | bytes 98312 | tf_op jit(solution)/shard_map/ppermute | solution.py:268
  15.1 3.3 %collective-permute-done.2 = bf16[16,1024]{1,0:T(8,128)(2,1)S(1)} collective-permute-done((bf16[16,1024]{1,0:T(8,128)(2,1)S(1)}, bf16[16,1024]{1,0:T(8,128)(2,1)S(1)}, u32[]{:S(2)}, u32[]{:S(2)}) %collective-permute-start.2) | collective-permute-done | bytes 32800 | tf_op jit(solution)/shard_map/ppermute | solution.py:268
  18.4 1.5 %collective-permute-start.3 = (bf16[32,1024]{1,0:T(8,128)(2,1)S(1)}, bf16[32,1024]{1,0:T(8,128)(2,1)S(1)}, u32[]{:S(2)}, u32[]{:S(2)}) collective-permute-start(bf16[32,1024]{1,0:T(8,128)(2,1)S(1)} %pad_maximum_fusion.1), channel_id=1, source_target_pairs={{0,8},{4,12},{8,16},{12,20},{16,24},{20,28},{24,0},{28,4},{32,40},... | collective-permute-start | bytes 196616 | tf_op jit(solution)/shard_map/ppermute | solution.py:268
  19.9 4.3 %collective-permute-start.4 = (bf16[32,1024]{1,0:T(8,128)(2,1)S(1)}, bf16[32,1024]{1,0:T(8,128)(2,1)S(1)}, u32[]{:S(2)}, u32[]{:S(2)}) collective-permute-start(bf16[32,1024]{1,0:T(8,128)(2,1)S(1)} %pad_maximum_fusion.1), channel_id=1, source_target_pairs={{0,16},{4,20},{8,24},{12,28},{16,0},{20,4},{24,8},{28,12},{32,48},... | collective-permute-start | bytes 196616 | tf_op jit(solution)/shard_map/ppermute | solution.py:268
  28.5 1.9 %collective-permute-start.6 = (bf16[512,1024]{1,0:T(8,128)(2,1)}, bf16[512,1024]{1,0:T(8,128)(2,1)S(1)}, u32[]{:S(2)}, u32[]{:S(2)}) collective-permute-start(bf16[512,1024]{1,0:T(8,128)(2,1)} %refs_2_.1), channel_id=1, source_target_pairs={{0,4},{4,8},{8,12},{12,16},{16,20},{20,24},{24,28},{28,32},{32,36}... | collective-permute-start | bytes 3145736 | tf_op jit(solution)/shard_map/ppermute | solution.py:244
  31.8 2.8 %collective-permute-start.11 = (bf16[128,1024]{1,0:T(8,128)(2,1)S(1)}, bf16[128,1024]{1,0:T(8,128)(2,1)S(1)}, u32[]{:S(2)}, u32[]{:S(2)}) collective-permute-start(bf16[128,1024]{1,0:T(8,128)(2,1)S(1)} %constant_dynamic-update-slice_fusion), channel_id=1, source_target_pairs={{0,32},{4,36},{8,40},{12,44},{16,48},{20,52},{24,56},{28,60},{32,6... | collective-permute-start | bytes 786440 | tf_op jit(solution)/shard_map/ppermute | solution.py:268
  34.6 2.4 %collective-permute-start.13 = (bf16[128,1024]{1,0:T(8,128)(2,1)S(1)}, bf16[128,1024]{1,0:T(8,128)(2,1)S(1)}, u32[]{:S(2)}, u32[]{:S(2)}) collective-permute-start(bf16[128,1024]{1,0:T(8,128)(2,1)S(1)} %constant_dynamic-update-slice_fusion), channel_id=1, source_target_pairs={{0,64},{4,68},{8,72},{12,76},{16,80},{20,84},{24,88},{28,92},{32,9... | collective-permute-start | bytes 786440 | tf_op jit(solution)/shard_map/ppermute | solution.py:268
  37.0 7.5 %collective-permute-done.7 = bf16[2,128,1024]{2,1,0:T(8,128)(2,1)S(1)} collective-permute-done((bf16[2,128,1024]{2,1,0:T(8,128)(2,1)}, bf16[2,128,1024]{2,1,0:T(8,128)(2,1)S(1)}, u32[]{:S(2)}, u32[]{:S(2)}) %collective-permute-start.7) | collective-permute-done | bytes 524320 | tf_op jit(solution)/shard_map/ppermute | solution.py:268
  44.4 10.9 %collective-permute-done.6.refs_4_ = bf16[512,1024]{1,0:T(8,128)(2,1)S(1)} collective-permute-done((bf16[512,1024]{1,0:T(8,128)(2,1)}, bf16[512,1024]{1,0:T(8,128)(2,1)S(1)}, u32[]{:S(2)}, u32[]{:S(2)}) %collective-permute-start.6) | collective-permute-done | bytes 1048608 | tf_op jit(solution)/shard_map/ppermute | solution.py:244
  55.3 1.9 %collective-permute-start.8 = (bf16[2,128,1024]{2,1,0:T(8,128)(2,1)}, bf16[2,128,1024]{2,1,0:T(8,128)(2,1)S(1)}, u32[]{:S(2)}, u32[]{:S(2)}) collective-permute-start(bf16[2,128,1024]{2,1,0:T(8,128)(2,1)} %get-tuple-element.30), channel_id=1, source_target_pairs={{0,8},{4,12},{8,16},{12,20},{16,24},{20,28},{24,32},{28,36},{32,40... | collective-permute-start | bytes 1572872 | tf_op jit(solution)/shard_map/ppermute | solution.py:244
  57.2 7.1 %collective-permute-start.9 = (bf16[2,128,1024]{2,1,0:T(8,128)(2,1)S(1)}, bf16[2,128,1024]{2,1,0:T(8,128)(2,1)S(1)}, u32[]{:S(2)}, u32[]{:S(2)}) collective-permute-start(bf16[2,128,1024]{2,1,0:T(8,128)(2,1)S(1)} %collective-permute-done.7), channel_id=1, source_target_pairs={{0,24},{4,28},{8,32},{12,36},{16,40},{20,44},{24,16},{28,20},{32,5... | collective-permute-start | bytes 1572872 | tf_op jit(solution)/shard_map/ppermute | solution.py:293
  64.5 10.0 %collective-permute-done.8.refs_5_ = bf16[2,128,1024]{2,1,0:T(8,128)(2,1)S(1)} collective-permute-done((bf16[2,128,1024]{2,1,0:T(8,128)(2,1)}, bf16[2,128,1024]{2,1,0:T(8,128)(2,1)S(1)}, u32[]{:S(2)}, u32[]{:S(2)}) %collective-permute-start.8) | collective-permute-done | bytes 524320 | tf_op jit(solution)/shard_map/ppermute | solution.py:244
  75.7 2.0 %collective-permute-done.10.refs_6_ = bf16[2,128,1024]{2,1,0:T(8,128)(2,1)} collective-permute-done((bf16[2,128,1024]{2,1,0:T(8,128)(2,1)}, bf16[2,128,1024]{2,1,0:T(8,128)(2,1)}, u32[]{:S(2)}, u32[]{:S(2)}) %collective-permute-start.10) | collective-permute-done | bytes 524320 | tf_op jit(solution)/shard_map/ppermute | solution.py:296
  78.9 11.1 %attend.2 = (bf16[256,1024]{1,0:T(8,128)(2,1)S(1)}, bf16[256,1024]{1,0:T(8,128)(2,1)S(1)}, bf16[256,1024]{1,0:T(8,128)(2,1)S(1)}, bf16[256,1024]{1,0:T(8,128)(2,1)S(1)}) custom-call(s32[1]{0:T(128)} %bitcast.pos_ref, s32[1]{0:T(128)} %bitcast.1.head_ref, bf16[512,1024]{1,0:T(8,128)(2,1)} %refs_0_.3, bf16[512,1024]{1,0:T(8,128)(2,1)} %refs_1_.3, ...), custom_call_target="tpu_custom_call" | custom-call | flops 5368709120 | bytes 8388608 | tf_op jit(solution)/shard_map/attend/pallas_call | solution.py:220
  90.0 3.3 %collective-permute-start.15 = (bf16[256,1024]{1,0:T(8,128)(2,1)S(1)}, bf16[256,1024]{1,0:T(8,128)(2,1)S(1)}, u32[]{:S(2)}, u32[]{:S(2)}) collective-permute-start(bf16[256,1024]{1,0:T(8,128)(2,1)S(1)} %get-tuple-element.34), channel_id=1, source_target_pairs={{0,2},{1,3},{2,0},{3,1},{4,6},{5,7},{6,4},{7,5},{8,10},{9,11},{10,... | collective-permute-start | bytes 1572872 | tf_op jit(solution)/shard_map/ppermute | solution.py:315
  93.9 2.6 %collective-permute-start.17 = (bf16[256,1024]{1,0:T(8,128)(2,1)S(1)}, bf16[256,1024]{1,0:T(8,128)(2,1)S(1)}, u32[]{:S(2)}, u32[]{:S(2)}) collective-permute-start(bf16[256,1024]{1,0:T(8,128)(2,1)S(1)} %get-tuple-element.36), channel_id=1, source_target_pairs={{0,3},{1,0},{2,1},{3,2},{4,7},{5,4},{6,5},{7,6},{8,11},{9,8},{10,9... | collective-permute-start | bytes 1572872 | tf_op jit(solution)/shard_map/ppermute | solution.py:315
  96.5 11.7 %attend.3 = (bf16[256,1024]{1,0:T(8,128)(2,1)S(1)}, bf16[256,1024]{1,0:T(8,128)(2,1)S(1)}, bf16[256,1024]{1,0:T(8,128)(2,1)S(1)}, bf16[256,1024]{1,0:T(8,128)(2,1)S(1)}) custom-call(s32[1]{0:T(128)} %bitcast.pos_ref, s32[1]{0:T(128)} %bitcast.1.head_ref, bf16[512,1024]{1,0:T(8,128)(2,1)} %refs_0_.3, bf16[512,1024]{1,0:T(8,128)(2,1)} %refs_1_.3, ...), custom_call_target="tpu_custom_call" | custom-call | flops 5905580032 | bytes 8388608 | tf_op jit(solution)/shard_map/attend/pallas_call | solution.py:220
  109.1 2.5 %collective-permute-start.20 = (bf16[256,1024]{1,0:T(8,128)(2,1)S(1)}, bf16[256,1024]{1,0:T(8,128)(2,1)S(1)}, u32[]{:S(2)}, u32[]{:S(2)}) collective-permute-start(bf16[256,1024]{1,0:T(8,128)(2,1)S(1)} %get-tuple-element.40), channel_id=1, source_target_pairs={{0,3},{1,0},{2,1},{3,2},{4,7},{5,4},{6,5},{7,6},{8,11},{9,8},{10,9... | collective-permute-start | bytes 1572872 | tf_op jit(solution)/shard_map/ppermute | solution.py:315
  111.6 6.1 %collective-permute-done.16 = bf16[256,1024]{1,0:T(8,128)(2,1)S(1)} collective-permute-done((bf16[256,1024]{1,0:T(8,128)(2,1)S(1)}, bf16[256,1024]{1,0:T(8,128)(2,1)S(1)}, u32[]{:S(2)}, u32[]{:S(2)}) %collective-permute-start.16) | collective-permute-done | bytes 524320 | tf_op jit(solution)/shard_map/ppermute | solution.py:315
  118.3 10.5 %collective-permute-done.18 = bf16[256,1024]{1,0:T(8,128)(2,1)S(1)} collective-permute-done((bf16[256,1024]{1,0:T(8,128)(2,1)S(1)}, bf16[256,1024]{1,0:T(8,128)(2,1)S(1)}, u32[]{:S(2)}, u32[]{:S(2)}) %collective-permute-start.18) | collective-permute-done | bytes 524320 | tf_op jit(solution)/shard_map/ppermute | solution.py:315
  128.9 10.5 %collective-permute-done.19 = bf16[256,1024]{1,0:T(8,128)(2,1)S(1)} collective-permute-done((bf16[256,1024]{1,0:T(8,128)(2,1)S(1)}, bf16[256,1024]{1,0:T(8,128)(2,1)S(1)}, u32[]{:S(2)}, u32[]{:S(2)}) %collective-permute-start.19) | collective-permute-done | bytes 524320 | tf_op jit(solution)/shard_map/ppermute | solution.py:315
  (42 shorter events, 14.6 us)
Async XLA Ops:
  0.0 28.5 %collective-permute-start = (bf16[512,1024]{1,0:T(8,128)(2,1)}, bf16[512,1024]{1,0:T(8,128)(2,1)S(1)}, u32[]{:S(2)}, u32[]{:S(2)}) collective-permute-start(bf16[512,1024]{1,0:T(8,128)(2,1)} %refs_1_.3), channel_id=1, source_target_pairs={{0,4},{4,8},{8,12},{12,16},{16,20},{20,24},{24,28},{28,32},{32,36}... | collective-permute-start | bytes 3145736 | tf_op jit(solution)/shard_map/ppermute | solution.py:244
  2.7 0.7 copy-start
  8.0 2.5 %collective-permute-start.1 = (bf16[8,1024]{1,0:T(8,128)(2,1)S(1)}, bf16[8,1024]{1,0:T(8,128)(2,1)S(1)}, u32[]{:S(2)}, u32[]{:S(2)}) collective-permute-start(bf16[8,1024]{1,0:T(8,128)(2,1)S(1)} %get-tuple-element.24), channel_id=1, source_target_pairs={{0,4},{4,0},{8,12},{12,8},{16,20},{20,16},{24,28},{28,24},{32,36},... | collective-permute-start | bytes 49160 | tf_op jit(solution)/shard_map/ppermute | solution.py:273
  10.5 7.9 %collective-permute-start.2 = (bf16[16,1024]{1,0:T(8,128)(2,1)S(1)}, bf16[16,1024]{1,0:T(8,128)(2,1)S(1)}, u32[]{:S(2)}, u32[]{:S(2)}) collective-permute-start(bf16[16,1024]{1,0:T(8,128)(2,1)S(1)} %get-tuple-element.42), channel_id=1, source_target_pairs={{0,128},{4,132},{8,136},{12,140},{16,144},{20,148},{24,152},{28,15... | collective-permute-start | bytes 98312 | tf_op jit(solution)/shard_map/ppermute | solution.py:268
  18.4 7.3 %collective-permute-start.3 = (bf16[32,1024]{1,0:T(8,128)(2,1)S(1)}, bf16[32,1024]{1,0:T(8,128)(2,1)S(1)}, u32[]{:S(2)}, u32[]{:S(2)}) collective-permute-start(bf16[32,1024]{1,0:T(8,128)(2,1)S(1)} %pad_maximum_fusion.1), channel_id=1, source_target_pairs={{0,8},{4,12},{8,16},{12,20},{16,24},{20,28},{24,0},{28,4},{32,40},... | collective-permute-start | bytes 196616 | tf_op jit(solution)/shard_map/ppermute | solution.py:268
  19.9 7.2 %collective-permute-start.4 = (bf16[32,1024]{1,0:T(8,128)(2,1)S(1)}, bf16[32,1024]{1,0:T(8,128)(2,1)S(1)}, u32[]{:S(2)}, u32[]{:S(2)}) collective-permute-start(bf16[32,1024]{1,0:T(8,128)(2,1)S(1)} %pad_maximum_fusion.1), channel_id=1, source_target_pairs={{0,16},{4,20},{8,24},{12,28},{16,0},{20,4},{24,8},{28,12},{32,48},... | collective-permute-start | bytes 196616 | tf_op jit(solution)/shard_map/ppermute | solution.py:268
  24.2 4.3 %collective-permute-start.5 = (bf16[32,1024]{1,0:T(8,128)(2,1)S(1)}, bf16[32,1024]{1,0:T(8,128)(2,1)S(1)}, u32[]{:S(2)}, u32[]{:S(2)}) collective-permute-start(bf16[32,1024]{1,0:T(8,128)(2,1)S(1)} %pad_maximum_fusion.1), channel_id=1, source_target_pairs={{0,24},{4,28},{8,0},{12,4},{16,8},{20,12},{24,16},{28,20},{32,56},... | collective-permute-start | bytes 196616 | tf_op jit(solution)/shard_map/ppermute | solution.py:268
  28.5 26.8 %collective-permute-start.6 = (bf16[512,1024]{1,0:T(8,128)(2,1)}, bf16[512,1024]{1,0:T(8,128)(2,1)S(1)}, u32[]{:S(2)}, u32[]{:S(2)}) collective-permute-start(bf16[512,1024]{1,0:T(8,128)(2,1)} %refs_2_.1), channel_id=1, source_target_pairs={{0,4},{4,8},{8,12},{12,16},{16,20},{20,24},{24,28},{28,32},{32,36}... | collective-permute-start | bytes 3145736 | tf_op jit(solution)/shard_map/ppermute | solution.py:244
  30.4 14.0 %collective-permute-start.7 = (bf16[2,128,1024]{2,1,0:T(8,128)(2,1)}, bf16[2,128,1024]{2,1,0:T(8,128)(2,1)S(1)}, u32[]{:S(2)}, u32[]{:S(2)}) collective-permute-start(bf16[2,128,1024]{2,1,0:T(8,128)(2,1)} %get-tuple-element.30), channel_id=1, source_target_pairs={{0,24},{4,28},{8,0},{12,4},{16,8},{20,12},{24,16},{28,20},{32,56},... | collective-permute-start | bytes 1572872 | tf_op jit(solution)/shard_map/ppermute | solution.py:268
  31.8 32.5 %collective-permute-start.11 = (bf16[128,1024]{1,0:T(8,128)(2,1)S(1)}, bf16[128,1024]{1,0:T(8,128)(2,1)S(1)}, u32[]{:S(2)}, u32[]{:S(2)}) collective-permute-start(bf16[128,1024]{1,0:T(8,128)(2,1)S(1)} %constant_dynamic-update-slice_fusion), channel_id=1, source_target_pairs={{0,32},{4,36},{8,40},{12,44},{16,48},{20,52},{24,56},{28,60},{32,6... | collective-permute-start | bytes 786440 | tf_op jit(solution)/shard_map/ppermute | solution.py:268
  34.6 29.7 %collective-permute-start.12 = (bf16[128,1024]{1,0:T(8,128)(2,1)S(1)}, bf16[128,1024]{1,0:T(8,128)(2,1)S(1)}, u32[]{:S(2)}, u32[]{:S(2)}) collective-permute-start(bf16[128,1024]{1,0:T(8,128)(2,1)S(1)} %constant_dynamic-update-slice_fusion), channel_id=1, source_target_pairs={{0,224},{4,228},{8,232},{12,236},{16,240},{20,244},{24,248},{28,25... | collective-permute-start | bytes 786440 | tf_op jit(solution)/shard_map/ppermute | solution.py:268
  34.6 29.8 %collective-permute-start.13 = (bf16[128,1024]{1,0:T(8,128)(2,1)S(1)}, bf16[128,1024]{1,0:T(8,128)(2,1)S(1)}, u32[]{:S(2)}, u32[]{:S(2)}) collective-permute-start(bf16[128,1024]{1,0:T(8,128)(2,1)S(1)} %constant_dynamic-update-slice_fusion), channel_id=1, source_target_pairs={{0,64},{4,68},{8,72},{12,76},{16,80},{20,84},{24,88},{28,92},{32,9... | collective-permute-start | bytes 786440 | tf_op jit(solution)/shard_map/ppermute | solution.py:268
  55.3 19.3 %copy-start.1 = (bf16[512,1024]{1,0:T(8,128)(2,1)}, bf16[512,1024]{1,0:T(8,128)(2,1)S(1)}, u32[]{:S(2)}) copy-start(bf16[512,1024]{1,0:T(8,128)(2,1)S(1)} %collective-permute-done.6.refs_4_) | copy-start | bytes 3145732
  55.3 19.3 %collective-permute-start.8 = (bf16[2,128,1024]{2,1,0:T(8,128)(2,1)}, bf16[2,128,1024]{2,1,0:T(8,128)(2,1)S(1)}, u32[]{:S(2)}, u32[]{:S(2)}) collective-permute-start(bf16[2,128,1024]{2,1,0:T(8,128)(2,1)} %get-tuple-element.30), channel_id=1, source_target_pairs={{0,8},{4,12},{8,16},{12,20},{16,24},{20,28},{24,32},{28,36},{32,40... | collective-permute-start | bytes 1572872 | tf_op jit(solution)/shard_map/ppermute | solution.py:244
  57.2 17.3 %collective-permute-start.9 = (bf16[2,128,1024]{2,1,0:T(8,128)(2,1)S(1)}, bf16[2,128,1024]{2,1,0:T(8,128)(2,1)S(1)}, u32[]{:S(2)}, u32[]{:S(2)}) collective-permute-start(bf16[2,128,1024]{2,1,0:T(8,128)(2,1)S(1)} %collective-permute-done.7), channel_id=1, source_target_pairs={{0,24},{4,28},{8,32},{12,36},{16,40},{20,44},{24,16},{28,20},{32,5... | collective-permute-start | bytes 1572872 | tf_op jit(solution)/shard_map/ppermute | solution.py:293
  64.4 11.3 %collective-permute-start.14 = (bf16[512,1024]{1,0:T(8,128)(2,1)S(1)}, bf16[512,1024]{1,0:T(8,128)(2,1)}, u32[]{:S(2)}, u32[]{:S(2)}) collective-permute-start(bf16[512,1024]{1,0:T(8,128)(2,1)S(1)} %constant_dynamic-update-slice_fusion.5.refs_8_), channel_id=1, source_target_pairs={{0,4},{4,0},{8,12},{12,8},{16,20},{20,16},{24,28},{28,24},{32,36},... | collective-permute-start | bytes 3145736 | tf_op jit(solution)/shard_map/ppermute | solution.py:295
  75.4 2.3 %collective-permute-start.10 = (bf16[2,128,1024]{2,1,0:T(8,128)(2,1)}, bf16[2,128,1024]{2,1,0:T(8,128)(2,1)}, u32[]{:S(2)}, u32[]{:S(2)}) collective-permute-start(bf16[2,128,1024]{2,1,0:T(8,128)(2,1)} %broadcast_select_fusion), channel_id=1, source_target_pairs={{0,4},{4,0},{8,12},{12,8},{16,20},{20,16},{24,28},{28,24},{32,36},... | collective-permute-start | bytes 1572872 | tf_op jit(solution)/shard_map/ppermute | solution.py:296
  77.6 1.2 copy-start.2
  90.0 19.1 %collective-permute-start.15 = (bf16[256,1024]{1,0:T(8,128)(2,1)S(1)}, bf16[256,1024]{1,0:T(8,128)(2,1)S(1)}, u32[]{:S(2)}, u32[]{:S(2)}) collective-permute-start(bf16[256,1024]{1,0:T(8,128)(2,1)S(1)} %get-tuple-element.34), channel_id=1, source_target_pairs={{0,2},{1,3},{2,0},{3,1},{4,6},{5,7},{6,4},{7,5},{8,10},{9,11},{10,... | collective-permute-start | bytes 1572872 | tf_op jit(solution)/shard_map/ppermute | solution.py:315
  93.3 24.4 %collective-permute-start.16 = (bf16[256,1024]{1,0:T(8,128)(2,1)S(1)}, bf16[256,1024]{1,0:T(8,128)(2,1)S(1)}, u32[]{:S(2)}, u32[]{:S(2)}) collective-permute-start(bf16[256,1024]{1,0:T(8,128)(2,1)S(1)} %get-tuple-element.35), channel_id=1, source_target_pairs={{0,1},{1,2},{2,3},{3,0},{4,5},{5,6},{6,7},{7,4},{8,9},{9,10},{10,1... | collective-permute-start | bytes 1572872 | tf_op jit(solution)/shard_map/ppermute | solution.py:315
  93.9 24.0 %collective-permute-start.17 = (bf16[256,1024]{1,0:T(8,128)(2,1)S(1)}, bf16[256,1024]{1,0:T(8,128)(2,1)S(1)}, u32[]{:S(2)}, u32[]{:S(2)}) collective-permute-start(bf16[256,1024]{1,0:T(8,128)(2,1)S(1)} %get-tuple-element.36), channel_id=1, source_target_pairs={{0,3},{1,0},{2,1},{3,2},{4,7},{5,4},{6,5},{7,6},{8,11},{9,8},{10,9... | collective-permute-start | bytes 1572872 | tf_op jit(solution)/shard_map/ppermute | solution.py:315
  108.2 20.7 %collective-permute-start.18 = (bf16[256,1024]{1,0:T(8,128)(2,1)S(1)}, bf16[256,1024]{1,0:T(8,128)(2,1)S(1)}, u32[]{:S(2)}, u32[]{:S(2)}) collective-permute-start(bf16[256,1024]{1,0:T(8,128)(2,1)S(1)} %get-tuple-element.38), channel_id=1, source_target_pairs={{0,2},{1,3},{2,0},{3,1},{4,6},{5,7},{6,4},{7,5},{8,10},{9,11},{10,... | collective-permute-start | bytes 1572872 | tf_op jit(solution)/shard_map/ppermute | solution.py:315
  108.3 31.1 %collective-permute-start.19 = (bf16[256,1024]{1,0:T(8,128)(2,1)S(1)}, bf16[256,1024]{1,0:T(8,128)(2,1)S(1)}, u32[]{:S(2)}, u32[]{:S(2)}) collective-permute-start(bf16[256,1024]{1,0:T(8,128)(2,1)S(1)} %get-tuple-element.39), channel_id=1, source_target_pairs={{0,1},{1,2},{2,3},{3,0},{4,5},{5,6},{6,7},{7,4},{8,9},{9,10},{10,1... | collective-permute-start | bytes 1572872 | tf_op jit(solution)/shard_map/ppermute | solution.py:315
  109.1 30.7 %collective-permute-start.20 = (bf16[256,1024]{1,0:T(8,128)(2,1)S(1)}, bf16[256,1024]{1,0:T(8,128)(2,1)S(1)}, u32[]{:S(2)}, u32[]{:S(2)}) collective-permute-start(bf16[256,1024]{1,0:T(8,128)(2,1)S(1)} %get-tuple-element.40), channel_id=1, source_target_pairs={{0,3},{1,0},{2,1},{3,2},{4,7},{5,4},{6,5},{7,6},{8,11},{9,8},{10,9... | collective-permute-start | bytes 1572872 | tf_op jit(solution)/shard_map/ppermute | solution.py:315

commit v4 on v3

--- a/solution.py
+++ b/solution.py
@@ -267,9 +267,12 @@
         ]
         return lax.ppermute(block, "seq", route)
 
+    width = keys.shape[1]
     edge_keys = shifted(keys, "seq", 1)
 
     med, kept, sent = pool(pos, keys, values, med_weight, coarse_weight)
+    med2 = shifted(med, "seq", 2)
+    turned = move(med, 0, -1)
     swapped = lax.ppermute(sent, "seq", swap)
     pair = jnp.where(
         core0, jnp.concatenate([kept, swapped], 0), jnp.concatenate([swapped, kept], 0)
@@ -277,12 +280,11 @@
     quad = jnp.concatenate([pair, move(pair, 4, 0)], 0)
     ring = jnp.concatenate([quad] + [move(quad, 0, d) for d in range(1, CHIPS_X)], 0)
 
-    edge_keys, values, ring, med = lax.optimization_barrier((edge_keys, values, ring, med))
+    edge_keys, values, ring, turned, med2 = lax.optimization_barrier(
+        (edge_keys, values, ring, turned, med2)
+    )
     edge_values = shifted(values, "seq", 1)
     rings = [move(ring, d, 0) for d in (1, -1, 2)]
-    turned = move(med, 0, -1)
-    edge_values, turned, med = lax.optimization_barrier((edge_values, turned, med))
-    med2 = shifted(med, "seq", 2)
     last = [
         (place(z, x, c), place(z + (x + 1) % CHIPS_X // 2, (x - 1) % CHIPS_X, c))
         for z in range(PLANES)
@@ -295,11 +297,16 @@
     other = lax.ppermute(mine, "seq", swap)
     med3 = lax.ppermute(jnp.where(core0, med2, med4), "seq", swap)
 
+    def send(block, distance):
+        return lax.ppermute(
+            block, "head", [(i, (i + distance) % members) for i in range(members)]
+        )
+
     chunks = 2
     part = queries.shape[0] // chunks
     pieces = []
     for c in range(chunks):
-        partial = attend(
+        own, ahead, across, behind = attend(
             pos,
             head,
             queries,
@@ -310,12 +317,23 @@
             c * part,
             part,
         )
-        total = partial[0].astype(F32)
-        for k in (2, 1, 3):
-            got = lax.ppermute(
-                partial[k], "head", [(i, (i + k) % members) for i in range(members)]
+        if c < chunks - 1:
+            own, pos = lax.optimization_barrier((own, pos))
+            got = [send(across, 2), send(ahead, 1), send(behind, -1)]
+        else:
+            middle = width // 2
+            left = send(across[:, :middle], 1)
+            right = send(across[:, middle:], -1)
+            ahead = jnp.concatenate(
+                [(ahead[:, :middle].astype(F32) + left.astype(F32)).astype(BF16), ahead[:, middle:]], 1
             )
-            total = total + got.astype(F32)
+            behind = jnp.concatenate(
+                [behind[:, :middle], (behind[:, middle:].astype(F32) + right.astype(F32)).astype(BF16)], 1
+            )
+            got = [send(ahead, 1), send(behind, -1)]
+        total = own.astype(F32)
+        for block in got:
+            total = total + block.astype(F32)
         pieces.append(total.astype(BF16))
     return jnp.concatenate(pieces, axis=0)
 

time: 142 us -> 147 us (1.035); the launches traced: 141 us -> 145 us
  starting transfers between devices: 41.7 us -> 47 us
    ppermute x3, waiting for transfers between devices: 20.9 us -> 0.01 us  [shifted(): lax.ppermute(block, axis, [(i - distance, i) for i in devices if i - dist...]
    ppermute x8, waiting for transfers between devices: 15 us -> 27.7 us  [move(): return lax.ppermute(block, 'seq', route)]
    ppermute x6 -> x7, starting transfers between devices: 9.93 us -> 20.7 us  [send(): lax.ppermute(block, 'head', [(i, (i + distance) % members) for i in range...]
    ppermute x1, waiting for transfers between devices: 0.01 us -> 9.33 us  [body(): med4 = lax.ppermute(turned, 'seq', last)]
    ppermute x1, starting transfers between devices: 7.08 us -> 3.15 us  [body(): med4 = lax.ppermute(turned, 'seq', last)]
    ppermute x8, starting transfers between devices: 16.9 us -> 15.2 us  [move(): return lax.ppermute(block, 'seq', route)]
    ppermute x6 -> x7, waiting for transfers between devices: 27.9 us -> 26.2 us  [send(): lax.ppermute(block, 'head', [(i, (i + distance) % members) for i in range...]
  transfers between devices with their start and end apart: 21 -> 22, of which waited for: 14 -> 11; matrix products, arithmetic and copies ran while one was open for 1% -> 2% of each run, Pallas kernels for 12% -> 3%
where the time goes in v4:
time: 147 us; the launch traced here: 145 us
  waiting for transfers between devices  66.3 us (45%)
  starting transfers between devices  47 us (32%)
  Pallas kernels  26.6 us (18%)
  other arithmetic  2.8 us (2%)
  local copies, waits for them, and re-layouts  1.63 us (1%)
    ppermute x8, waiting for transfers between devices, move(): return lax.ppermute(block, 'seq', route)  27.7 us
    ppermute x7, waiting for transfers between devices, send(): lax.ppermute(block, 'head', [(i, (i + distance) % members) for i in range...  26.2 us
    pallas_call x2, Pallas kernels, attend(): pl.pallas_call(functools.partial(attend_kernel, first_row, members, heads...  23 us
    ppermute x7, starting transfers between devices, send(): lax.ppermute(block, 'head', [(i, (i + distance) % members) for i in range...  20.7 us
    ppermute x8, starting transfers between devices, move(): return lax.ppermute(block, 'seq', route)  15.2 us
    ppermute x1, waiting for transfers between devices, body(): med4 = lax.ppermute(turned, 'seq', last)  9.33 us
    ppermute x3, starting transfers between devices, shifted(): lax.ppermute(block, axis, [(i - distance, i) for i in devices if i - dist...  6.25 us
    pallas_call x1, Pallas kernels, pool(): pl.pallas_call(functools.partial(pool_kernel, heads), out_shape=(jax.Shap...  3.67 us
  transfers between devices with their start and end apart: 22, of which 11 were waited for; matrix products, arithmetic and copies ran while one was open for 2% of the time, Pallas kernels for 3%

profile of v4, /device:TPU:96, one launch (start us, length us, event | category | flops | bytes accessed | tf_op | source)
XLA Modules:
  0.0 144.7 jit_solution(6850189195911004658)
XLA Ops:
  0.0 1.9 %collective-permute-start = (bf16[512,1024]{1,0:T(8,128)(2,1)}, bf16[512,1024]{1,0:T(8,128)(2,1)S(1)}, u32[]{:S(2)}, u32[]{:S(2)}) collective-permute-start(bf16[512,1024]{1,0:T(8,128)(2,1)} %refs_1_.3), channel_id=1, source_target_pairs={{0,4},{4,8},{8,12},{12,16},{16,20},{20,24},{24,28},{28,32},{32,36}... | collective-permute-start | bytes 3145736 | tf_op jit(solution)/shard_map/ppermute | solution.py:244
  3.4 3.7 %pool.1 = (bf16[2,128,1024]{2,1,0:T(8,128)(2,1)S(1)}, bf16[8,1024]{1,0:T(8,128)(2,1)S(1)}, bf16[8,1024]{1,0:T(8,128)(2,1)S(1)}) custom-call(s32[1]{0:T(128)} %bitcast.pos_ref, bf16[512,1024]{1,0:T(8,128)(2,1)} %refs_1_.3, bf16[512,1024]{1,0:T(8,128)(2,1)} %refs_2_.1, f32[2,8,4]{2,1,0:T(8,128)S(1)} %copy.7.mw_ref, f32[2,8,64]{2,1,0:T(8,128)S(1)} %copy-done), custom_call_target="tpu_custom_call" | custom-call | flops 570425344 | bytes 3145728 | tf_op jit(solution)/shard_map/pool/pallas_call | solution.py:105
  9.6 4.6 %collective-permute-start.2 = (bf16[16,1024]{1,0:T(8,128)(2,1)S(1)}, bf16[16,1024]{1,0:T(8,128)(2,1)S(1)}, u32[]{:S(2)}, u32[]{:S(2)}) collective-permute-start(bf16[16,1024]{1,0:T(8,128)(2,1)S(1)} %get-tuple-element.42), channel_id=1, source_target_pairs={{0,128},{4,132},{8,136},{12,140},{16,144},{20,148},{24,152},{28,15... | collective-permute-start | bytes 98312 | tf_op jit(solution)/shard_map/ppermute | solution.py:268
  15.7 2.4 %collective-permute-start.7 = (bf16[2,128,1024]{2,1,0:T(8,128)(2,1)S(1)}, bf16[2,128,1024]{2,1,0:T(8,128)(2,1)S(1)}, u32[]{:S(2)}, u32[]{:S(2)}) collective-permute-start(bf16[2,128,1024]{2,1,0:T(8,128)(2,1)S(1)} %get-tuple-element.25), channel_id=1, source_target_pairs={{0,8},{4,12},{8,16},{12,20},{16,24},{20,28},{24,32},{28,36},{32,40... | collective-permute-start | bytes 1572872 | tf_op jit(solution)/shard_map/ppermute | solution.py:244
  19.7 3.6 %collective-permute-start.4 = (bf16[32,1024]{1,0:T(8,128)(2,1)S(1)}, bf16[32,1024]{1,0:T(8,128)(2,1)S(1)}, u32[]{:S(2)}, u32[]{:S(2)}) collective-permute-start(bf16[32,1024]{1,0:T(8,128)(2,1)S(1)} %pad_maximum_fusion.3), channel_id=1, source_target_pairs={{0,16},{4,20},{8,24},{12,28},{16,0},{20,4},{24,8},{28,12},{32,48},... | collective-permute-start | bytes 196616 | tf_op jit(solution)/shard_map/ppermute | solution.py:268
  23.3 12.6 %collective-permute-done.3 = bf16[32,1024]{1,0:T(8,128)(2,1)S(1)} collective-permute-done((bf16[32,1024]{1,0:T(8,128)(2,1)S(1)}, bf16[32,1024]{1,0:T(8,128)(2,1)S(1)}, u32[]{:S(2)}, u32[]{:S(2)}) %collective-permute-start.3) | collective-permute-done | bytes 65568 | tf_op jit(solution)/shard_map/ppermute | solution.py:268
  36.0 4.2 %collective-permute-done.5 = bf16[32,1024]{1,0:T(8,128)(2,1)S(1)} collective-permute-done((bf16[32,1024]{1,0:T(8,128)(2,1)S(1)}, bf16[32,1024]{1,0:T(8,128)(2,1)S(1)}, u32[]{:S(2)}, u32[]{:S(2)}) %collective-permute-start.5) | collective-permute-done | bytes 65568 | tf_op jit(solution)/shard_map/ppermute | solution.py:268
  40.2 2.4 %collective-permute-start.11 = (bf16[128,1024]{1,0:T(8,128)(2,1)S(1)}, bf16[128,1024]{1,0:T(8,128)(2,1)S(1)}, u32[]{:S(2)}, u32[]{:S(2)}) collective-permute-start(bf16[128,1024]{1,0:T(8,128)(2,1)S(1)} %constant_dynamic-update-slice_fusion), channel_id=1, source_target_pairs={{0,32},{4,36},{8,40},{12,44},{16,48},{20,52},{24,56},{28,60},{32,6... | collective-permute-start | bytes 786440 | tf_op jit(solution)/shard_map/ppermute | solution.py:268
  44.2 3.2 %collective-permute-start.9 = (bf16[2,128,1024]{2,1,0:T(8,128)(2,1)S(1)}, bf16[2,128,1024]{2,1,0:T(8,128)(2,1)S(1)}, u32[]{:S(2)}, u32[]{:S(2)}) collective-permute-start(bf16[2,128,1024]{2,1,0:T(8,128)(2,1)S(1)} %collective-permute-done.6), channel_id=1, source_target_pairs={{0,24},{4,28},{8,32},{12,36},{16,40},{20,44},{24,16},{28,20},{32,5... | collective-permute-start | bytes 1572872 | tf_op jit(solution)/shard_map/ppermute | solution.py:295
  47.3 1.9 %collective-permute-start.8 = (bf16[512,1024]{1,0:T(8,128)(2,1)}, bf16[512,1024]{1,0:T(8,128)(2,1)}, u32[]{:S(2)}, u32[]{:S(2)}) collective-permute-start(bf16[512,1024]{1,0:T(8,128)(2,1)} %refs_2_.1), channel_id=1, source_target_pairs={{0,4},{4,8},{8,12},{12,16},{16,20},{20,24},{24,28},{28,32},{32,36}... | collective-permute-start | bytes 3145736 | tf_op jit(solution)/shard_map/ppermute | solution.py:244
  49.3 5.6 %collective-permute-done.11 = bf16[128,1024]{1,0:T(8,128)(2,1)S(1)} collective-permute-done((bf16[128,1024]{1,0:T(8,128)(2,1)S(1)}, bf16[128,1024]{1,0:T(8,128)(2,1)S(1)}, u32[]{:S(2)}, u32[]{:S(2)}) %collective-permute-start.11) | collective-permute-done | bytes 262176 | tf_op jit(solution)/shard_map/ppermute | solution.py:268
  54.9 5.3 %collective-permute-done.13 = bf16[128,1024]{1,0:T(8,128)(2,1)S(1)} collective-permute-done((bf16[128,1024]{1,0:T(8,128)(2,1)S(1)}, bf16[128,1024]{1,0:T(8,128)(2,1)S(1)}, u32[]{:S(2)}, u32[]{:S(2)}) %collective-permute-start.13) | collective-permute-done | bytes 262176 | tf_op jit(solution)/shard_map/ppermute | solution.py:268
  60.3 9.3 %collective-permute-done.9.refs_7_ = bf16[2,128,1024]{2,1,0:T(8,128)(2,1)S(1)} collective-permute-done((bf16[2,128,1024]{2,1,0:T(8,128)(2,1)S(1)}, bf16[2,128,1024]{2,1,0:T(8,128)(2,1)S(1)}, u32[]{:S(2)}, u32[]{:S(2)}) %collective-permute-start.9) | collective-permute-done | bytes 524320 | tf_op jit(solution)/shard_map/ppermute | solution.py:295
  70.5 2.2 %collective-permute-done.10.refs_6_ = bf16[2,128,1024]{2,1,0:T(8,128)(2,1)} collective-permute-done((bf16[2,128,1024]{2,1,0:T(8,128)(2,1)}, bf16[2,128,1024]{2,1,0:T(8,128)(2,1)}, u32[]{:S(2)}, u32[]{:S(2)}) %collective-permute-start.10) | collective-permute-done | bytes 524320 | tf_op jit(solution)/shard_map/ppermute | solution.py:298
  72.7 11.1 %attend.2 = (bf16[256,1024]{1,0:T(8,128)(2,1)S(1)}, bf16[256,1024]{1,0:T(8,128)(2,1)S(1)}, bf16[256,1024]{1,0:T(8,128)(2,1)S(1)}, bf16[256,1024]{1,0:T(8,128)(2,1)S(1)}) custom-call(s32[1]{0:T(128)} %bitcast.pos_ref, s32[1]{0:T(128)} %bitcast.1.head_ref, bf16[512,1024]{1,0:T(8,128)(2,1)} %refs_0_.3, bf16[512,1024]{1,0:T(8,128)(2,1)} %refs_1_.3, ...), custom_call_target="tpu_custom_call" | custom-call | flops 5368709120 | bytes 8388608 | tf_op jit(solution)/shard_map/attend/pallas_call | solution.py:220
  83.8 11.9 %attend.3 = (bf16[256,1024]{1,0:T(8,128)(2,1)S(1)}, bf16[256,1024]{1,0:T(8,128)(2,1)S(1)}, bf16[256,1024]{1,0:T(8,128)(2,1)S(1)}, bf16[256,1024]{1,0:T(8,128)(2,1)S(1)}) custom-call(s32[1]{0:T(128)} %bitcast.pos_ref, s32[1]{0:T(128)} %bitcast.1.head_ref, bf16[512,1024]{1,0:T(8,128)(2,1)} %refs_0_.3, bf16[512,1024]{1,0:T(8,128)(2,1)} %refs_1_.3, ...), custom_call_target="tpu_custom_call" | custom-call | flops 5905580032 | bytes 8388608 | tf_op jit(solution)/shard_map/attend/pallas_call | solution.py:220
  97.4 2.9 %collective-permute-start.15 = (bf16[256,1024]{1,0:T(8,128)(2,1)S(1)}, bf16[256,1024]{1,0:T(8,128)(2,1)S(1)}, u32[]{:S(2)}, u32[]{:S(2)}) collective-permute-start(bf16[256,1024]{1,0:T(8,128)(2,1)S(1)} %get-tuple-element.33), channel_id=1, source_target_pairs={{0,2},{1,3},{2,0},{3,1},{4,6},{5,7},{6,4},{7,5},{8,10},{9,11},{10,... | collective-permute-start | bytes 1572872 | tf_op jit(solution)/shard_map/ppermute | solution.py:301
  100.3 3.2 %collective-permute-start.17 = (bf16[256,1024]{1,0:T(8,128)(2,1)S(1)}, bf16[256,1024]{1,0:T(8,128)(2,1)S(1)}, u32[]{:S(2)}, u32[]{:S(2)}) collective-permute-start(bf16[256,1024]{1,0:T(8,128)(2,1)S(1)} %get-tuple-element.35), channel_id=1, source_target_pairs={{0,3},{1,0},{2,1},{3,2},{4,7},{5,4},{6,5},{7,6},{8,11},{9,8},{10,9... | collective-permute-start | bytes 1572872 | tf_op jit(solution)/shard_map/ppermute | solution.py:301
  103.8 2.8 %collective-permute-done.18 = bf16[256,512]{1,0:T(8,128)(2,1)S(1)} collective-permute-done((bf16[256,512]{1,0:T(8,128)(2,1)S(1)}, bf16[256,512]{1,0:T(8,128)(2,1)S(1)}, u32[]{:S(2)}, u32[]{:S(2)}) %collective-permute-start.18) | collective-permute-done | bytes 262176 | tf_op jit(solution)/shard_map/ppermute | solution.py:301
  106.7 10.0 %collective-permute-start.19 = (bf16[256,1024]{1,0:T(8,128)(2,1)S(1)}, bf16[256,1024]{1,0:T(8,128)(2,1)S(1)}, u32[]{:S(2)}, u32[]{:S(2)}) collective-permute-start(bf16[256,1024]{1,0:T(8,128)(2,1)S(1)} %pad_maximum_fusion.1), channel_id=1, source_target_pairs={{0,1},{1,2},{2,3},{3,0},{4,5},{5,6},{6,7},{7,4},{8,9},{9,10},{10,1... | collective-permute-start | bytes 1572872 | tf_op jit(solution)/shard_map/ppermute | solution.py:301
  116.7 11.9 %collective-permute-done.20 = bf16[256,512]{1,0:T(8,128)(2,1)S(1)} collective-permute-done((bf16[256,512]{1,0:T(8,128)(2,1)S(1)}, bf16[256,512]{1,0:T(8,128)(2,1)S(1)}, u32[]{:S(2)}, u32[]{:S(2)}) %collective-permute-start.20) | collective-permute-done | bytes 262176 | tf_op jit(solution)/shard_map/ppermute | solution.py:301
  128.8 2.7 %collective-permute-start.21 = (bf16[256,1024]{1,0:T(8,128)(2,1)S(1)}, bf16[256,1024]{1,0:T(8,128)(2,1)S(1)}, u32[]{:S(2)}, u32[]{:S(2)}) collective-permute-start(bf16[256,1024]{1,0:T(8,128)(2,1)S(1)} %pad_maximum_fusion.2), channel_id=1, source_target_pairs={{0,3},{1,0},{2,1},{3,2},{4,7},{5,4},{6,5},{7,6},{8,11},{9,8},{10,9... | collective-permute-start | bytes 1572872 | tf_op jit(solution)/shard_map/ppermute | solution.py:301
  131.8 7.3 %collective-permute-done.19 = bf16[256,1024]{1,0:T(8,128)(2,1)S(1)} collective-permute-done((bf16[256,1024]{1,0:T(8,128)(2,1)S(1)}, bf16[256,1024]{1,0:T(8,128)(2,1)S(1)}, u32[]{:S(2)}, u32[]{:S(2)}) %collective-permute-start.19) | collective-permute-done | bytes 524320 | tf_op jit(solution)/shard_map/ppermute | solution.py:301
  139.1 4.2 %collective-permute-done.21 = bf16[256,1024]{1,0:T(8,128)(2,1)S(1)} collective-permute-done((bf16[256,1024]{1,0:T(8,128)(2,1)S(1)}, bf16[256,1024]{1,0:T(8,128)(2,1)S(1)}, u32[]{:S(2)}, u32[]{:S(2)}) %collective-permute-start.21) | collective-permute-done | bytes 524320 | tf_op jit(solution)/shard_map/ppermute | solution.py:301
  (47 shorter events, 13.6 us)
Async XLA Ops:
  0.0 40.2 %collective-permute-start = (bf16[512,1024]{1,0:T(8,128)(2,1)}, bf16[512,1024]{1,0:T(8,128)(2,1)S(1)}, u32[]{:S(2)}, u32[]{:S(2)}) collective-permute-start(bf16[512,1024]{1,0:T(8,128)(2,1)} %refs_1_.3), channel_id=1, source_target_pairs={{0,4},{4,8},{8,12},{12,16},{16,20},{20,24},{24,28},{28,32},{32,36}... | collective-permute-start | bytes 3145736 | tf_op jit(solution)/shard_map/ppermute | solution.py:244
  2.7 0.7 copy-start
  7.1 2.5 %collective-permute-start.1 = (bf16[8,1024]{1,0:T(8,128)(2,1)S(1)}, bf16[8,1024]{1,0:T(8,128)(2,1)S(1)}, u32[]{:S(2)}, u32[]{:S(2)}) collective-permute-start(bf16[8,1024]{1,0:T(8,128)(2,1)S(1)} %get-tuple-element.24), channel_id=1, source_target_pairs={{0,4},{4,0},{8,12},{12,8},{16,20},{20,16},{24,28},{28,24},{32,36},... | collective-permute-start | bytes 49160 | tf_op jit(solution)/shard_map/ppermute | solution.py:276
  9.6 8.5 %collective-permute-start.2 = (bf16[16,1024]{1,0:T(8,128)(2,1)S(1)}, bf16[16,1024]{1,0:T(8,128)(2,1)S(1)}, u32[]{:S(2)}, u32[]{:S(2)}) collective-permute-start(bf16[16,1024]{1,0:T(8,128)(2,1)S(1)} %get-tuple-element.42), channel_id=1, source_target_pairs={{0,128},{4,132},{8,136},{12,140},{16,144},{20,148},{24,152},{28,15... | collective-permute-start | bytes 98312 | tf_op jit(solution)/shard_map/ppermute | solution.py:268
  14.2 26.0 %collective-permute-start.6 = (bf16[2,128,1024]{2,1,0:T(8,128)(2,1)S(1)}, bf16[2,128,1024]{2,1,0:T(8,128)(2,1)S(1)}, u32[]{:S(2)}, u32[]{:S(2)}) collective-permute-start(bf16[2,128,1024]{2,1,0:T(8,128)(2,1)S(1)} %get-tuple-element.25), channel_id=1, source_target_pairs={{0,24},{4,28},{8,0},{12,4},{16,8},{20,12},{24,16},{28,20},{32,56},... | collective-permute-start | bytes 1572872 | tf_op jit(solution)/shard_map/ppermute | solution.py:268
  15.7 24.5 %collective-permute-start.7 = (bf16[2,128,1024]{2,1,0:T(8,128)(2,1)S(1)}, bf16[2,128,1024]{2,1,0:T(8,128)(2,1)S(1)}, u32[]{:S(2)}, u32[]{:S(2)}) collective-permute-start(bf16[2,128,1024]{2,1,0:T(8,128)(2,1)S(1)} %get-tuple-element.25), channel_id=1, source_target_pairs={{0,8},{4,12},{8,16},{12,20},{16,24},{20,28},{24,32},{28,36},{32,40... | collective-permute-start | bytes 1572872 | tf_op jit(solution)/shard_map/ppermute | solution.py:244
  18.1 17.8 %collective-permute-start.3 = (bf16[32,1024]{1,0:T(8,128)(2,1)S(1)}, bf16[32,1024]{1,0:T(8,128)(2,1)S(1)}, u32[]{:S(2)}, u32[]{:S(2)}) collective-permute-start(bf16[32,1024]{1,0:T(8,128)(2,1)S(1)} %pad_maximum_fusion.3), channel_id=1, source_target_pairs={{0,8},{4,12},{8,16},{12,20},{16,24},{20,28},{24,0},{28,4},{32,40},... | collective-permute-start | bytes 196616 | tf_op jit(solution)/shard_map/ppermute | solution.py:268
  19.7 16.2 %collective-permute-start.4 = (bf16[32,1024]{1,0:T(8,128)(2,1)S(1)}, bf16[32,1024]{1,0:T(8,128)(2,1)S(1)}, u32[]{:S(2)}, u32[]{:S(2)}) collective-permute-start(bf16[32,1024]{1,0:T(8,128)(2,1)S(1)} %pad_maximum_fusion.3), channel_id=1, source_target_pairs={{0,16},{4,20},{8,24},{12,28},{16,0},{20,4},{24,8},{28,12},{32,48},... | collective-permute-start | bytes 196616 | tf_op jit(solution)/shard_map/ppermute | solution.py:268
  35.9 4.3 %collective-permute-start.5 = (bf16[32,1024]{1,0:T(8,128)(2,1)S(1)}, bf16[32,1024]{1,0:T(8,128)(2,1)S(1)}, u32[]{:S(2)}, u32[]{:S(2)}) collective-permute-start(bf16[32,1024]{1,0:T(8,128)(2,1)S(1)} %pad_maximum_fusion.3), channel_id=1, source_target_pairs={{0,24},{4,28},{8,0},{12,4},{16,8},{20,12},{24,16},{28,20},{32,56},... | collective-permute-start | bytes 196616 | tf_op jit(solution)/shard_map/ppermute | solution.py:268
  40.2 14.6 %collective-permute-start.11 = (bf16[128,1024]{1,0:T(8,128)(2,1)S(1)}, bf16[128,1024]{1,0:T(8,128)(2,1)S(1)}, u32[]{:S(2)}, u32[]{:S(2)}) collective-permute-start(bf16[128,1024]{1,0:T(8,128)(2,1)S(1)} %constant_dynamic-update-slice_fusion), channel_id=1, source_target_pairs={{0,32},{4,36},{8,40},{12,44},{16,48},{20,52},{24,56},{28,60},{32,6... | collective-permute-start | bytes 786440 | tf_op jit(solution)/shard_map/ppermute | solution.py:268
  42.6 12.3 %collective-permute-start.12 = (bf16[128,1024]{1,0:T(8,128)(2,1)S(1)}, bf16[128,1024]{1,0:T(8,128)(2,1)S(1)}, u32[]{:S(2)}, u32[]{:S(2)}) collective-permute-start(bf16[128,1024]{1,0:T(8,128)(2,1)S(1)} %constant_dynamic-update-slice_fusion), channel_id=1, source_target_pairs={{0,224},{4,228},{8,232},{12,236},{16,240},{20,244},{24,248},{28,25... | collective-permute-start | bytes 786440 | tf_op jit(solution)/shard_map/ppermute | solution.py:268
  42.6 17.5 %collective-permute-start.13 = (bf16[128,1024]{1,0:T(8,128)(2,1)S(1)}, bf16[128,1024]{1,0:T(8,128)(2,1)S(1)}, u32[]{:S(2)}, u32[]{:S(2)}) collective-permute-start(bf16[128,1024]{1,0:T(8,128)(2,1)S(1)} %constant_dynamic-update-slice_fusion), channel_id=1, source_target_pairs={{0,64},{4,68},{8,72},{12,76},{16,80},{20,84},{24,88},{28,92},{32,9... | collective-permute-start | bytes 786440 | tf_op jit(solution)/shard_map/ppermute | solution.py:268
  44.2 25.4 %collective-permute-start.9 = (bf16[2,128,1024]{2,1,0:T(8,128)(2,1)S(1)}, bf16[2,128,1024]{2,1,0:T(8,128)(2,1)S(1)}, u32[]{:S(2)}, u32[]{:S(2)}) collective-permute-start(bf16[2,128,1024]{2,1,0:T(8,128)(2,1)S(1)} %collective-permute-done.6), channel_id=1, source_target_pairs={{0,24},{4,28},{8,32},{12,36},{16,40},{20,44},{24,16},{28,20},{32,5... | collective-permute-start | bytes 1572872 | tf_op jit(solution)/shard_map/ppermute | solution.py:295
  47.3 25.4 %collective-permute-start.8 = (bf16[512,1024]{1,0:T(8,128)(2,1)}, bf16[512,1024]{1,0:T(8,128)(2,1)}, u32[]{:S(2)}, u32[]{:S(2)}) collective-permute-start(bf16[512,1024]{1,0:T(8,128)(2,1)} %refs_2_.1), channel_id=1, source_target_pairs={{0,4},{4,8},{8,12},{12,16},{16,20},{20,24},{24,28},{28,32},{32,36}... | collective-permute-start | bytes 3145736 | tf_op jit(solution)/shard_map/ppermute | solution.py:244
  60.2 12.5 %collective-permute-start.14 = (bf16[512,1024]{1,0:T(8,128)(2,1)S(1)}, bf16[512,1024]{1,0:T(8,128)(2,1)}, u32[]{:S(2)}, u32[]{:S(2)}) collective-permute-start(bf16[512,1024]{1,0:T(8,128)(2,1)S(1)} %constant_dynamic-update-slice_fusion.5.refs_8_), channel_id=1, source_target_pairs={{0,4},{4,0},{8,12},{12,8},{16,20},{20,16},{24,28},{28,24},{32,36},... | collective-permute-start | bytes 3145736 | tf_op jit(solution)/shard_map/ppermute | solution.py:297
  70.5 2.3 %collective-permute-start.10 = (bf16[2,128,1024]{2,1,0:T(8,128)(2,1)}, bf16[2,128,1024]{2,1,0:T(8,128)(2,1)}, u32[]{:S(2)}, u32[]{:S(2)}) collective-permute-start(bf16[2,128,1024]{2,1,0:T(8,128)(2,1)} %broadcast_select_fusion), channel_id=1, source_target_pairs={{0,4},{4,0},{8,12},{12,8},{16,20},{20,16},{24,28},{28,24},{32,36},... | collective-permute-start | bytes 1572872 | tf_op jit(solution)/shard_map/ppermute | solution.py:298
  95.7 10.8 %collective-permute-start.18 = (bf16[256,512]{1,0:T(8,128)(2,1)S(1)}, bf16[256,512]{1,0:T(8,128)(2,1)S(1)}, u32[]{:S(2)}, u32[]{:S(2)}) collective-permute-start(bf16[256,512]{1,0:T(8,128)(2,1)S(1)} %get-tuple-element.43), channel_id=1, source_target_pairs={{0,1},{1,2},{2,3},{3,0},{4,5},{5,6},{6,7},{7,4},{8,9},{9,10},{10,1... | collective-permute-start | bytes 786440 | tf_op jit(solution)/shard_map/ppermute | solution.py:301
  97.4 34.1 %collective-permute-start.15 = (bf16[256,1024]{1,0:T(8,128)(2,1)S(1)}, bf16[256,1024]{1,0:T(8,128)(2,1)S(1)}, u32[]{:S(2)}, u32[]{:S(2)}) collective-permute-start(bf16[256,1024]{1,0:T(8,128)(2,1)S(1)} %get-tuple-element.33), channel_id=1, source_target_pairs={{0,2},{1,3},{2,0},{3,1},{4,6},{5,7},{6,4},{7,5},{8,10},{9,11},{10,... | collective-permute-start | bytes 1572872 | tf_op jit(solution)/shard_map/ppermute | solution.py:301
  100.3 31.2 %collective-permute-start.16 = (bf16[256,1024]{1,0:T(8,128)(2,1)S(1)}, bf16[256,1024]{1,0:T(8,128)(2,1)S(1)}, u32[]{:S(2)}, u32[]{:S(2)}) collective-permute-start(bf16[256,1024]{1,0:T(8,128)(2,1)S(1)} %get-tuple-element.34), channel_id=1, source_target_pairs={{0,1},{1,2},{2,3},{3,0},{4,5},{5,6},{6,7},{7,4},{8,9},{9,10},{10,1... | collective-permute-start | bytes 1572872 | tf_op jit(solution)/shard_map/ppermute | solution.py:301
  100.3 31.2 %collective-permute-start.17 = (bf16[256,1024]{1,0:T(8,128)(2,1)S(1)}, bf16[256,1024]{1,0:T(8,128)(2,1)S(1)}, u32[]{:S(2)}, u32[]{:S(2)}) collective-permute-start(bf16[256,1024]{1,0:T(8,128)(2,1)S(1)} %get-tuple-element.35), channel_id=1, source_target_pairs={{0,3},{1,0},{2,1},{3,2},{4,7},{5,4},{6,5},{7,6},{8,11},{9,8},{10,9... | collective-permute-start | bytes 1572872 | tf_op jit(solution)/shard_map/ppermute | solution.py:301
  103.6 25.1 %collective-permute-start.20 = (bf16[256,512]{1,0:T(8,128)(2,1)S(1)}, bf16[256,512]{1,0:T(8,128)(2,1)S(1)}, u32[]{:S(2)}, u32[]{:S(2)}) collective-permute-start(bf16[256,512]{1,0:T(8,128)(2,1)S(1)} %get-tuple-element.44), channel_id=1, source_target_pairs={{0,3},{1,0},{2,1},{3,2},{4,7},{5,4},{6,5},{7,6},{8,11},{9,8},{10,9... | collective-permute-start | bytes 786440 | tf_op jit(solution)/shard_map/ppermute | solution.py:301
  106.7 32.4 %collective-permute-start.19 = (bf16[256,1024]{1,0:T(8,128)(2,1)S(1)}, bf16[256,1024]{1,0:T(8,128)(2,1)S(1)}, u32[]{:S(2)}, u32[]{:S(2)}) collective-permute-start(bf16[256,1024]{1,0:T(8,128)(2,1)S(1)} %pad_maximum_fusion.1), channel_id=1, source_target_pairs={{0,1},{1,2},{2,3},{3,0},{4,5},{5,6},{6,7},{7,4},{8,9},{9,10},{10,1... | collective-permute-start | bytes 1572872 | tf_op jit(solution)/shard_map/ppermute | solution.py:301
  128.8 14.6 %collective-permute-start.21 = (bf16[256,1024]{1,0:T(8,128)(2,1)S(1)}, bf16[256,1024]{1,0:T(8,128)(2,1)S(1)}, u32[]{:S(2)}, u32[]{:S(2)}) collective-permute-start(bf16[256,1024]{1,0:T(8,128)(2,1)S(1)} %pad_maximum_fusion.2), channel_id=1, source_target_pairs={{0,3},{1,0},{2,1},{3,2},{4,7},{5,4},{6,5},{7,6},{8,11},{9,8},{10,9... | collective-permute-start | bytes 1572872 | tf_op jit(solution)/shard_map/ppermute | solution.py:301

commit v5 on v3

--- a/solution.py
+++ b/solution.py
@@ -15,6 +15,7 @@
 CHIPS_X = 4
 PLANE = 2 * CHIPS_X
 PLANES = 8
+FIRST_ROWS = 192
 NEG = -1e30
 EXP2_SCALE = math.log2(math.e) / math.sqrt(HEAD_DIM)
 F32 = jnp.float32
@@ -57,14 +58,21 @@
 
 
 def pool_kernel(
-    heads, pos_ref, k_hbm, v_hbm, mw_ref, cw_ref, med_ref, kept_ref, sent_ref, k_ref, v_ref, rows_ref, sems
+    heads,
+    pos_ref, k_hbm, v_hbm, mw_ref, cw_hbm,
+    med_ref, kept_ref, sent_ref,
+    k_ref, v_ref, cw_ref, rows_ref, sems, w_sem,
 ):
+    w_copy = pltpu.make_async_copy(cw_hbm, cw_ref, w_sem.at[0])
+    w_copy.start()
     copies = fetch_heads(((k_hbm, k_ref), (v_hbm, v_ref)), sems, heads)
     rows = k_ref.shape[0]
     n_med, n_coarse = rows // MED, rows // COARSE
     lane = lax.broadcasted_iota(jnp.int32, (heads, rows), 1)
     for slot, (ref, ratio) in enumerate(((mw_ref, MED), (cw_ref, COARSE))):
         at = lane % ratio
+        if slot:
+            w_copy.wait()
         for t in range(2):
             w = ref[t]
             spread = jnp.zeros((heads, rows), F32)
@@ -105,13 +113,15 @@
     return pl.pallas_call(
         functools.partial(pool_kernel, heads),
         out_shape=(jax.ShapeDtypeStruct((2, rows // MED, width), BF16), half, half),
-        in_specs=[SMEM, HBM, HBM, VMEM, VMEM],
+        in_specs=[SMEM, HBM, HBM, VMEM, HBM],
         out_specs=(VMEM, VMEM, VMEM),
         scratch_shapes=[
             pltpu.VMEM((rows, width), BF16),
             pltpu.VMEM((rows, width), BF16),
+            pltpu.VMEM(coarse_weight.shape, F32),
             pltpu.VMEM((2, 2, 2, heads, rows), F32),
             pltpu.SemaphoreType.DMA((2, heads)),
+            pltpu.SemaphoreType.DMA((1,)),
         ],
         compiler_params=pltpu.CompilerParams(vmem_limit_bytes=12 << 20),
         cost_estimate=pl.CostEstimate(
@@ -123,7 +133,7 @@
         in_hbm(keys),
         in_hbm(values),
         med_weight,
-        coarse_weight,
+        in_hbm(coarse_weight),
     )
 
 
@@ -132,48 +142,68 @@
     pos_ref, head_ref, *refs,
 ):
     sources, w_hbm, outs = refs[:10], refs[10], refs[11 : 11 + members]
-    refs = refs[11 + members :]
-    targets, w_ref, att_ref, sems, w_sem = refs[:10], *refs[10:]
-    q_ref, k_ref, v_ref, ek_ref, ev_ref, m2, m3, m4, mine, other = targets
+    q_ref, k_ref, v_ref, w_ref, att_ref, sems, w_sem = refs[11 + members :]
+    q, k, v, ek, ev, m2, m3, m4, mine, other = sources
     rows, width = att_ref.shape
     n_own = first_row + rows
-    spans = [pl.ds(first_row, rows), pl.ds(0, n_own), pl.ds(0, n_own)] + [None] * 7
+    n_edge, n_med, n_coarse = ek.shape[0], m2.shape[1], mine.shape[0]
+    first = pos_ref[0] % 2 == 0
+    n = n_own + n_edge
+    moves = [(q, q_ref, first_row, 0, rows)]
+    moves += [(k, k_ref, 0, 0, n_own), (v, v_ref, 0, 0, n_own)]
+    moves += [(ek, k_ref, 0, n_own, n_edge), (ev, v_ref, 0, n_own, n_edge)]
+    for m in (m2, m3, m4):
+        moves += [(m.at[0], k_ref, 0, n, n_med), (m.at[1], v_ref, 0, n, n_med)]
+        n += n_med
     groups = heads // 2
-    copies = {}
+
+    def copy(g, t, src, dst, at, to, size):
+        cols = pl.ds(g * 2 * HEAD_DIM, 2 * HEAD_DIM)
+        return pltpu.make_async_copy(
+            src.at[pl.ds(at, size), cols], dst.at[pl.ds(to, size), cols], sems.at[t, g]
+        )
+
+    def summaries(g, kv):
+        return [copy(g, len(moves) + i, src, dst, 0, n, n_coarse) for i, (src, dst) in enumerate(kv)]
 
     def start(g):
-        cols = pl.ds(g * 2 * HEAD_DIM, 2 * HEAD_DIM)
-        copies[g] = []
-        for t, (src, dst, span) in enumerate(zip(sources, targets, spans)):
-            if len(src.shape) == 3:
-                src, dst = src.at[:, :, cols], dst.at[:, :, cols]
-            elif span is None:
-                src, dst = src.at[:, cols], dst.at[:, cols]
-            else:
-                src, dst = src.at[span, cols], dst.at[:, cols]
-            copies[g].append(pltpu.make_async_copy(src, dst, sems.at[t, g]))
-            copies[g][-1].start()
+        for t, args in enumerate(moves):
+            copy(g, t, *args).start()
+
+        @pl.when(first)
+        def _():
+            for c in summaries(g, ((mine, k_ref), (other, v_ref))):
+                c.start()
+
+        @pl.when(jnp.logical_not(first))
+        def _():
+            for c in summaries(g, ((other, k_ref), (mine, v_ref))):
+                c.start()
+
+    def finish(g):
+        for t, args in enumerate(moves):
+            copy(g, t, *args).wait()
+        for c in summaries(g, ((mine, k_ref), (other, v_ref))):
+            c.wait()
 
     start(0)
     start(1)
     pos = pos_ref[0]
-    n_edge, n_med, n_coarse = ek_ref.shape[0], m2.shape[1], mine.shape[0]
     j = lax.broadcasted_iota(jnp.int32, (1, n_coarse), 1)
     pair = 2 * per_coarse
     group = j // (pair * 2 * CHIPS_X)
-    step = jnp.where(group == 2, -1, jnp.where(group == 3, 2, group))
+    step = jnp.where(group == 3, 1, jnp.where(group > 0, group - 3, 0))
     slot = j // (2 * pair) % CHIPS_X
     half = j // pair % 2
     core = j // per_coarse % 2
     z = (pos // PLANE - step - 4 * half) & (PLANES - 1)
-    x = (pos % PLANE // 2 - slot) & (CHIPS_X - 1)
+    x = (pos % PLANE // 2 + slot) & (CHIPS_X - 1)
     bias = [
-        jnp.where(pos >= d, jnp.zeros((1, n), F32), jnp.full((1, n), NEG, F32))
-        for d, n in ((1, n_edge), (2, n_med), (3, n_med), (4, n_med))
+        jnp.where(pos >= d, jnp.zeros((1, size), F32), jnp.full((1, size), NEG, F32))
+        for d, size in ((1, n_edge), (2, n_med), (3, n_med), (4, n_med))
     ]
     bias.append(jnp.where(z * PLANE + x * 2 + core < pos, 0.0, NEG))
     bias = jnp.concatenate(bias, axis=1)
-    first = pos % 2 == 0
     on_diag = lax.broadcasted_iota(jnp.int32, (rows, rows), 1) <= lax.broadcasted_iota(
         jnp.int32, (rows, rows), 0
     )
@@ -181,8 +211,7 @@
     for h in range(heads):
         if h % 2 == 0:
             g = h // 2
-            for copy in copies[g]:
-                copy.wait()
+            finish(g)
             if g + 2 < groups:
                 start(g + 2)
             block = lax.rem(head_ref[0] + g, members)
@@ -190,18 +219,14 @@
             w_copies.append(pltpu.make_async_copy(w_hbm.at[:, cols], w_ref.at[g], w_sem.at[g]))
             w_copies[g].start()
         c = head_cols(h)
-        a, b = mine[:, c], other[:, c]
-        keys = [k_ref[:, c], ek_ref[:, c]] + [m[0, :, c] for m in (m2, m3, m4)]
-        values = [v_ref[:, c], ev_ref[:, c]] + [m[1, :, c] for m in (m2, m3, m4)]
-        keys = jnp.concatenate(keys + [jnp.where(first, a, b)], axis=0)
-        values = jnp.concatenate(values + [jnp.where(first, b, a)], axis=0)
-        s = mm_t(q_ref[:, c], keys)
+        s = mm_t(q_ref[:, c], k_ref[:, c])
         parts = [s[:, :first_row]] if first_row else []
         parts.append(jnp.where(on_diag, s[:, first_row:n_own], NEG))
         parts.append(s[:, n_own:] + bias)
         s = jnp.concatenate(parts, axis=1)
         peak = jnp.max(s, axis=1, keepdims=True)
         p = jnp.exp2((s - peak) * EXP2_SCALE).astype(BF16)
+        values = v_ref[:, c]
         got = mm(p, jnp.concatenate([values, jnp.ones_like(values)], axis=1))
         att_ref[:, c] = (got[:, :HEAD_DIM] / got[:, HEAD_DIM:]).astype(BF16)
     for k in range(members):
@@ -214,25 +239,25 @@
     heads = width // HEAD_DIM
     members = weight.shape[1] // width
     operands = [queries, *pairs, *meds, *coarse]
-    shapes = [x.shape for x in operands]
-    shapes[:3] = [(part, width)] + [(first_row + part, width)] * 2
-    n_keys = sum(shape[-2] for shape in shapes[1::2])
+    n_keys = first_row + part + pairs[2].shape[0] + 3 * meds[0].shape[1] + coarse[0].shape[0]
     return pl.pallas_call(
         functools.partial(attend_kernel, first_row, members, heads, rows // COARSE),
         out_shape=[jax.ShapeDtypeStruct((part, width), BF16)] * members,
         in_specs=[SMEM, SMEM] + [HBM] * 11,
         out_specs=[VMEM] * members,
-        scratch_shapes=[pltpu.VMEM(shape, BF16) for shape in shapes]
-        + [
+        scratch_shapes=[
+            pltpu.VMEM((part, width), BF16),
+            pltpu.VMEM((n_keys, width), BF16),
+            pltpu.VMEM((n_keys, width), BF16),
             pltpu.VMEM((members, width, width), BF16),
             pltpu.VMEM((part, width), BF16),
-            pltpu.SemaphoreType.DMA((10, heads // 2)),
+            pltpu.SemaphoreType.DMA((13, heads // 2)),
             pltpu.SemaphoreType.DMA((members,)),
         ],
         compiler_params=pltpu.CompilerParams(vmem_limit_bytes=40 << 20),
         cost_estimate=pl.CostEstimate(
-            flops=8 * part * n_keys * width + 2 * part * width * width * members,
-            bytes_accessed=2 * width * width * members,
+            flops=part * n_keys * width,
+            bytes_accessed=2 * width * width,
             transcendentals=0,
         ),
         name="attend",
@@ -267,57 +292,64 @@
         ]
         return lax.ppermute(block, "seq", route)
 
+    width = keys.shape[1]
     edge_keys = shifted(keys, "seq", 1)
 
     med, kept, sent = pool(pos, keys, values, med_weight, coarse_weight)
+    med2 = shifted(med, "seq", 2)
+    med4 = shifted(med, "seq", 4)
     swapped = lax.ppermute(sent, "seq", swap)
     pair = jnp.where(
         core0, jnp.concatenate([kept, swapped], 0), jnp.concatenate([swapped, kept], 0)
     )
-    quad = jnp.concatenate([pair, move(pair, 4, 0)], 0)
-    ring = jnp.concatenate([quad] + [move(quad, 0, d) for d in range(1, CHIPS_X)], 0)
-
-    edge_keys, values, ring, med = lax.optimization_barrier((edge_keys, values, ring, med))
+    quads = [jnp.concatenate([pair, move(pair, 4, 0)], 0)]
+    for _ in range(1, CHIPS_X):
+        quads.append(move(quads[-1], 0, -1))
+    ring = jnp.concatenate(quads, 0)
+
+    edge_keys, values, ring, med2, med4 = lax.optimization_barrier(
+        (edge_keys, values, ring, med2, med4)
+    )
     edge_values = shifted(values, "seq", 1)
-    rings = [move(ring, d, 0) for d in (1, -1, 2)]
-    turned = move(med, 0, -1)
-    edge_values, turned, med = lax.optimization_barrier((edge_values, turned, med))
-    med2 = shifted(med, "seq", 2)
-    last = [
-        (place(z, x, c), place(z + (x + 1) % CHIPS_X // 2, (x - 1) % CHIPS_X, c))
-        for z in range(PLANES)
-        for x in range(CHIPS_X)
-        for c in range(2)
-        if z + (x + 1) % CHIPS_X // 2 < PLANES
-    ]
-    med4 = lax.ppermute(turned, "seq", last)
+    rings = [move(ring, d, 0) for d in (-2, -1, 1)]
     mine = jnp.concatenate([ring] + rings, 0)
     other = lax.ppermute(mine, "seq", swap)
     med3 = lax.ppermute(jnp.where(core0, med2, med4), "seq", swap)
 
-    chunks = 2
-    part = queries.shape[0] // chunks
-    pieces = []
-    for c in range(chunks):
-        partial = attend(
-            pos,
+    def send(block, distance):
+        return lax.ppermute(
+            block, "head", [(i, (i + distance) % members) for i in range(members)]
+        )
+
+    def attend_rows(position, first_row, rows):
+        return attend(
+            position,
             head,
             queries,
             (keys, values, edge_keys, edge_values),
             (med2, med3, med4),
             (mine, other),
             out_weight,
-            c * part,
-            part,
+            first_row,
+            rows,
         )
-        total = partial[0].astype(F32)
-        for k in (2, 1, 3):
-            got = lax.ppermute(
-                partial[k], "head", [(i, (i + k) % members) for i in range(members)]
-            )
-            total = total + got.astype(F32)
-        pieces.append(total.astype(BF16))
-    return jnp.concatenate(pieces, axis=0)
+
+    def total(blocks):
+        return functools.reduce(jnp.add, [b.astype(F32) for b in blocks]).astype(BF16)
+
+    split = FIRST_ROWS
+    own, ahead, across, behind = attend_rows(pos, 0, split)
+    own, pos = lax.optimization_barrier((own, pos))
+    first = total([own, send(across, 2), send(ahead, 1), send(behind, -1)])
+    own, ahead, across, behind = attend_rows(pos, split, queries.shape[0] - split)
+    first, across = lax.optimization_barrier((first, across))
+    middle = width // 2
+    left = send(across[:, :middle], 1)
+    right = send(across[:, middle:], -1)
+    ahead = jnp.concatenate([total([ahead[:, :middle], left]), ahead[:, middle:]], 1)
+    behind = jnp.concatenate([behind[:, :middle], total([behind[:, middle:], right])], 1)
+    second = total([own, send(ahead, 1), send(behind, -1)])
+    return jnp.concatenate([first, second], axis=0)
 
 
 def solution(mesh):

time: 142 us -> 141 us (level)
  the two profiles are of different devices: /device:TPU:96 before, /device:TPU:2 now
where the time goes in v5:
time: 141 us
  waiting for transfers between devices  57.2 us (41%)
  starting transfers between devices  50.9 us (36%)
  Pallas kernels  28.5 us (20%)
  other arithmetic  2.85 us (2%)
    ppermute x7, waiting for transfers between devices, move(): return lax.ppermute(block, 'seq', route)  28.6 us
    ppermute x7, starting transfers between devices, move(): return lax.ppermute(block, 'seq', route)  27.4 us
    ppermute x7, waiting for transfers between devices, send(): lax.ppermute(block, 'head', [(i, (i + distance) % members) for i in range...  25.3 us
    pallas_call x2, Pallas kernels, attend(): pl.pallas_call(functools.partial(attend_kernel, first_row, members, heads...  24.1 us
    ppermute x4, starting transfers between devices, shifted(): lax.ppermute(block, axis, [(i - distance, i) for i in devices if i - dist...  10.7 us
    ppermute x7, starting transfers between devices, send(): lax.ppermute(block, 'head', [(i, (i + distance) % members) for i in range...  10.5 us
    pallas_call x1, Pallas kernels, pool(): pl.pallas_call(functools.partial(pool_kernel, heads), out_shape=(jax.Shap...  4.48 us
  transfers between devices with their start and end apart: 21, of which 12 were waited for; matrix products, arithmetic and copies ran while one was open for 2% of the time, Pallas kernels for 13%

profile of v5, /device:TPU:2, one launch (start us, length us, event | category | flops | bytes accessed | tf_op | source)
XLA Modules:
  0.0 140.6 jit_solution(17979034415999281801)
XLA Ops:
  0.0 1.9 %collective-permute-start = (bf16[512,1024]{1,0:T(8,128)(2,1)}, bf16[512,1024]{1,0:T(8,128)(2,1)S(1)}, u32[]{:S(2)}, u32[]{:S(2)}) collective-permute-start(bf16[512,1024]{1,0:T(8,128)(2,1)} %refs_1_.3), channel_id=1, source_target_pairs={{0,4},{4,8},{8,12},{12,16},{16,20},{20,24},{24,28},{28,32},{32,36}... | collective-permute-start | bytes 3145736 | tf_op jit(solution)/shard_map/ppermute | solution.py:269
  2.7 4.5 %pool.1 = (bf16[2,128,1024]{2,1,0:T(8,128)(2,1)S(1)}, bf16[8,1024]{1,0:T(8,128)(2,1)S(1)}, bf16[8,1024]{1,0:T(8,128)(2,1)S(1)}) custom-call(s32[1]{0:T(128)} %bitcast.pos_ref, bf16[512,1024]{1,0:T(8,128)(2,1)} %refs_1_.3, bf16[512,1024]{1,0:T(8,128)(2,1)} %refs_2_.1, f32[2,8,4]{2,1,0:T(8,128)S(1)} %copy.7.mw_ref, f32[2,8,64]{2,1,0:T(8,128)} %cw_hbm.1), custom_call_target="tpu_custom_call" | custom-call | flops 570425344 | bytes 3145728 | tf_op jit(solution)/shard_map/pool/pallas_call | solution.py:113
  9.7 7.3 %collective-permute-start.2 = (bf16[16,1024]{1,0:T(8,128)(2,1)S(1)}, bf16[16,1024]{1,0:T(8,128)(2,1)S(1)}, u32[]{:S(2)}, u32[]{:S(2)}) collective-permute-start(bf16[16,1024]{1,0:T(8,128)(2,1)S(1)} %get-tuple-element.46), channel_id=1, source_target_pairs={{0,128},{4,132},{8,136},{12,140},{16,144},{20,148},{24,152},{28,15... | collective-permute-start | bytes 98312 | tf_op jit(solution)/shard_map/ppermute | solution.py:293
  17.0 3.1 %collective-permute-start.6 = (bf16[2,128,1024]{2,1,0:T(8,128)(2,1)S(1)}, bf16[2,128,1024]{2,1,0:T(8,128)(2,1)S(1)}, u32[]{:S(2)}, u32[]{:S(2)}) collective-permute-start(bf16[2,128,1024]{2,1,0:T(8,128)(2,1)S(1)} %get-tuple-element.27), channel_id=1, source_target_pairs={{0,8},{4,12},{8,16},{12,20},{16,24},{20,28},{24,32},{28,36},{32,40... | collective-permute-start | bytes 1572872 | tf_op jit(solution)/shard_map/ppermute | solution.py:269
  20.1 3.8 %collective-permute-start.7 = (bf16[2,128,1024]{2,1,0:T(8,128)(2,1)S(1)}, bf16[2,128,1024]{2,1,0:T(8,128)(2,1)S(1)}, u32[]{:S(2)}, u32[]{:S(2)}) collective-permute-start(bf16[2,128,1024]{2,1,0:T(8,128)(2,1)S(1)} %get-tuple-element.27), channel_id=1, source_target_pairs={{0,16},{4,20},{8,24},{12,28},{16,32},{20,36},{24,40},{28,44},{32,4... | collective-permute-start | bytes 1572872 | tf_op jit(solution)/shard_map/ppermute | solution.py:269
  25.1 11.3 %collective-permute-done.3 = bf16[32,1024]{1,0:T(8,128)(2,1)S(1)} collective-permute-done((bf16[32,1024]{1,0:T(8,128)(2,1)S(1)}, bf16[32,1024]{1,0:T(8,128)(2,1)S(1)}, u32[]{:S(2)}, u32[]{:S(2)}) %collective-permute-start.3) | collective-permute-done | bytes 65568 | tf_op jit(solution)/shard_map/ppermute | solution.py:293
  36.4 2.5 %collective-permute-start.4 = (bf16[32,1024]{1,0:T(8,128)(2,1)S(1)}, bf16[32,1024]{1,0:T(8,128)(2,1)S(1)}, u32[]{:S(2)}, u32[]{:S(2)}) collective-permute-start(bf16[32,1024]{1,0:T(8,128)(2,1)S(1)} %collective-permute-done.3), channel_id=1, source_target_pairs={{0,24},{4,28},{8,0},{12,4},{16,8},{20,12},{24,16},{28,20},{32,56},... | collective-permute-start | bytes 196616 | tf_op jit(solution)/shard_map/ppermute | solution.py:293
  40.8 2.6 %collective-permute-start.5 = (bf16[32,1024]{1,0:T(8,128)(2,1)S(1)}, bf16[32,1024]{1,0:T(8,128)(2,1)S(1)}, u32[]{:S(2)}, u32[]{:S(2)}) collective-permute-start(bf16[32,1024]{1,0:T(8,128)(2,1)S(1)} %collective-permute-done.4), channel_id=1, source_target_pairs={{0,24},{4,28},{8,0},{12,4},{16,8},{20,12},{24,16},{28,20},{32,56},... | collective-permute-start | bytes 196616 | tf_op jit(solution)/shard_map/ppermute | solution.py:293
  43.4 2.1 %collective-permute-done.5 = bf16[32,1024]{1,0:T(8,128)(2,1)S(1)} collective-permute-done((bf16[32,1024]{1,0:T(8,128)(2,1)S(1)}, bf16[32,1024]{1,0:T(8,128)(2,1)S(1)}, u32[]{:S(2)}, u32[]{:S(2)}) %collective-permute-start.5) | collective-permute-done | bytes 65568 | tf_op jit(solution)/shard_map/ppermute | solution.py:293
  45.5 11.8 %collective-permute-start.10 = (bf16[128,1024]{1,0:T(8,128)(2,1)S(1)}, bf16[128,1024]{1,0:T(8,128)(2,1)S(1)}, u32[]{:S(2)}, u32[]{:S(2)}) collective-permute-start(bf16[128,1024]{1,0:T(8,128)(2,1)S(1)} %constant_dynamic-update-slice_fusion), channel_id=1, source_target_pairs={{0,192},{4,196},{8,200},{12,204},{16,208},{20,212},{24,216},{28,22... | collective-permute-start | bytes 786440 | tf_op jit(solution)/shard_map/ppermute | solution.py:293
  57.4 2.0 %collective-permute-start.12 = (bf16[128,1024]{1,0:T(8,128)(2,1)S(1)}, bf16[128,1024]{1,0:T(8,128)(2,1)S(1)}, u32[]{:S(2)}, u32[]{:S(2)}) collective-permute-start(bf16[128,1024]{1,0:T(8,128)(2,1)S(1)} %constant_dynamic-update-slice_fusion), channel_id=1, source_target_pairs={{0,32},{4,36},{8,40},{12,44},{16,48},{20,52},{24,56},{28,60},{32,6... | collective-permute-start | bytes 786440 | tf_op jit(solution)/shard_map/ppermute | solution.py:293
  59.4 1.9 %collective-permute-start.8 = (bf16[512,1024]{1,0:T(8,128)(2,1)}, bf16[512,1024]{1,0:T(8,128)(2,1)}, u32[]{:S(2)}, u32[]{:S(2)}) collective-permute-start(bf16[512,1024]{1,0:T(8,128)(2,1)} %refs_2_.1), channel_id=1, source_target_pairs={{0,4},{4,8},{8,12},{12,16},{16,20},{20,24},{24,28},{28,32},{32,36}... | collective-permute-start | bytes 3145736 | tf_op jit(solution)/shard_map/ppermute | solution.py:269
  61.3 7.7 %collective-permute-done.10 = bf16[128,1024]{1,0:T(8,128)(2,1)S(1)} collective-permute-done((bf16[128,1024]{1,0:T(8,128)(2,1)S(1)}, bf16[128,1024]{1,0:T(8,128)(2,1)S(1)}, u32[]{:S(2)}, u32[]{:S(2)}) %collective-permute-start.10) | collective-permute-done | bytes 262176 | tf_op jit(solution)/shard_map/ppermute | solution.py:293
  69.1 5.6 %collective-permute-done.11 = bf16[128,1024]{1,0:T(8,128)(2,1)S(1)} collective-permute-done((bf16[128,1024]{1,0:T(8,128)(2,1)S(1)}, bf16[128,1024]{1,0:T(8,128)(2,1)S(1)}, u32[]{:S(2)}, u32[]{:S(2)}) %collective-permute-start.11) | collective-permute-done | bytes 262176 | tf_op jit(solution)/shard_map/ppermute | solution.py:293
  76.2 2.4 %collective-permute-done.9.refs_6_ = bf16[2,128,1024]{2,1,0:T(8,128)(2,1)} collective-permute-done((bf16[2,128,1024]{2,1,0:T(8,128)(2,1)}, bf16[2,128,1024]{2,1,0:T(8,128)(2,1)}, u32[]{:S(2)}, u32[]{:S(2)}) %collective-permute-start.9) | collective-permute-done | bytes 524320 | tf_op jit(solution)/shard_map/ppermute | solution.py:317
  78.6 9.7 %attend.2 = (bf16[192,1024]{1,0:T(8,128)(2,1)S(1)}, bf16[192,1024]{1,0:T(8,128)(2,1)S(1)}, bf16[192,1024]{1,0:T(8,128)(2,1)S(1)}, bf16[192,1024]{1,0:T(8,128)(2,1)S(1)}) custom-call(s32[1]{0:T(128)} %bitcast.pos_ref, s32[1]{0:T(128)} %bitcast.1.head_ref, bf16[512,1024]{1,0:T(8,128)(2,1)} %refs_0_.3, bf16[512,1024]{1,0:T(8,128)(2,1)} %refs_1_.3, ...), custom_call_target="tpu_custom_call" | custom-call | flops 314572800 | bytes 2097152 | tf_op jit(solution)/shard_map/attend/pallas_call | solution.py:243
  88.3 3.1 %collective-permute-start.16 = (bf16[192,1024]{1,0:T(8,128)(2,1)S(1)}, bf16[192,1024]{1,0:T(8,128)(2,1)S(1)}, u32[]{:S(2)}, u32[]{:S(2)}) collective-permute-start(bf16[192,1024]{1,0:T(8,128)(2,1)S(1)} %get-tuple-element.37), channel_id=1, source_target_pairs={{0,3},{1,0},{2,1},{3,2},{4,7},{5,4},{6,5},{7,6},{8,11},{9,8},{10,9... | collective-permute-start | bytes 1179656 | tf_op jit(solution)/shard_map/ppermute | solution.py:320
  91.4 2.2 %collective-permute-start.14 = (bf16[192,1024]{1,0:T(8,128)(2,1)S(1)}, bf16[192,1024]{1,0:T(8,128)(2,1)S(1)}, u32[]{:S(2)}, u32[]{:S(2)}) collective-permute-start(bf16[192,1024]{1,0:T(8,128)(2,1)S(1)} %get-tuple-element.35), channel_id=1, source_target_pairs={{0,2},{1,3},{2,0},{3,1},{4,6},{5,7},{6,4},{7,5},{8,10},{9,11},{10,... | collective-permute-start | bytes 1179656 | tf_op jit(solution)/shard_map/ppermute | solution.py:320
  93.6 14.4 %attend.3 = (bf16[320,1024]{1,0:T(8,128)(2,1)S(1)}, bf16[320,1024]{1,0:T(8,128)(2,1)S(1)}, bf16[320,1024]{1,0:T(8,128)(2,1)S(1)}, bf16[320,1024]{1,0:T(8,128)(2,1)S(1)}) custom-call(s32[1]{0:T(128)} %bitcast.pos_ref, s32[1]{0:T(128)} %bitcast.1.head_ref, bf16[512,1024]{1,0:T(8,128)(2,1)} %refs_0_.3, bf16[512,1024]{1,0:T(8,128)(2,1)} %refs_1_.3, ...), custom_call_target="tpu_custom_call" | custom-call | flops 629145600 | bytes 2097152 | tf_op jit(solution)/shard_map/attend/pallas_call | solution.py:243
  108.5 3.4 %collective-permute-done.15 = bf16[192,1024]{1,0:T(8,128)(2,1)S(1)} collective-permute-done((bf16[192,1024]{1,0:T(8,128)(2,1)S(1)}, bf16[192,1024]{1,0:T(8,128)(2,1)S(1)}, u32[]{:S(2)}, u32[]{:S(2)}) %collective-permute-start.15) | collective-permute-done | bytes 393248 | tf_op jit(solution)/shard_map/ppermute | solution.py:320
  114.5 5.4 %collective-permute-done.19 = bf16[320,512]{1,0:T(8,128)(2,1)S(1)} collective-permute-done((bf16[320,512]{1,0:T(8,128)(2,1)S(1)}, bf16[320,512]{1,0:T(8,128)(2,1)S(1)}, u32[]{:S(2)}, u32[]{:S(2)}) %collective-permute-start.19) | collective-permute-done | bytes 327712 | tf_op jit(solution)/shard_map/ppermute | solution.py:320
  120.1 2.9 %collective-permute-start.20 = (bf16[320,1024]{1,0:T(8,128)(2,1)S(1)}, bf16[320,1024]{1,0:T(8,128)(2,1)S(1)}, u32[]{:S(2)}, u32[]{:S(2)}) collective-permute-start(bf16[320,1024]{1,0:T(8,128)(2,1)S(1)} %pad_maximum_fusion.2), channel_id=1, source_target_pairs={{0,3},{1,0},{2,1},{3,2},{4,7},{5,4},{6,5},{7,6},{8,11},{9,8},{10,9... | collective-permute-start | bytes 1966088 | tf_op jit(solution)/shard_map/ppermute | solution.py:320
  123.3 12.3 %collective-permute-done.20 = bf16[320,1024]{1,0:T(8,128)(2,1)S(1)} collective-permute-done((bf16[320,1024]{1,0:T(8,128)(2,1)S(1)}, bf16[320,1024]{1,0:T(8,128)(2,1)S(1)}, u32[]{:S(2)}, u32[]{:S(2)}) %collective-permute-start.20) | collective-permute-done | bytes 655392 | tf_op jit(solution)/shard_map/ppermute | solution.py:320
  135.5 3.7 %collective-permute-done.18 = bf16[320,1024]{1,0:T(8,128)(2,1)S(1)} collective-permute-done((bf16[320,1024]{1,0:T(8,128)(2,1)S(1)}, bf16[320,1024]{1,0:T(8,128)(2,1)S(1)}, u32[]{:S(2)}, u32[]{:S(2)}) %collective-permute-start.18) | collective-permute-done | bytes 655392 | tf_op jit(solution)/shard_map/ppermute | solution.py:320
  (43 shorter events, 12.8 us)
Async XLA Ops:
  0.0 45.5 %collective-permute-start = (bf16[512,1024]{1,0:T(8,128)(2,1)}, bf16[512,1024]{1,0:T(8,128)(2,1)S(1)}, u32[]{:S(2)}, u32[]{:S(2)}) collective-permute-start(bf16[512,1024]{1,0:T(8,128)(2,1)} %refs_1_.3), channel_id=1, source_target_pairs={{0,4},{4,8},{8,12},{12,16},{16,20},{20,24},{24,28},{28,32},{32,36}... | collective-permute-start | bytes 3145736 | tf_op jit(solution)/shard_map/ppermute | solution.py:269
  7.2 2.5 %collective-permute-start.1 = (bf16[8,1024]{1,0:T(8,128)(2,1)S(1)}, bf16[8,1024]{1,0:T(8,128)(2,1)S(1)}, u32[]{:S(2)}, u32[]{:S(2)}) collective-permute-start(bf16[8,1024]{1,0:T(8,128)(2,1)S(1)} %get-tuple-element.26), channel_id=1, source_target_pairs={{0,4},{4,0},{8,12},{12,8},{16,20},{20,16},{24,28},{28,24},{32,36},... | collective-permute-start | bytes 49160 | tf_op jit(solution)/shard_map/ppermute | solution.py:301
  9.7 14.2 %collective-permute-start.2 = (bf16[16,1024]{1,0:T(8,128)(2,1)S(1)}, bf16[16,1024]{1,0:T(8,128)(2,1)S(1)}, u32[]{:S(2)}, u32[]{:S(2)}) collective-permute-start(bf16[16,1024]{1,0:T(8,128)(2,1)S(1)} %get-tuple-element.46), channel_id=1, source_target_pairs={{0,128},{4,132},{8,136},{12,140},{16,144},{20,148},{24,152},{28,15... | collective-permute-start | bytes 98312 | tf_op jit(solution)/shard_map/ppermute | solution.py:293
  17.0 28.5 %collective-permute-start.6 = (bf16[2,128,1024]{2,1,0:T(8,128)(2,1)S(1)}, bf16[2,128,1024]{2,1,0:T(8,128)(2,1)S(1)}, u32[]{:S(2)}, u32[]{:S(2)}) collective-permute-start(bf16[2,128,1024]{2,1,0:T(8,128)(2,1)S(1)} %get-tuple-element.27), channel_id=1, source_target_pairs={{0,8},{4,12},{8,16},{12,20},{16,24},{20,28},{24,32},{28,36},{32,40... | collective-permute-start | bytes 1572872 | tf_op jit(solution)/shard_map/ppermute | solution.py:269
  20.1 25.4 %collective-permute-start.7 = (bf16[2,128,1024]{2,1,0:T(8,128)(2,1)S(1)}, bf16[2,128,1024]{2,1,0:T(8,128)(2,1)S(1)}, u32[]{:S(2)}, u32[]{:S(2)}) collective-permute-start(bf16[2,128,1024]{2,1,0:T(8,128)(2,1)S(1)} %get-tuple-element.27), channel_id=1, source_target_pairs={{0,16},{4,20},{8,24},{12,28},{16,32},{20,36},{24,40},{28,44},{32,4... | collective-permute-start | bytes 1572872 | tf_op jit(solution)/shard_map/ppermute | solution.py:269
  23.9 12.5 %collective-permute-start.3 = (bf16[32,1024]{1,0:T(8,128)(2,1)S(1)}, bf16[32,1024]{1,0:T(8,128)(2,1)S(1)}, u32[]{:S(2)}, u32[]{:S(2)}) collective-permute-start(bf16[32,1024]{1,0:T(8,128)(2,1)S(1)} %pad_maximum_fusion.3), channel_id=1, source_target_pairs={{0,24},{4,28},{8,0},{12,4},{16,8},{20,12},{24,16},{28,20},{32,56},... | collective-permute-start | bytes 196616 | tf_op jit(solution)/shard_map/ppermute | solution.py:293
  36.4 4.4 %collective-permute-start.4 = (bf16[32,1024]{1,0:T(8,128)(2,1)S(1)}, bf16[32,1024]{1,0:T(8,128)(2,1)S(1)}, u32[]{:S(2)}, u32[]{:S(2)}) collective-permute-start(bf16[32,1024]{1,0:T(8,128)(2,1)S(1)} %collective-permute-done.3), channel_id=1, source_target_pairs={{0,24},{4,28},{8,0},{12,4},{16,8},{20,12},{24,16},{28,20},{32,56},... | collective-permute-start | bytes 196616 | tf_op jit(solution)/shard_map/ppermute | solution.py:293
  40.8 4.7 %collective-permute-start.5 = (bf16[32,1024]{1,0:T(8,128)(2,1)S(1)}, bf16[32,1024]{1,0:T(8,128)(2,1)S(1)}, u32[]{:S(2)}, u32[]{:S(2)}) collective-permute-start(bf16[32,1024]{1,0:T(8,128)(2,1)S(1)} %collective-permute-done.4), channel_id=1, source_target_pairs={{0,24},{4,28},{8,0},{12,4},{16,8},{20,12},{24,16},{28,20},{32,56},... | collective-permute-start | bytes 196616 | tf_op jit(solution)/shard_map/ppermute | solution.py:293
  45.5 23.5 %collective-permute-start.10 = (bf16[128,1024]{1,0:T(8,128)(2,1)S(1)}, bf16[128,1024]{1,0:T(8,128)(2,1)S(1)}, u32[]{:S(2)}, u32[]{:S(2)}) collective-permute-start(bf16[128,1024]{1,0:T(8,128)(2,1)S(1)} %constant_dynamic-update-slice_fusion), channel_id=1, source_target_pairs={{0,192},{4,196},{8,200},{12,204},{16,208},{20,212},{24,216},{28,22... | collective-permute-start | bytes 786440 | tf_op jit(solution)/shard_map/ppermute | solution.py:293
  57.4 17.3 %collective-permute-start.11 = (bf16[128,1024]{1,0:T(8,128)(2,1)S(1)}, bf16[128,1024]{1,0:T(8,128)(2,1)S(1)}, u32[]{:S(2)}, u32[]{:S(2)}) collective-permute-start(bf16[128,1024]{1,0:T(8,128)(2,1)S(1)} %constant_dynamic-update-slice_fusion), channel_id=1, source_target_pairs={{0,224},{4,228},{8,232},{12,236},{16,240},{20,244},{24,248},{28,25... | collective-permute-start | bytes 786440 | tf_op jit(solution)/shard_map/ppermute | solution.py:293
  57.4 17.3 %collective-permute-start.12 = (bf16[128,1024]{1,0:T(8,128)(2,1)S(1)}, bf16[128,1024]{1,0:T(8,128)(2,1)S(1)}, u32[]{:S(2)}, u32[]{:S(2)}) collective-permute-start(bf16[128,1024]{1,0:T(8,128)(2,1)S(1)} %constant_dynamic-update-slice_fusion), channel_id=1, source_target_pairs={{0,32},{4,36},{8,40},{12,44},{16,48},{20,52},{24,56},{28,60},{32,6... | collective-permute-start | bytes 786440 | tf_op jit(solution)/shard_map/ppermute | solution.py:293
  59.4 19.2 %collective-permute-start.8 = (bf16[512,1024]{1,0:T(8,128)(2,1)}, bf16[512,1024]{1,0:T(8,128)(2,1)}, u32[]{:S(2)}, u32[]{:S(2)}) collective-permute-start(bf16[512,1024]{1,0:T(8,128)(2,1)} %refs_2_.1), channel_id=1, source_target_pairs={{0,4},{4,8},{8,12},{12,16},{16,20},{20,24},{24,28},{28,32},{32,36}... | collective-permute-start | bytes 3145736 | tf_op jit(solution)/shard_map/ppermute | solution.py:269
  74.7 3.8 %collective-permute-start.13 = (bf16[512,1024]{1,0:T(8,128)(2,1)S(1)}, bf16[512,1024]{1,0:T(8,128)(2,1)}, u32[]{:S(2)}, u32[]{:S(2)}) collective-permute-start(bf16[512,1024]{1,0:T(8,128)(2,1)S(1)} %constant_dynamic-update-slice_fusion.5.refs_8_), channel_id=1, source_target_pairs={{0,4},{4,0},{8,12},{12,8},{16,20},{20,16},{24,28},{28,24},{32,36},... | collective-permute-start | bytes 3145736 | tf_op jit(solution)/shard_map/ppermute | solution.py:316
  75.7 2.8 %collective-permute-start.9 = (bf16[2,128,1024]{2,1,0:T(8,128)(2,1)}, bf16[2,128,1024]{2,1,0:T(8,128)(2,1)}, u32[]{:S(2)}, u32[]{:S(2)}) collective-permute-start(bf16[2,128,1024]{2,1,0:T(8,128)(2,1)} %broadcast_select_fusion), channel_id=1, source_target_pairs={{0,4},{4,0},{8,12},{12,8},{16,20},{20,16},{24,28},{28,24},{32,36},... | collective-permute-start | bytes 1572872 | tf_op jit(solution)/shard_map/ppermute | solution.py:317
  88.3 20.2 %collective-permute-start.16 = (bf16[192,1024]{1,0:T(8,128)(2,1)S(1)}, bf16[192,1024]{1,0:T(8,128)(2,1)S(1)}, u32[]{:S(2)}, u32[]{:S(2)}) collective-permute-start(bf16[192,1024]{1,0:T(8,128)(2,1)S(1)} %get-tuple-element.37), channel_id=1, source_target_pairs={{0,3},{1,0},{2,1},{3,2},{4,7},{5,4},{6,5},{7,6},{8,11},{9,8},{10,9... | collective-permute-start | bytes 1179656 | tf_op jit(solution)/shard_map/ppermute | solution.py:320
  91.4 20.5 %collective-permute-start.15 = (bf16[192,1024]{1,0:T(8,128)(2,1)S(1)}, bf16[192,1024]{1,0:T(8,128)(2,1)S(1)}, u32[]{:S(2)}, u32[]{:S(2)}) collective-permute-start(bf16[192,1024]{1,0:T(8,128)(2,1)S(1)} %get-tuple-element.36), channel_id=1, source_target_pairs={{0,1},{1,2},{2,3},{3,0},{4,5},{5,6},{6,7},{7,4},{8,9},{9,10},{10,1... | collective-permute-start | bytes 1179656 | tf_op jit(solution)/shard_map/ppermute | solution.py:320
  91.4 20.5 %collective-permute-start.14 = (bf16[192,1024]{1,0:T(8,128)(2,1)S(1)}, bf16[192,1024]{1,0:T(8,128)(2,1)S(1)}, u32[]{:S(2)}, u32[]{:S(2)}) collective-permute-start(bf16[192,1024]{1,0:T(8,128)(2,1)S(1)} %get-tuple-element.35), channel_id=1, source_target_pairs={{0,2},{1,3},{2,0},{3,1},{4,6},{5,7},{6,4},{7,5},{8,10},{9,11},{10,... | collective-permute-start | bytes 1179656 | tf_op jit(solution)/shard_map/ppermute | solution.py:320
  112.2 7.7 %collective-permute-start.19 = (bf16[320,512]{1,0:T(8,128)(2,1)S(1)}, bf16[320,512]{1,0:T(8,128)(2,1)S(1)}, u32[]{:S(2)}, u32[]{:S(2)}) collective-permute-start(bf16[320,512]{1,0:T(8,128)(2,1)S(1)} %get-tuple-element.48), channel_id=1, source_target_pairs={{0,3},{1,0},{2,1},{3,2},{4,7},{5,4},{6,5},{7,6},{8,11},{9,8},{10,9... | collective-permute-start | bytes 983048 | tf_op jit(solution)/shard_map/ppermute | solution.py:320
  112.7 10.3 %collective-permute-start.17 = (bf16[320,512]{1,0:T(8,128)(2,1)S(1)}, bf16[320,512]{1,0:T(8,128)(2,1)S(1)}, u32[]{:S(2)}, u32[]{:S(2)}) collective-permute-start(bf16[320,512]{1,0:T(8,128)(2,1)S(1)} %get-tuple-element.47), channel_id=1, source_target_pairs={{0,1},{1,2},{2,3},{3,0},{4,5},{5,6},{6,7},{7,4},{8,9},{9,10},{10,1... | collective-permute-start | bytes 983048 | tf_op jit(solution)/shard_map/ppermute | solution.py:320
  120.1 15.4 %collective-permute-start.20 = (bf16[320,1024]{1,0:T(8,128)(2,1)S(1)}, bf16[320,1024]{1,0:T(8,128)(2,1)S(1)}, u32[]{:S(2)}, u32[]{:S(2)}) collective-permute-start(bf16[320,1024]{1,0:T(8,128)(2,1)S(1)} %pad_maximum_fusion.2), channel_id=1, source_target_pairs={{0,3},{1,0},{2,1},{3,2},{4,7},{5,4},{6,5},{7,6},{8,11},{9,8},{10,9... | collective-permute-start | bytes 1966088 | tf_op jit(solution)/shard_map/ppermute | solution.py:320
  123.2 16.0 %collective-permute-start.18 = (bf16[320,1024]{1,0:T(8,128)(2,1)S(1)}, bf16[320,1024]{1,0:T(8,128)(2,1)S(1)}, u32[]{:S(2)}, u32[]{:S(2)}) collective-permute-start(bf16[320,1024]{1,0:T(8,128)(2,1)S(1)} %pad_maximum_fusion.1), channel_id=1, source_target_pairs={{0,1},{1,2},{2,3},{3,0},{4,5},{5,6},{6,7},{7,4},{8,9},{9,10},{10,1... | collective-permute-start | bytes 1966088 | tf_op jit(solution)/shard_map/ppermute | solution.py:320
